TPU v7x, 512 devices: a whole 4x8x8 slice. The times are simulated.
512 devices in a mesh: slab: 32 (over x, z), mode: 16 (over y, core).
Axes of the slice: x: 4, y: 8, z: 8, core: 2. Of those that a mesh axis runs over, the one named last changes fastest.
Arguments:
- design: float32 [64, 128, 128], P('slab', 'mode'), may hold values from 0.03 to 1
- mode_shapes: float32 [16, 3, 64, 128, 128], P('mode', None, 'slab'), may hold values from -2.4 to 2.4
- eigenvalues: float32 [16], P('mode'), may hold values from 0.5 to 2
Outputs:
- sensitivity: float32 [64, 128, 128], P('slab', 'mode')
- new_design: float32 [64, 128, 128], P('slab', 'mode')
All inputs are finite; a program needn't handle non-finite values.
Results may differ from a plain program's by a relative error of at most 0.0003.
Values sent between devices are 32-bit elements; how exact they have to be, the bound alone decides.
No kernel may reach another device: no remote copies, remote signals or barrier semaphores. Data moves between devices by JAX's collectives and lax.ppermute only.
A program may use at most 64 MiB of HBM per device.

v0:
```python
import jax
import jax.numpy as jnp
import numpy as np
from jax import lax
from jax.sharding import Mesh
from jax.sharding import PartitionSpec as P

FR = 3
BISECT = 12
SLAB = ("slab_0", "slab_1")
MODE = ("mode_0", "mode_1")


KS_SHARP = 2.0
PENALTY = 3.0
FLOOR_MODULUS = 0.001
MOVE_LIMIT = 0.2
POISSON = 0.3
LEVEL_LOW = -14.0
LEVEL_HIGH = 14.0


def padded_2(value, sides, width):
    for axis, dim in sides:
        count, length = (lax.axis_size(axis), value.shape[dim])
        up = [(i, (i + 1) % count) for i in range(count - 1)]
        down = [(j, i) for i, j in up]
        last = lax.slice_in_dim(value, length - width, length, axis=dim)
        leading = lax.slice_in_dim(value, 0, width, axis=dim)
        before = lax.ppermute(last, axis, up)
        after = lax.ppermute(leading, axis, down)
        value = jnp.concatenate([before, value, after], axis=dim)
    return value


def sent_to_all(value, axis):
    count = lax.axis_size(axis)
    return lax.all_to_all(
        jnp.broadcast_to(value[None], (count, *value.shape)), axis, 0, 0, tiled=True
    )


def laid_out(pieces, dim):
    pieces = jnp.moveaxis(pieces, 0, dim)
    lengths = pieces.shape
    return pieces.reshape(*lengths[:dim], lengths[dim] * lengths[dim + 1], *lengths[dim + 2 :])


def gathered_copies(value, axis, dim):
    pieces = sent_to_all(value, axis)
    return laid_out(pieces, dim)


def over_copies(value, axis):
    everything = sent_to_all(value, axis)
    return jnp.sum(everything, axis=0)


def over_axes(value, axes):
    far, near = axes
    nearer = over_copies(value, near)
    return over_copies(nearer, far)


def shifted_2(value, axis, by):
    count = lax.axis_size(axis)
    pairs = [(i, i + by) for i in range(count) if 0 <= i + by < count]
    return lax.ppermute(value, axis, pairs)


def cut_along(value, dim, count):
    before, after = (value.shape[:dim], value.shape[dim + 1 :])
    return jnp.moveaxis(value.reshape(*before, count, -1, *after), dim, 0)


def summed_on_arrival(value, axis, dim):
    count = lax.axis_size(axis)
    pieces = lax.all_to_all(cut_along(value, dim, count), axis, 0, 0, tiled=True)
    return jnp.sum(pieces, axis=0)


def element_tables():
    lame_first = POISSON / ((1.0 + POISSON) * (1.0 - 2.0 * POISSON))
    shear_modulus = 0.5 / (1.0 + POISSON)
    elastic = np.zeros((6, 6))
    elastic[:3, :3] = lame_first
    for i in range(3):
        elastic[i, i] += 2.0 * shear_modulus
        elastic[i + 3, i + 3] = shear_modulus
    corner_signs = np.array([[a, b, c] for a in (0, 1) for b in (0, 1) for c in (0, 1)]) * 2.0 - 1.0
    gauss_points = [-1.0 / np.sqrt(3.0), 1.0 / np.sqrt(3.0)]
    stiffness = np.zeros((24, 24))
    mass_matrix = np.zeros((24, 24))
    for first in gauss_points:
        for second in gauss_points:
            for third in gauss_points:
                sample = np.array([first, second, third])
                factors = 1.0 + corner_signs * sample
                shape_values = np.prod(factors, axis=1) / 8.0
                gradients = np.zeros((8, 3))
                for d in range(3):
                    others = [e for e in range(3) if e != d]
                    gradients[:, d] = (
                        corner_signs[:, d] * factors[:, others[0]] * factors[:, others[1]] / 4.0
                    )
                strain = np.zeros((6, 24))
                shape_rows = np.zeros((3, 24))
                for n in range(8):
                    strain[0, 3 * n] = gradients[n, 0]
                    strain[1, 3 * n + 1] = gradients[n, 1]
                    strain[2, 3 * n + 2] = gradients[n, 2]
                    strain[3, 3 * n] = gradients[n, 1]
                    strain[3, 3 * n + 1] = gradients[n, 0]
                    strain[4, 3 * n + 1] = gradients[n, 2]
                    strain[4, 3 * n + 2] = gradients[n, 1]
                    strain[5, 3 * n] = gradients[n, 2]
                    strain[5, 3 * n + 2] = gradients[n, 0]
                    for i in range(3):
                        shape_rows[i, 3 * n + i] = shape_values[n]
                stiffness += strain.T @ elastic @ strain / 8.0
                mass_matrix += shape_rows.T @ shape_rows / 8.0
    return np.concatenate([stiffness, mass_matrix], 0)


def tent_valid(values, along):
    margin = FR - 1
    length = values.shape[along] - 2 * margin
    summed = None
    for offset in range(-margin, margin + 1):
        shifted = (FR - abs(offset)) * lax.slice_in_dim(
            values, margin + offset, margin + offset + length, axis=along
        )
        summed = shifted if summed is None else summed + shifted
    return summed


def tent_padded(values, along):
    margin = FR - 1
    widths = [(0, 0)] * values.ndim
    widths[along] = (margin, margin)
    return tent_valid(jnp.pad(values, widths), along)


def edge_weights(positions, count):
    summed = jnp.zeros(positions.shape, jnp.float32)
    for offset in range(-(FR - 1), FR):
        inside = (positions + offset >= 0) & (positions + offset < count)
        summed = summed + (FR - abs(offset)) * inside.astype(jnp.float32)
    return summed


def grid_positions(start, count):
    return start + jnp.arange(count, dtype=jnp.int32)


def span_block(x_start, x_count, y_start, y_count, total_x, total_rows, depth_count):
    first_weight = edge_weights(grid_positions(x_start, x_count), total_x)
    second_weight = edge_weights(grid_positions(y_start, y_count), total_rows)
    third_weight = edge_weights(grid_positions(0, depth_count), depth_count)
    return first_weight[:, None, None] * second_weight[None, :, None] * third_weight[None, None, :]


def inverse_block(x_start, x_count, y_start, y_count, total_x, total_rows, depth_count):
    first_index = grid_positions(x_start, x_count)
    second_index = grid_positions(y_start, y_count)
    spans = span_block(x_start, x_count, y_start, y_count, total_x, total_rows, depth_count)
    first_inside = ((first_index >= 0) & (first_index < total_x)).astype(jnp.float32)
    second_inside = ((second_index >= 0) & (second_index < total_rows)).astype(jnp.float32)
    inside = first_inside[:, None, None] * second_inside[None, :, None]
    return inside / jnp.maximum(spans, 1.0)


def update(design, sensitivity, measure, level):
    factor = jnp.sqrt(jnp.maximum(sensitivity, 0.0) / (jnp.exp(level) * measure))
    return jnp.clip(
        design * factor,
        jnp.maximum(design - MOVE_LIMIT, 0.0),
        jnp.minimum(design + MOVE_LIMIT, 1.0),
    )


def element_forms(node_values, tables):
    layer_count = node_values.shape[1] - 1
    row_count = node_values.shape[2]
    depth_count = node_values.shape[3]
    block_rows = 32
    padded = jnp.concatenate(
        [node_values, jnp.zeros((3, layer_count + 1, 1, depth_count), jnp.float32)], 2
    )
    lifted = jnp.concatenate(
        [padded[:, :, :, 1:], jnp.zeros((3, layer_count + 1, row_count + 1, 1), jnp.float32)], 3
    )

    def one_block(start):
        corners = []
        for a in (0, 1):
            for b in (0, 1):
                for c in (0, 1):
                    source = lifted if c else padded
                    corners.append(
                        lax.dynamic_slice(
                            source, (0, a, start + b, 0), (3, layer_count, block_rows, depth_count)
                        )
                    )
        stacked = jnp.stack(corners, 0).reshape(24, layer_count * block_rows * depth_count)
        product = jnp.dot(tables, stacked, precision=lax.Precision.HIGHEST)
        stiff_form = jnp.sum(product[:24] * stacked, 0).reshape(
            layer_count, block_rows, depth_count
        )
        mass_form = jnp.sum(product[24:] * stacked, 0).reshape(layer_count, block_rows, depth_count)
        return (stiff_form, mass_form)

    starts = jnp.arange(row_count // block_rows, dtype=jnp.int32) * block_rows
    stiff_blocks, mass_blocks = lax.map(one_block, starts)
    stiff_form = jnp.moveaxis(stiff_blocks, 0, 1).reshape(layer_count, row_count, depth_count)
    mass_form = jnp.moveaxis(mass_blocks, 0, 1).reshape(layer_count, row_count, depth_count)
    return (stiff_form, mass_form)


def local(design, mode_shapes, eigenvalues):
    margin = FR - 1
    slab_cells, own_rows, depth_count = design.shape
    total_x = slab_cells * lax.axis_size(SLAB)
    total_rows = own_rows * lax.axis_size(MODE)
    x_start = lax.axis_index(SLAB) * slab_cells
    y_start = lax.axis_index(MODE) * own_rows
    tables = jnp.asarray(element_tables(), jnp.float32)
    own_span = span_block(x_start, slab_cells, y_start, own_rows, total_x, total_rows, depth_count)
    extended = padded_2(design, ((SLAB, 0), (MODE, 1)), margin)
    own_density = tent_valid(tent_valid(tent_padded(extended, 2), 0), 1) / own_span
    density = gathered_copies(own_density, MODE, 1)
    target = over_axes(jnp.sum(own_density), (("slab_0", "slab_1"), ("mode_0", "mode_1")))
    plane = shifted_2(mode_shapes[:, :, 0], SLAB, -1)
    node_values = jnp.concatenate([mode_shapes, plane[:, :, None]], 2)
    weights = jnp.exp(-KS_SHARP * eigenvalues)
    summed_weight = over_copies(jnp.sum(weights), MODE)
    slope = PENALTY * (1.0 - FLOOR_MODULUS) * density * density

    def add_mode(number, partial_value):
        stiff_form, mass_form = element_forms(node_values[number], tables)
        return partial_value + weights[number] * (
            slope * stiff_form - eigenvalues[number] * mass_form
        )

    partial_value = lax.fori_loop(0, node_values.shape[0], add_mode, jnp.zeros_like(density))
    own_sum = summed_on_arrival(partial_value, MODE, 1)
    gradient = own_sum / summed_weight
    rim_values = padded_2(gradient / own_span, ((SLAB, 0), (MODE, 1)), margin)
    sensitivity = tent_valid(tent_valid(tent_padded(rim_values, 2), 0), 1)
    inverse = inverse_block(
        x_start - margin,
        slab_cells + 2 * margin,
        y_start - margin,
        own_rows + 2 * margin,
        total_x,
        total_rows,
        depth_count,
    )
    measure = tent_valid(tent_valid(tent_padded(inverse, 2), 0), 1)
    start_bounds = (jnp.asarray(LEVEL_LOW, jnp.float32), jnp.asarray(LEVEL_HIGH, jnp.float32))

    def bracket(count, bounds):
        lower, upper = bounds
        intervals = [(lower, upper)]
        middles = []
        for depth_step in range(4):
            following = []
            for bounds_pair in intervals:
                middle = (bounds_pair[0] + bounds_pair[1]) * 0.5
                middles.append(middle)
                following.append((bounds_pair[0], middle))
                following.append((middle, bounds_pair[1]))
            intervals = following
        candidates = jnp.stack(middles)
        partial_volumes = jnp.stack(
            [
                jnp.sum(update(design, sensitivity, measure, candidate) * measure)
                for candidate in middles
            ]
        )
        volumes = over_axes(partial_volumes, (("slab_0", "slab_1"), ("mode_0", "mode_1")))
        heap_slot = jnp.asarray(0, jnp.int32)
        for depth_step in range(4):
            middle = candidates[heap_slot]
            above = volumes[heap_slot] > target
            lower = jnp.where(above, middle, lower)
            upper = jnp.where(above, upper, middle)
            heap_slot = 2 * heap_slot + 1 + above.astype(jnp.int32)
        return (lower, upper)

    lower, upper = lax.fori_loop(0, BISECT // 4, bracket, start_bounds)
    new_design = update(design, sensitivity, measure, (lower + upper) * 0.5)
    return (sensitivity, new_design)


def solution(mesh):
    split = Mesh(mesh.devices.reshape(4, 8, 8, 2), ("slab_0", "slab_1", "mode_0", "mode_1"))
    in_specs = (P(SLAB, MODE, None), P(MODE, None, SLAB, None, None), P(MODE))
    out_specs = (P(SLAB, MODE, None), P(SLAB, MODE, None))
    return jax.shard_map(local, mesh=split, in_specs=in_specs, out_specs=out_specs, check_vma=False)
```

profile of v0, /device:TPU:1, one launch (start us, length us, event | category | flops | bytes accessed | tf_op | source)
XLA Modules:
  0.0 274.4 jit_solution(2070934616573847096)
XLA Ops:
  0.6 4.8 %collective-permute-start = (f32[2,8,128]{2,1,0:T(8,128)}, f32[2,8,128]{2,1,0:T(8,128)S(1)}, u32[]{:S(2)}, u32[]{:S(2)}) collective-permute-start(f32[2,8,128]{2,1,0:T(8,128)} %param.8), channel_id=1, source_target_pairs={{0,16},{16,32},{32,48},{48,64},{64,80},{80,96},{96,112},{112,128},... | collective-permute-start | bytes 24584 | tf_op jit(solution)/shard_map/ppermute | solution.py:30
  5.5 1.3 collective-permute-start.1
  6.8 0.9 slice_bitcast_fusion
  7.7 1.3 collective-permute-start.4
  9.3 0.7 constant_dynamic-update-slice_fusion.3
  10.0 0.7 collective-permute-done.1
  10.7 5.8 %collective-permute-start.3 = (f32[6,2,128]{2,1,0:T(2,128)S(1)}, f32[6,2,128]{2,1,0:T(2,128)S(1)}, u32[]{:S(2)}, u32[]{:S(2)}) collective-permute-start(f32[6,2,128]{2,1,0:T(2,128)S(1)} %get-tuple-element.285), channel_id=1, source_target_pairs={{1,0},{2,1},{3,2},{4,3},{5,4},{6,5},{7,6},{8,7},{9,8},{10,9},{11,1... | collective-permute-start | bytes 18440 | tf_op jit(solution)/shard_map/ppermute | solution.py:31
  16.5 1.9 collective-permute-start.2
  19.8 0.7 fusion.65
  20.4 1.0 maximum_bitcast_fusion
  21.8 0.6 broadcast_in_dim.27
  22.4 8.1 %all-to-all-start.2 = ((f32[16,2,8,128]{3,2,1,0:T(8,128)}), f32[16,2,8,128]{3,2,1,0:T(8,128)S(1)}, u32[]{:S(2)}, u32[]{:S(2)}) async-start(f32[16,2,8,128]{3,2,1,0:T(8,128)} %broadcast_in_dim.27), calls=%async_computation.2 | async-start | bytes 262144 | tf_op jit(solution)/shard_map/all_to_all | solution.py:38
  30.6 23.4 %while.39 = (s32[]{:T(128)}, f32[4,2,32,128]{3,2,0,1:T(8,128)S(1)}, f32[4,2,32,128]{3,2,0,1:T(8,128)S(1)}, s32[4]{0:T(128)S(1)}, f32[3,3,129,128]{3,2,1,0:T(8,12...) while((s32[]{:T(128)}, f32[4,2,32,128]{3,2,0,1:T(8,128)S(1)}, ...), condition=%wide.region_3.4_spmd.clone, body=%wide.region_0.3_spmd.sunk.clone.sunk | while | flops 114016264 | bytes 8065781 | solution.py:214
  30.6 0.6 dynamic_slice.161
  34.7 1.4 fusion.79
  36.5 0.6 dynamic_slice.161
  40.6 1.4 fusion.79
  46.4 1.4 fusion.79
  52.3 1.4 fusion.79
  54.6 7.2 %all-to-all-start.4 = ((f32[16,1,1]{2,1,0:T(1,128)}), f32[16,1,1]{2,1,0:T(1,128)S(1)}, u32[]{:S(2)}, u32[]{:S(2)}) async-start(f32[16,1,1]{2,1,0:T(1,128)} %broadcast_in_dim.29), calls=%async_computation.4 | async-start | bytes 16384 | tf_op jit(solution)/shard_map/all_to_all | solution.py:38
  61.9 0.6 copy.36
  62.5 6.3 %all-to-all-done.4 = f32[16,1,1]{2,1,0:T(1,128)S(1)} async-done(((f32[16,1,1]{2,1,0:T(1,128)}), f32[16,1,1]{2,1,0:T(1,128)S(1)}, u32[]{:S(2)}, u32[]{:S(2)}) %all-to-all-start.4) | async-done | bytes 96 | tf_op jit(solution)/shard_map/all_to_all | solution.py:38
  68.8 4.0 %all-to-all-start.3 = ((f32[16,2,8,128]{3,2,1,0:T(8,128)}), f32[16,2,8,128]{3,2,1,0:T(8,128)S(1)}, u32[]{:S(2)}, u32[]{:S(2)}) async-start(f32[16,2,8,128]{3,2,1,0:T(8,128)} %copy.36), calls=%async_computation.3 | async-start | bytes 262144 | tf_op jit(solution)/shard_map/all_to_all | solution.py:78
  73.6 8.3 %all-to-all-done.3 = f32[16,2,8,128]{3,2,1,0:T(8,128)S(1)} async-done(((f32[16,2,8,128]{3,2,1,0:T(8,128)}), f32[16,2,8,128]{3,2,1,0:T(8,128)S(1)}, u32[]{:S(2)}, u32[]{:S(2)}) %all-to-all-start.3) | async-done | bytes 131104 | tf_op jit(solution)/shard_map/all_to_all | solution.py:78
  82.0 0.7 fusion.33
  82.7 1.3 collective-permute-start.6
  84.0 4.6 %collective-permute-start.5 = (f32[2,8,128]{2,1,0:T(8,128)S(1)}, f32[2,8,128]{2,1,0:T(8,128)S(1)}, u32[]{:S(2)}, u32[]{:S(2)}) collective-permute-start(f32[2,8,128]{2,1,0:T(8,128)S(1)} %fusion.33), channel_id=1, source_target_pairs={{0,16},{16,32},{32,48},{48,64},{64,80},{80,96},{96,112},{112,128},... | collective-permute-start | bytes 24584 | tf_op jit(solution)/shard_map/ppermute | solution.py:30
  88.7 0.7 collective-permute-done.5
  89.4 2.4 collective-permute-start.8
  91.8 3.1 %collective-permute-start.7 = (f32[6,2,128]{2,1,0:T(2,128)S(1)}, f32[6,2,128]{2,1,0:T(2,128)S(1)}, u32[]{:S(2)}, u32[]{:S(2)}) collective-permute-start(f32[6,2,128]{2,1,0:T(2,128)S(1)} %get-tuple-element.282), channel_id=1, source_target_pairs={{0,1},{1,2},{2,3},{3,4},{4,5},{5,6},{6,7},{7,8},{8,9},{9,10},{10,1... | collective-permute-start | bytes 18440 | tf_op jit(solution)/shard_map/ppermute | solution.py:30
  95.0 1.2 broadcast_in_dim.30
  96.1 3.4 %all-to-all-start.5 = ((f32[16,1,1]{2,1,0:T(1,128)}), f32[16,1,1]{2,1,0:T(1,128)S(1)}, u32[]{:S(2)}, u32[]{:S(2)}) async-start(f32[16,1,1]{2,1,0:T(1,128)} %broadcast_in_dim.30), calls=%async_computation.5 | async-start | bytes 16384 | tf_op jit(solution)/shard_map/all_to_all | solution.py:38
  99.5 6.8 %all-to-all-done.5 = f32[16,1,1]{2,1,0:T(1,128)S(1)} async-done(((f32[16,1,1]{2,1,0:T(1,128)}), f32[16,1,1]{2,1,0:T(1,128)S(1)}, u32[]{:S(2)}, u32[]{:S(2)}) %all-to-all-start.5) | async-done | bytes 96 | tf_op jit(solution)/shard_map/all_to_all | solution.py:38
  107.0 1.2 broadcast_in_dim.31
  108.3 15.3 %all-to-all-start.6 = ((f32[32,1,1]{2,1,0:T(1,128)}), f32[32,1,1]{2,1,0:T(1,128)S(1)}, u32[]{:S(2)}, u32[]{:S(2)}) async-start(f32[32,1,1]{2,1,0:T(1,128)} %broadcast_in_dim.31), calls=%async_computation.6 | async-start | bytes 32768 | tf_op jit(solution)/shard_map/all_to_all | solution.py:38
  123.6 8.7 %all-to-all-done.6 = f32[32,1,1]{2,1,0:T(1,128)S(1)} async-done(((f32[32,1,1]{2,1,0:T(1,128)}), f32[32,1,1]{2,1,0:T(1,128)S(1)}, u32[]{:S(2)}, u32[]{:S(2)}) %all-to-all-start.6) | async-done | bytes 160 | tf_op jit(solution)/shard_map/all_to_all | solution.py:38
  133.1 140.7 %while.38 = (s32[]{:T(128)}, f32[]{:T(128)}, f32[]{:T(128)}, f32[2,8,128]{2,1,0:T(8,128)S(1)}, f32[2,8,128]{2,1,0:T(8,128)S(1)}, /*index=5*/f32[2,8,128]{2,1,0:T...) while((s32[]{:T(128)}, f32[]{:T(128)}, f32[]{:T(128)}, ...), condition=%wide.region_27.28_spmd, body=%wide.region_9.27_spmd.sunk | while | flops 226018 | bytes 68610 | solution.py:291
  133.7 0.8 multiply_reduce_fusion.16
  134.5 9.6 %stack.266 = f32[15]{0:T(128)S(1)} concatenate(f32[1]{0:T(128)} %bitcast.135, f32[1]{0:T(128)} %bitcast.136, f32[1]{0:T(128)} %bitcast.137, f32[1]{0:T(128)} %bitcast.138, f32[1]{0:T(128)} %bitcast.139, f32[1]{0:T(128)} %bitcast.140, f32[1]{0:T(128)} %bitcast.141, f32[1]{0:T(128)} %bitcast.142, f32[1]{0:T(128)} %bitcast.143, f32[1]{0:T(128)} %bitcast.144, f32[1]{0:T(128)} %bitcast.145, ...), dimensions={0} | concatenate | bytes 120 | tf_op jit(solution)/shard_map/while/body/eval_jaxpr/stack | solution.py:275
  144.2 11.6 %all_to_all.48 = f32[16,1,15]{2,1,0:T(1,128)S(1)} all-to-all(f32[16,1,15]{2,1,0:T(1,128)S(1)} %broadcast_in_dim.72), channel_id=1, replica_groups=mesh['slab_0'=4,'slab_1'=8,'mode_0'=8,'mode_1'=2] {'mode_0','mode_1'}, dimensions={0} | all-to-all | bytes 1920 | tf_op jit(solution)/shard_map/while/body/eval_jaxpr/all_to_all | solution.py:38
  156.4 3.9 %all-to-all-start.1 = ((f32[32,1,15]{2,1,0:T(1,128)}), f32[32,1,15]{2,1,0:T(1,128)S(1)}, u32[]{:S(2)}, u32[]{:S(2)}) async-start(f32[32,1,15]{2,1,0:T(1,128)} %broadcast_in_dim.73), calls=%async_computation.1 | async-start | bytes 32768 | tf_op jit(solution)/shard_map/while/body/eval_jaxpr/all_to_all | solution.py:38
  160.3 8.5 %all-to-all-done.1 = f32[32,1,15]{2,1,0:T(1,128)S(1)} async-done(((f32[32,1,15]{2,1,0:T(1,128)}), f32[32,1,15]{2,1,0:T(1,128)S(1)}, u32[]{:S(2)}, u32[]{:S(2)}) %all-to-all-start.1) | async-done | bytes 1952 | tf_op jit(solution)/shard_map/while/body/eval_jaxpr/all_to_all | solution.py:38
  169.6 0.7 dynamic_slice.150
  171.6 0.7 dynamic_slice.151
  173.7 0.7 dynamic_slice.152
  175.7 0.7 fusion.76
  180.8 0.8 multiply_reduce_fusion.16
  181.6 9.6 %stack.266 = f32[15]{0:T(128)S(1)} concatenate(f32[1]{0:T(128)} %bitcast.135, f32[1]{0:T(128)} %bitcast.136, f32[1]{0:T(128)} %bitcast.137, f32[1]{0:T(128)} %bitcast.138, f32[1]{0:T(128)} %bitcast.139, f32[1]{0:T(128)} %bitcast.140, f32[1]{0:T(128)} %bitcast.141, f32[1]{0:T(128)} %bitcast.142, f32[1]{0:T(128)} %bitcast.143, f32[1]{0:T(128)} %bitcast.144, f32[1]{0:T(128)} %bitcast.145, ...), dimensions={0} | concatenate | bytes 120 | tf_op jit(solution)/shard_map/while/body/eval_jaxpr/stack | solution.py:275
  191.2 11.3 %all_to_all.48 = f32[16,1,15]{2,1,0:T(1,128)S(1)} all-to-all(f32[16,1,15]{2,1,0:T(1,128)S(1)} %broadcast_in_dim.72), channel_id=1, replica_groups=mesh['slab_0'=4,'slab_1'=8,'mode_0'=8,'mode_1'=2] {'mode_0','mode_1'}, dimensions={0} | all-to-all | bytes 1920 | tf_op jit(solution)/shard_map/while/body/eval_jaxpr/all_to_all | solution.py:38
  203.2 3.9 %all-to-all-start.1 = ((f32[32,1,15]{2,1,0:T(1,128)}), f32[32,1,15]{2,1,0:T(1,128)S(1)}, u32[]{:S(2)}, u32[]{:S(2)}) async-start(f32[32,1,15]{2,1,0:T(1,128)} %broadcast_in_dim.73), calls=%async_computation.1 | async-start | bytes 32768 | tf_op jit(solution)/shard_map/while/body/eval_jaxpr/all_to_all | solution.py:38
  207.1 8.5 %all-to-all-done.1 = f32[32,1,15]{2,1,0:T(1,128)S(1)} async-done(((f32[32,1,15]{2,1,0:T(1,128)}), f32[32,1,15]{2,1,0:T(1,128)S(1)}, u32[]{:S(2)}, u32[]{:S(2)}) %all-to-all-start.1) | async-done | bytes 1952 | tf_op jit(solution)/shard_map/while/body/eval_jaxpr/all_to_all | solution.py:38
  216.4 0.7 dynamic_slice.150
  218.5 0.7 dynamic_slice.151
  220.5 0.7 dynamic_slice.152
  222.5 0.7 fusion.76
  227.6 0.8 multiply_reduce_fusion.16
  228.4 9.6 %stack.266 = f32[15]{0:T(128)S(1)} concatenate(f32[1]{0:T(128)} %bitcast.135, f32[1]{0:T(128)} %bitcast.136, f32[1]{0:T(128)} %bitcast.137, f32[1]{0:T(128)} %bitcast.138, f32[1]{0:T(128)} %bitcast.139, f32[1]{0:T(128)} %bitcast.140, f32[1]{0:T(128)} %bitcast.141, f32[1]{0:T(128)} %bitcast.142, f32[1]{0:T(128)} %bitcast.143, f32[1]{0:T(128)} %bitcast.144, f32[1]{0:T(128)} %bitcast.145, ...), dimensions={0} | concatenate | bytes 120 | tf_op jit(solution)/shard_map/while/body/eval_jaxpr/stack | solution.py:275
  238.0 11.3 %all_to_all.48 = f32[16,1,15]{2,1,0:T(1,128)S(1)} all-to-all(f32[16,1,15]{2,1,0:T(1,128)S(1)} %broadcast_in_dim.72), channel_id=1, replica_groups=mesh['slab_0'=4,'slab_1'=8,'mode_0'=8,'mode_1'=2] {'mode_0','mode_1'}, dimensions={0} | all-to-all | bytes 1920 | tf_op jit(solution)/shard_map/while/body/eval_jaxpr/all_to_all | solution.py:38
  250.0 3.9 %all-to-all-start.1 = ((f32[32,1,15]{2,1,0:T(1,128)}), f32[32,1,15]{2,1,0:T(1,128)S(1)}, u32[]{:S(2)}, u32[]{:S(2)}) async-start(f32[32,1,15]{2,1,0:T(1,128)} %broadcast_in_dim.73), calls=%async_computation.1 | async-start | bytes 32768 | tf_op jit(solution)/shard_map/while/body/eval_jaxpr/all_to_all | solution.py:38
  253.9 8.5 %all-to-all-done.1 = f32[32,1,15]{2,1,0:T(1,128)S(1)} async-done(((f32[32,1,15]{2,1,0:T(1,128)}), f32[32,1,15]{2,1,0:T(1,128)S(1)}, u32[]{:S(2)}, u32[]{:S(2)}) %all-to-all-start.1) | async-done | bytes 1952 | tf_op jit(solution)/shard_map/while/body/eval_jaxpr/all_to_all | solution.py:38
  263.2 0.7 dynamic_slice.150
  265.3 0.7 dynamic_slice.151
  267.3 0.7 dynamic_slice.152
  269.3 0.7 fusion.76
  (113 shorter events, 10.7 us)
Async XLA Ops:
  0.6 8.6 %collective-permute-start = (f32[2,8,128]{2,1,0:T(8,128)}, f32[2,8,128]{2,1,0:T(8,128)S(1)}, u32[]{:S(2)}, u32[]{:S(2)}) collective-permute-start(f32[2,8,128]{2,1,0:T(8,128)} %param.8), channel_id=1, source_target_pairs={{0,16},{16,32},{32,48},{48,64},{64,80},{80,96},{96,112},{112,128},... | collective-permute-start | bytes 24584 | tf_op jit(solution)/shard_map/ppermute | solution.py:30
  5.5 5.3 %collective-permute-start.1 = (f32[2,8,128]{2,1,0:T(8,128)}, f32[2,8,128]{2,1,0:T(8,128)S(1)}, u32[]{:S(2)}, u32[]{:S(2)}) collective-permute-start(f32[2,8,128]{2,1,0:T(8,128)} %param.8), channel_id=1, source_target_pairs={{16,0},{32,16},{48,32},{64,48},{80,64},{96,80},{112,96},{128,112},... | collective-permute-start | bytes 24584 | tf_op jit(solution)/shard_map/ppermute | solution.py:31
  7.7 12.7 %collective-permute-start.4 = (f32[1,3,128,128]{3,2,1,0:T(8,128)S(1)}, f32[1,3,128,128]{3,2,1,0:T(8,128)S(1)}, u32[]{:S(2)}, u32[]{:S(2)}) collective-permute-start(f32[1,3,128,128]{3,2,1,0:T(8,128)S(1)} %slice_bitcast_fusion), channel_id=1, source_target_pairs={{16,0},{32,16},{48,32},{64,48},{80,64},{96,80},{112,96},{128,112},... | collective-permute-start | bytes 589832 | tf_op jit(solution)/shard_map/ppermute | solution.py:68
  10.7 8.5 %collective-permute-start.3 = (f32[6,2,128]{2,1,0:T(2,128)S(1)}, f32[6,2,128]{2,1,0:T(2,128)S(1)}, u32[]{:S(2)}, u32[]{:S(2)}) collective-permute-start(f32[6,2,128]{2,1,0:T(2,128)S(1)} %get-tuple-element.285), channel_id=1, source_target_pairs={{1,0},{2,1},{3,2},{4,3},{5,4},{6,5},{7,6},{8,7},{9,8},{10,9},{11,1... | collective-permute-start | bytes 18440 | tf_op jit(solution)/shard_map/ppermute | solution.py:31
  16.5 3.1 %collective-permute-start.2 = (f32[6,2,128]{2,1,0:T(2,128)S(1)}, f32[6,2,128]{2,1,0:T(2,128)S(1)}, u32[]{:S(2)}, u32[]{:S(2)}) collective-permute-start(f32[6,2,128]{2,1,0:T(2,128)S(1)} %get-tuple-element.284), channel_id=1, source_target_pairs={{0,1},{1,2},{2,3},{3,4},{4,5},{5,6},{6,7},{7,8},{8,9},{9,10},{10,1... | collective-permute-start | bytes 18440 | tf_op jit(solution)/shard_map/ppermute | solution.py:30
  21.7 8.9 %copy-start = (f32[48,24]{1,0:T(8,128)S(1)}, f32[48,24]{1,0:T(8,128)}, u32[]{:S(2)}) copy-start(f32[48,24]{1,0:T(8,128)} %constant.216.clone..sunk.2) | copy-start | bytes 13828
  22.4 31.6 %all-to-all-start.2 = ((f32[16,2,8,128]{3,2,1,0:T(8,128)}), f32[16,2,8,128]{3,2,1,0:T(8,128)S(1)}, u32[]{:S(2)}, u32[]{:S(2)}) async-start(f32[16,2,8,128]{3,2,1,0:T(8,128)} %broadcast_in_dim.27), calls=%async_computation.2 | async-start | bytes 262144 | tf_op jit(solution)/shard_map/all_to_all | solution.py:38
  54.0 79.1 %copy-start.1 = (f32[2,8,128]{2,1,0:T(8,128)S(1)}, f32[2,8,128]{2,1,0:T(8,128)}, u32[]{:S(2)}) copy-start(f32[2,8,128]{2,1,0:T(8,128)} %param.8) | copy-start | bytes 24580
  54.6 14.2 %all-to-all-start.4 = ((f32[16,1,1]{2,1,0:T(1,128)}), f32[16,1,1]{2,1,0:T(1,128)S(1)}, u32[]{:S(2)}, u32[]{:S(2)}) async-start(f32[16,1,1]{2,1,0:T(1,128)} %broadcast_in_dim.29), calls=%async_computation.4 | async-start | bytes 16384 | tf_op jit(solution)/shard_map/all_to_all | solution.py:38
  68.8 13.1 %all-to-all-start.3 = ((f32[16,2,8,128]{3,2,1,0:T(8,128)}), f32[16,2,8,128]{3,2,1,0:T(8,128)S(1)}, u32[]{:S(2)}, u32[]{:S(2)}) async-start(f32[16,2,8,128]{3,2,1,0:T(8,128)} %copy.36), calls=%async_computation.3 | async-start | bytes 262144 | tf_op jit(solution)/shard_map/all_to_all | solution.py:78
  82.7 5.9 %collective-permute-start.6 = (f32[2,8,128]{2,1,0:T(8,128)S(1)}, f32[2,8,128]{2,1,0:T(8,128)S(1)}, u32[]{:S(2)}, u32[]{:S(2)}) collective-permute-start(f32[2,8,128]{2,1,0:T(8,128)S(1)} %fusion.33), channel_id=1, source_target_pairs={{16,0},{32,16},{48,32},{64,48},{80,64},{96,80},{112,96},{128,112},... | collective-permute-start | bytes 24584 | tf_op jit(solution)/shard_map/ppermute | solution.py:31
  84.0 5.4 %collective-permute-start.5 = (f32[2,8,128]{2,1,0:T(8,128)S(1)}, f32[2,8,128]{2,1,0:T(8,128)S(1)}, u32[]{:S(2)}, u32[]{:S(2)}) collective-permute-start(f32[2,8,128]{2,1,0:T(8,128)S(1)} %fusion.33), channel_id=1, source_target_pairs={{0,16},{16,32},{32,48},{48,64},{64,80},{80,96},{96,112},{112,128},... | collective-permute-start | bytes 24584 | tf_op jit(solution)/shard_map/ppermute | solution.py:30
  89.4 43.5 %collective-permute-start.8 = (f32[6,2,128]{2,1,0:T(2,128)S(1)}, f32[6,2,128]{2,1,0:T(2,128)S(1)}, u32[]{:S(2)}, u32[]{:S(2)}) collective-permute-start(f32[6,2,128]{2,1,0:T(2,128)S(1)} %get-tuple-element.283), channel_id=1, source_target_pairs={{1,0},{2,1},{3,2},{4,3},{5,4},{6,5},{7,6},{8,7},{9,8},{10,9},{11,1... | collective-permute-start | bytes 18440 | tf_op jit(solution)/shard_map/ppermute | solution.py:31
  91.8 41.1 %collective-permute-start.7 = (f32[6,2,128]{2,1,0:T(2,128)S(1)}, f32[6,2,128]{2,1,0:T(2,128)S(1)}, u32[]{:S(2)}, u32[]{:S(2)}) collective-permute-start(f32[6,2,128]{2,1,0:T(2,128)S(1)} %get-tuple-element.282), channel_id=1, source_target_pairs={{0,1},{1,2},{2,3},{3,4},{4,5},{5,6},{6,7},{7,8},{8,9},{9,10},{10,1... | collective-permute-start | bytes 18440 | tf_op jit(solution)/shard_map/ppermute | solution.py:30
  96.1 10.2 %all-to-all-start.5 = ((f32[16,1,1]{2,1,0:T(1,128)}), f32[16,1,1]{2,1,0:T(1,128)S(1)}, u32[]{:S(2)}, u32[]{:S(2)}) async-start(f32[16,1,1]{2,1,0:T(1,128)} %broadcast_in_dim.30), calls=%async_computation.5 | async-start | bytes 16384 | tf_op jit(solution)/shard_map/all_to_all | solution.py:38
  108.3 24.0 %all-to-all-start.6 = ((f32[32,1,1]{2,1,0:T(1,128)}), f32[32,1,1]{2,1,0:T(1,128)S(1)}, u32[]{:S(2)}, u32[]{:S(2)}) async-start(f32[32,1,1]{2,1,0:T(1,128)} %broadcast_in_dim.31), calls=%async_computation.6 | async-start | bytes 32768 | tf_op jit(solution)/shard_map/all_to_all | solution.py:38
  156.4 12.5 %all-to-all-start.1 = ((f32[32,1,15]{2,1,0:T(1,128)}), f32[32,1,15]{2,1,0:T(1,128)S(1)}, u32[]{:S(2)}, u32[]{:S(2)}) async-start(f32[32,1,15]{2,1,0:T(1,128)} %broadcast_in_dim.73), calls=%async_computation.1 | async-start | bytes 32768 | tf_op jit(solution)/shard_map/while/body/eval_jaxpr/all_to_all | solution.py:38
  203.2 12.5 %all-to-all-start.1 = ((f32[32,1,15]{2,1,0:T(1,128)}), f32[32,1,15]{2,1,0:T(1,128)S(1)}, u32[]{:S(2)}, u32[]{:S(2)}) async-start(f32[32,1,15]{2,1,0:T(1,128)} %broadcast_in_dim.73), calls=%async_computation.1 | async-start | bytes 32768 | tf_op jit(solution)/shard_map/while/body/eval_jaxpr/all_to_all | solution.py:38
  250.0 12.5 %all-to-all-start.1 = ((f32[32,1,15]{2,1,0:T(1,128)}), f32[32,1,15]{2,1,0:T(1,128)S(1)}, u32[]{:S(2)}, u32[]{:S(2)}) async-start(f32[32,1,15]{2,1,0:T(1,128)} %broadcast_in_dim.73), calls=%async_computation.1 | async-start | bytes 32768 | tf_op jit(solution)/shard_map/while/body/eval_jaxpr/all_to_all | solution.py:38
  273.7 0.7 copy-start.2
where the time goes:
time: 276 us; the launch traced here: 274 us
  starting transfers between devices  76.2 us (28%)
  waiting for transfers between devices  57.7 us (21%)
  local copies, waits for them, and re-layouts  49.1 us (18%)
  loops' own time  40.6 us (15%)
  blocking collectives  34.2 us (12%)
  other arithmetic  9.48 us (3%)
  matrix products  5.45 us (2%)
    all_to_all x7, waiting for transfers between devices, sent_to_all(): lax.all_to_all(jnp.broadcast_to(value[None], (count, *value.shape)), axis...  47.4 us
    all_to_all x7, starting transfers between devices, sent_to_all(): lax.all_to_all(jnp.broadcast_to(value[None], (count, *value.shape)), axis...  45.6 us
    all_to_all x3, blocking collectives, sent_to_all(): lax.all_to_all(jnp.broadcast_to(value[None], (count, *value.shape)), axis...  34.2 us
    another operation x3, local copies, waits for them, and re-layouts, bracket(): jnp.stack([jnp.sum(update(design, sensitivity, measure, candidate) * meas...  28.9 us
    another operation x1, loops' own time, local(): lower, upper = lax.fori_loop(0, BISECT // 4, bracket, start_bounds)  27.6 us
    ppermute x4, starting transfers between devices, padded_2(): before = lax.ppermute(last, axis, up)  14.5 us
    another operation x1, loops' own time, element_forms(): stiff_blocks, mass_blocks = lax.map(one_block, starts)  13 us
    ppermute x4, starting transfers between devices, padded_2(): after = lax.ppermute(leading, axis, down)  10.8 us
  transfers between devices with their start and end apart: 17, of which 10 were waited for; matrix products, arithmetic and copies ran while one was open for 7% of the time, Pallas kernels for 0%

commit v1 on v0

v1 whole, which is shorter than its diff:
```python
import functools

import jax
import jax.numpy as jnp
import numpy as np
from jax import lax
from jax.experimental import pallas as pl
from jax.experimental.pallas import tpu as pltpu
from jax.sharding import PartitionSpec as P

FR = 3
KS_SHARP = 2.0
PENALTY = 3.0
FLOOR_MODULUS = 0.001
MOVE_LIMIT = 0.2
POISSON = 0.3
LEVEL_LOW = -14.0
LEVEL_HIGH = 14.0
FAN = 64
COARSE = (LEVEL_HIGH - LEVEL_LOW) / FAN
FINE = COARSE / FAN
SUB, LANE = 8, 128
F32 = jnp.float32
VMEM = pl.BlockSpec(memory_space=pltpu.VMEM)
SMEM = pl.BlockSpec(memory_space=pltpu.SMEM)


def tent_1d(values):
    padded = np.pad(values, FR - 1)
    n = len(values)
    return sum((FR - abs(o)) * padded[FR - 1 + o : FR - 1 + o + n] for o in range(1 - FR, FR))


def edge_tables(n):
    span = tent_1d(np.ones(n))
    return 1.0 / span, tent_1d(1.0 / span)


def along(position, n, table):
    middle = float(table[n // 2])
    value = jnp.where(position >= 0, F32(middle), F32(0.0))
    for k in range(2 * (FR - 1)):
        if abs(table[k] - middle) > 1e-12:
            value = jnp.where((position == k) | (position == n - 1 - k), F32(table[k]), value)
    return value


def iota(shape, axis):
    return lax.broadcasted_iota(jnp.int32, shape, axis)


def tent_lanes(v):
    lanes = iota(v.shape, v.ndim - 1)
    axis = v.ndim - 1
    total = 3.0 * v
    for o in (1, 2):
        above = jnp.where(lanes < LANE - o, pltpu.roll(v, LANE - o, axis), 0.0)
        below = jnp.where(lanes >= o, pltpu.roll(v, o, axis), 0.0)
        total = total + float(FR - o) * (above + below)
    return total


def forms(load, eigen, store, pairs, tiles):
    lame = POISSON / ((1.0 + POISSON) * (1.0 - 2.0 * POISSON))
    shear = 0.5 / (1.0 + POISSON)
    rows = tiles * SUB
    lanes = iota((rows, LANE), 1)
    for c in range(3):
        for a in (0, 1):
            u = load(c, a)
            up = jnp.where(lanes < LANE - 1, pltpu.roll(u, LANE - 1, 1), 0.0)
            pairs[c, a, 0, :rows] = up + u
            pairs[c, a, 1, :rows] = up - u
            pairs[c, a, :, rows:] = jnp.zeros((2, SUB, LANE), F32)
    eigen_v = jnp.full((SUB, LANE), eigen, F32)
    weight = jnp.exp(-KS_SHARP * eigen_v)
    eigen_weight = weight * eigen_v
    normal = lame + 2.0 * shear
    ms, md = 0.25, 1.0 / 12.0
    m0, m1, m2, m3 = ms**3, ms * ms * md, ms * md * md, md**3

    def tile(r, _):
        base = pl.multiple_of(r * SUB, SUB)
        coef = {}
        for c in range(3):
            planes = []
            for a in (0, 1):
                here = {}
                for z in (0, 1):
                    p0 = pairs[c, a, z, pl.ds(base, SUB)]
                    p1 = pairs[c, a, z, pl.ds(base + 1, SUB)]
                    here[0, z] = p1 + p0
                    here[1, z] = p1 - p0
                planes.append(here)
            for y in (0, 1):
                for z in (0, 1):
                    coef[c, 0, y, z] = planes[1][y, z] + planes[0][y, z]
                    coef[c, 1, y, z] = planes[1][y, z] - planes[0][y, z]
        groups = [None] * 6
        for c in range(3):
            for x in (0, 1):
                for y in (0, 1):
                    for z in (0, 1):
                        d = (x, y, z)
                        n = x + y + z
                        g = {0: 0, 1: 1 if d[c] else 2, 2: 3 if d[c] else 4, 3: 5}[n]
                        v = coef[c, x, y, z]
                        groups[g] = v * v if groups[g] is None else groups[g] + v * v
        mass = m0 * groups[0] + m1 * (groups[1] + groups[2]) + m2 * (groups[3] + groups[4]) + m3 * groups[5]
        stiff = (
            (12.0 * m1 * normal) * groups[1]
            + (12.0 * m1 * shear) * groups[2]
            + (12.0 * m2 * (normal + shear)) * groups[3]
            + (12.0 * m2 * 2.0 * shear) * groups[4]
            + (12.0 * m3 * (normal + 2.0 * shear)) * groups[5]
        )
        for third in (0, 1):
            along_sum = across_sum = None
            for i, j, k in ((0, 1, 2), (0, 2, 1), (1, 2, 0)):

                def at(c, di, dj):
                    d = [0, 0, 0]
                    d[i], d[j], d[k] = di, dj, third
                    return coef[c, d[0], d[1], d[2]]

                t = at(i, 1, 0) * at(j, 0, 1)
                s = at(i, 0, 1) * at(j, 1, 0)
                along_sum = t if along_sum is None else along_sum + t
                across_sum = s if across_sum is None else across_sum + s
            m = (ms, md)[third] * 0.25
            stiff = stiff + (2.0 * lame * m) * along_sum + (2.0 * shear * m) * across_sum
        store(r, weight * stiff, eigen_weight * mass)
        return 0

    lax.fori_loop(0, tiles, tile, 0, unroll=2)
    return weight


def first_layer(modes, eigen, design, out, pairs):
    def store(r, stiff, mass):
        out[r, 0] = stiff
        out[r, 1] = mass

    tiles = out.shape[0]
    weight = forms(lambda c, a: modes[0, c, a], eigen[0], store, pairs, tiles)
    for r in range(tiles):
        out[r, 2] = design[0]
        out[r, 3] = design[1]
        out[r, 4] = weight


def second_layer(modes, plane, eigen, out, pairs):
    def store(r, stiff, mass):
        out[r, 0] = stiff
        out[r, 1] = mass

    def load(c, a):
        return plane[0, c] if a else modes[0, c, 1]

    forms(load, eigen[0], store, pairs, out.shape[0])


def own_sums(got, sums, rows_out, padded, *, mode):
    tiles = got.shape[0]
    m = lax.axis_index(mode)
    for k, at in enumerate((0, 1, 4)):
        total = got[0, at]
        for r in range(1, tiles):
            total = total + got[r, at]
        sums[k] = total
    for l in (0, 1):
        padded[l, :SUB] = jnp.zeros((SUB, LANE), F32)
        padded[l, (tiles + 1) * SUB :] = jnp.zeros((SUB, LANE), F32)
        for r in range(tiles):
            padded[l, (r + 1) * SUB : (r + 2) * SUB] = got[r, 2 + l]
    for l in (0, 1):
        total = None
        for o in range(1 - FR, FR):
            t = float(FR - abs(o)) * padded[l, pl.ds(m * SUB + SUB + o, SUB)]
            total = t if total is None else total + t
        rows_out[l] = tent_lanes(total)


def across_x(own, before, after):
    first = before[0] + 2.0 * before[1] + 3.0 * own[0] + 2.0 * own[1] + after[0]
    second = before[1] + 2.0 * own[0] + 3.0 * own[1] + 2.0 * after[0] + after[1]
    return first, second


def own_gradient(got, sums, rows, before, after, out, *, slab, mode, sizes):
    total_x, total_y, total_z = sizes
    tiles = got.shape[0]
    s, m = lax.axis_index(slab), lax.axis_index(mode)
    later = []
    for at in (0, 1):
        total = got[0, at]
        for r in range(1, tiles):
            total = total + got[r, at]
        later.append(total)
    stiff = (sums[0], later[0])
    mass = (sums[1], later[1])
    inverse_yz = along(m * SUB + iota((SUB, LANE), 0), total_y, edge_tables(total_y)[0]) * along(
        iota((SUB, LANE), 1), total_z, edge_tables(total_z)[0]
    )
    filtered = across_x(rows, before, after)
    inverse_weight = 1.0 / sums[2]
    for l in (0, 1):
        x = jnp.full((SUB, LANE), 2 * s + l, jnp.int32)
        inverse = inverse_yz * along(x, total_x, edge_tables(total_x)[0])
        density = filtered[l] * inverse
        slope = (PENALTY * (1.0 - FLOOR_MODULUS)) * density * density
        out[l] = tent_lanes((slope * stiff[l] - mass[l]) * inverse_weight * inverse)


def gradient_copies(own, before, after, out):
    pair = across_x(own, before, after)
    for r in range(out.shape[0]):
        out[r, 0] = pair[0]
        out[r, 1] = pair[1]


def measure_xz(slab, total_x, total_z):
    s = lax.axis_index(slab)
    z = along(iota((SUB, LANE), 1), total_z, edge_tables(total_z)[1])
    return [
        z * along(jnp.full((SUB, LANE), 2 * s + l, jnp.int32), total_x, edge_tables(total_x)[1])
        for l in (0, 1)
    ]


def volumes(levels, gain, least, most, parts):
    count = gain.shape[0]
    for start in range(0, len(levels), 8):
        chunk = levels[start : start + 8]

        def body(v, totals):
            g, lo, hi = gain[v], least[v], most[v]
            return tuple(
                t + jnp.minimum(jnp.maximum(g * q, lo), hi) for t, q in zip(totals, chunk)
            )

        zeros = tuple(jnp.zeros((SUB, LANE), F32) for _ in chunk)
        totals = lax.fori_loop(0, count, body, zeros, unroll=4)
        for i, t in enumerate(totals):
            parts[start + i : start + i + 1] = jnp.sum(t, axis=0, keepdims=True)


def lane_totals(parts):
    column = jnp.sum(parts[...], axis=1, keepdims=True)
    shape = (FAN, LANE)
    spread = jnp.where(iota(shape, 0) == iota(shape, 1), jnp.broadcast_to(column, shape), 0.0)
    return jnp.sum(spread, axis=0, keepdims=True)


def first_round(got, early, gain, least, most, own, out, padded, parts, *, slab, mode, sizes):
    total_x, total_y, total_z = sizes
    tiles = got.shape[0]
    m = lax.axis_index(mode)
    for l in (0, 1):
        padded[l, :SUB] = jnp.zeros((SUB, LANE), F32)
        padded[l, (tiles + 1) * SUB :] = jnp.zeros((SUB, LANE), F32)
        for r in range(tiles):
            padded[l, (r + 1) * SUB : (r + 2) * SUB] = got[r, l]
    xz = measure_xz(slab, total_x, total_z)
    goal = jnp.zeros((SUB, LANE), F32)
    for l in (0, 1):
        for r in range(tiles):
            total = None
            for o in range(1 - FR, FR):
                start = (r + 1) * SUB + o
                t = float(FR - abs(o)) * padded[l, start : start + SUB]
                total = t if total is None else total + t
            measure = xz[l] * along(r * SUB + iota((SUB, LANE), 0), total_y, edge_tables(total_y)[1])
            design = early[r, 2 + l]
            at = l * tiles + r
            gain[at] = design * jnp.sqrt(jnp.maximum(total, 0.0) * measure)
            least[at] = jnp.maximum(design - MOVE_LIMIT, 0.0) * measure
            most[at] = jnp.minimum(design + MOVE_LIMIT, 1.0) * measure
            goal = goal + design * measure
        total = None
        for o in range(1 - FR, FR):
            t = float(FR - abs(o)) * padded[l, pl.ds(m * SUB + SUB + o, SUB)]
            total = t if total is None else total + t
        own[l] = total
    levels = [float(np.exp(-0.5 * (LEVEL_LOW + COARSE * (i + 1)))) for i in range(FAN - 1)]
    volumes(levels, gain, least, most, parts)
    parts[FAN - 1 : FAN] = jnp.sum(goal, axis=0, keepdims=True)
    row = lane_totals(parts)
    for k in range(out.shape[0]):
        out[k] = row


def added(got):
    total = got[0]
    for k in range(1, got.shape[0]):
        total = total + got[k]
    return total


def at_lane(row, k):
    return jnp.sum(jnp.where(iota(row.shape, 1) == k, row, 0.0), axis=1, keepdims=True)


def cells_above(row, goal):
    above = (row > goal) & (iota(row.shape, 1) < FAN - 1)
    return jnp.sum(jnp.where(above, 1.0, 0.0), axis=1, keepdims=True)


def second_round(got, gain, least, most, out, state, parts):
    row = added(got)
    goal = at_lane(row, FAN - 1)
    low = LEVEL_LOW + COARSE * cells_above(row, goal)
    state[0:1] = jnp.broadcast_to(low, (1, LANE))
    state[1:2] = jnp.broadcast_to(goal, (1, LANE))
    scale = jnp.exp(-0.5 * jnp.broadcast_to(low, (SUB, LANE)))
    levels = [scale * float(np.exp(-0.5 * FINE * (i + 1))) for i in range(FAN - 1)]
    volumes(levels, gain, least, most, parts)
    parts[FAN - 1 : FAN] = jnp.zeros((1, LANE), F32)
    row = lane_totals(parts)
    for k in range(out.shape[0]):
        out[k] = row


def last_update(got, state, own, design, sens_out, out, *, slab, mode, sizes):
    total_x, total_y, total_z = sizes
    m = lax.axis_index(mode)
    row = added(got)
    goal = state[1:2, 0:1]
    level = state[0:1, 0:1] + FINE * (cells_above(row, goal) + 0.5)
    scale = jnp.exp(jnp.broadcast_to(level, (SUB, LANE)))
    y = along(m * SUB + iota((SUB, LANE), 0), total_y, edge_tables(total_y)[1])
    xz = measure_xz(slab, total_x, total_z)
    for l in (0, 1):
        d, s = design[l], own[l]
        factor = jnp.sqrt(jnp.maximum(s, 0.0) / (scale * (xz[l] * y)))
        least = jnp.maximum(d - MOVE_LIMIT, 0.0)
        most = jnp.minimum(d + MOVE_LIMIT, 1.0)
        out[l] = jnp.minimum(jnp.maximum(d * factor, least), most)
        sens_out[l] = s


def call(kernel, outs, operands, specs=None, scratch=(), flops=1000, name=None):
    outs = [jax.ShapeDtypeStruct(o, F32) for o in outs]
    size = sum(4 * int(np.prod(o.shape)) for o in (*outs, *operands))
    single = len(outs) == 1
    return pl.pallas_call(
        kernel,
        out_shape=outs[0] if single else outs,
        in_specs=specs or [VMEM] * len(operands),
        out_specs=VMEM if single else [VMEM] * len(outs),
        scratch_shapes=[pltpu.VMEM(s, F32) for s in scratch],
        cost_estimate=pl.CostEstimate(flops=flops, bytes_accessed=size, transcendentals=0),
        name=name,
    )(*operands)


def neighbours(value, axis):
    count = lax.axis_size(axis)
    up = [(i, i + 1) for i in range(count - 1)]
    down = [(j, i) for i, j in up]
    return lax.ppermute(value, axis, up), lax.ppermute(value, axis, down)


def exchange(value, axis):
    return lax.all_to_all(value, axis, 0, 0, tiled=True)


def local(design, mode_shapes, eigenvalues):
    slab, mode = "slab", "mode"
    slabs, modes = lax.axis_size(slab), lax.axis_size(mode)
    _, _, _, total_y, total_z = mode_shapes.shape
    sizes = (2 * slabs, total_y, total_z)
    pairs = (3, 2, 2, total_y + SUB, LANE)
    block = (2, SUB, LANE)
    padded = (2, total_y + 2 * SUB, LANE)
    place = dict(slab=slab, mode=mode, sizes=sizes)

    down = [(i + 1, i) for i in range(slabs - 1)]
    plane = lax.ppermute(mode_shapes[:, :, 0], slab, down)
    early = call(
        first_layer,
        [(modes, 5, SUB, LANE)],
        [mode_shapes, eigenvalues, design],
        specs=[VMEM, SMEM, VMEM],
        scratch=[pairs],
        flops=5_000_000,
        name="first_layer",
    )
    early = exchange(early, mode)
    late = call(
        second_layer,
        [(modes, 2, SUB, LANE)],
        [mode_shapes, plane, eigenvalues],
        specs=[VMEM, VMEM, SMEM],
        scratch=[pairs],
        flops=5_000_000,
        name="second_layer",
    )
    late = exchange(late, mode)
    sums, rows = call(
        functools.partial(own_sums, mode=mode),
        [(3, SUB, LANE), block],
        [early],
        scratch=[padded],
        name="own_sums",
    )
    before, after = neighbours(rows, slab)
    gradient = call(
        functools.partial(own_gradient, **place),
        [block],
        [late, sums, rows, before, after],
        name="own_gradient",
    )
    before, after = neighbours(gradient, slab)
    copies = call(gradient_copies, [(modes, *block)], [gradient, before, after], name="copies")
    whole = exchange(copies, mode)
    vectors = 2 * modes
    gain, least, most, own, sent = call(
        functools.partial(first_round, **place),
        [(vectors, SUB, LANE)] * 3 + [block, (slabs, 1, LANE)],
        [whole, early],
        scratch=[padded, (FAN, LANE)],
        name="first_round",
    )
    got = exchange(sent, slab)
    sent, state = call(
        second_round,
        [(slabs, 1, LANE), (SUB, LANE)],
        [got, gain, least, most],
        scratch=[(FAN, LANE)],
        name="second_round",
    )
    got = exchange(sent, slab)
    return call(
        functools.partial(last_update, **place),
        [block, block],
        [got, state, own, design],
        name="last_update",
    )


def solution(mesh):
    in_specs = (P("slab", "mode", None), P("mode", None, "slab", None, None), P("mode"))
    out_specs = (P("slab", "mode", None), P("slab", "mode", None))

    def step(design, mode_shapes, eigenvalues):
        return tuple(local(design, mode_shapes, eigenvalues))

    return jax.shard_map(step, mesh=mesh, in_specs=in_specs, out_specs=out_specs, check_vma=False)
```

time: 276 us -> 119 us (0.43)
  starting transfers between devices: 76.2 us -> 27.9 us
  local copies, waits for them, and re-layouts: 49.1 us -> 1.92 us
  waiting for transfers between devices: 57.7 us -> 11.9 us
  loops' own time: 40.6 us -> 0 us
  blocking collectives: 34.2 us -> 57.9 us
  Pallas kernels: 0 us -> 17.4 us
  other arithmetic: 9.48 us -> 0 us
  matrix products: 5.45 us -> 0 us
    all_to_all x8 -> x2, waiting for transfers between devices: 55.8 us -> 4.14 us  [exchange(): return lax.all_to_all(value, axis, 0, 0, tiled=True)]
    another operation x2 -> x0, loops' own time: 40.6 us -> none  [the longest x1 27.6 us: local(): lower, upper = lax.fori_loop(0, BISECT // 4, bracket, start_bounds)]
    all_to_all x8 -> x2, starting transfers between devices: 49.6 us -> 16.1 us  [exchange(): return lax.all_to_all(value, axis, 0, 0, tiled=True)]
    another operation x10 -> x0, local copies, waits for them, and re-layouts: 29.2 us -> none  [the longest x3 28.9 us: bracket(): jnp.stack([jnp.sum(update(design, sensitivity, measure, candidate) * meas...]
    all_to_all x3, blocking collectives: 34.2 us -> 57.9 us  [exchange(): return lax.all_to_all(value, axis, 0, 0, tiled=True)]
    pallas_call x0 -> x8, Pallas kernels: none -> 17.4 us  [call(): pl.pallas_call(kernel, out_shape=outs[0] if single else outs, in_specs=sp...]
    ppermute x9 -> x5, starting transfers between devices: 26.6 us -> 11.8 us  [the longest x4 10.5 us: neighbours(): return (lax.ppermute(value, axis, up), lax.ppermute(value, axis, down))]
    dynamic_slice x16 -> x0, local copies, waits for them, and re-layouts: 10.6 us -> none  [the longest x9 6 us: bracket(): above = volumes[heap_slot] > target]
  transfers between devices with their start and end apart: 17 -> 7, of which waited for: 10 -> 4; matrix products, arithmetic and copies ran while one was open for 7% -> 0% of each run, Pallas kernels for 0% -> 3%
where the time goes in v1:
time: 119 us; the launch traced here: 118 us
  blocking collectives  57.9 us (49%)
  starting transfers between devices  27.9 us (23%)
  Pallas kernels  17.4 us (15%)
  waiting for transfers between devices  11.9 us (10%)
  local copies, waits for them, and re-layouts  1.92 us (2%)
  between operations  1.37 us (1%)
    all_to_all x3, blocking collectives, exchange(): return lax.all_to_all(value, axis, 0, 0, tiled=True)  57.9 us
    pallas_call x8, Pallas kernels, call(): pl.pallas_call(kernel, out_shape=outs[0] if single else outs, in_specs=sp...  17.4 us
    all_to_all x2, starting transfers between devices, exchange(): return lax.all_to_all(value, axis, 0, 0, tiled=True)  16.1 us
    ppermute x4, starting transfers between devices, neighbours(): return (lax.ppermute(value, axis, up), lax.ppermute(value, axis, down))  10.5 us
    ppermute x1, waiting for transfers between devices, local(): plane = lax.ppermute(mode_shapes[:, :, 0], slab, down)  6.83 us
    all_to_all x2, waiting for transfers between devices, exchange(): return lax.all_to_all(value, axis, 0, 0, tiled=True)  4.14 us
  transfers between devices with their start and end apart: 7, of which 4 were waited for; matrix products, arithmetic and copies ran while one was open for 0% of the time, Pallas kernels for 3%

profile of v1, /device:TPU:1, one launch (start us, length us, event | category | flops | bytes accessed | tf_op | source)
XLA Modules:
  0.0 118.4 jit_solution(16742799802607163155)
XLA Ops:
  1.3 2.3 %first_layer.1 = f32[16,5,8,128]{3,2,1,0:T(8,128)} custom-call(f32[1,3,2,128,128]{4,3,2,1,0:T(8,128)} %modes.3, f32[1]{0:T(128)S(6)} %copy.7.eigen, f32[2,8,128]{2,1,0:T(8,128)} %design.3), custom_call_target="tpu_custom_call" | custom-call | flops 5000000 | bytes 729092 | tf_op jit(solution)/shard_map/first_layer/pallas_call | solution.py:346
  3.5 0.0 copy-start.1
  3.5 10.3 %all-to-all-start.1 = ((f32[16,5,8,128]{3,2,1,0:T(8,128)}), f32[16,5,8,128]{3,2,1,0:T(8,128)S(1)}, u32[]{:S(2)}, u32[]{:S(2)}) async-start(f32[16,5,8,128]{3,2,1,0:T(8,128)} %first_layer.1), calls=%async_computation.1 | async-start | bytes 655360 | tf_op jit(solution)/shard_map/all_to_all | solution.py:365
  13.8 0.0 copy-done.1
  13.9 1.3 %collective-permute-start = (f32[1,3,128,128]{3,2,1,0:T(8,128)S(1)}, f32[1,3,128,128]{3,2,1,0:T(8,128)S(1)}, u32[]{:S(2)}, u32[]{:S(2)}) collective-permute-start(f32[1,3,128,128]{3,2,1,0:T(8,128)S(1)} %slice_bitcast_fusion), channel_id=1, source_target_pairs={{16,0},{32,16},{48,32},{64,48},{80,64},{96,80},{112,96},{128,112},... | collective-permute-start | bytes 589832 | tf_op jit(solution)/shard_map/ppermute | solution.py:379
  15.2 6.8 %collective-permute-done.plane = f32[1,3,128,128]{3,2,1,0:T(8,128)S(1)} collective-permute-done((f32[1,3,128,128]{3,2,1,0:T(8,128)S(1)}, f32[1,3,128,128]{3,2,1,0:T(8,128)S(1)}, u32[]{:S(2)}, u32[]{:S(2)}) %collective-permute-start) | collective-permute-done | bytes 196640 | tf_op jit(solution)/shard_map/ppermute | solution.py:379
  22.0 0.0 copy-start.3
  22.0 0.7 copy-done.3
  22.7 2.2 %second_layer.1 = f32[16,2,8,128]{3,2,1,0:T(8,128)} custom-call(f32[1,3,2,128,128]{4,3,2,1,0:T(8,128)} %modes.3, f32[1,3,128,128]{3,2,1,0:T(8,128)} %copy-done.3, f32[1]{0:T(128)S(6)} %copy.7.eigen), custom_call_target="tpu_custom_call" | custom-call | flops 5000000 | bytes 720900 | tf_op jit(solution)/shard_map/second_layer/pallas_call | solution.py:346
  24.9 2.2 %all-to-all-done.1.got.early = f32[16,5,8,128]{3,2,1,0:T(8,128)S(1)} async-done(((f32[16,5,8,128]{3,2,1,0:T(8,128)}), f32[16,5,8,128]{3,2,1,0:T(8,128)S(1)}, u32[]{:S(2)}, u32[]{:S(2)}) %all-to-all-start.1) | async-done | bytes 327712 | tf_op jit(solution)/shard_map/all_to_all | solution.py:365
  27.1 0.0 copy-start
  27.1 5.8 %all-to-all-start = ((f32[16,2,8,128]{3,2,1,0:T(8,128)}), f32[16,2,8,128]{3,2,1,0:T(8,128)S(1)}, u32[]{:S(2)}, u32[]{:S(2)}) async-start(f32[16,2,8,128]{3,2,1,0:T(8,128)} %second_layer.1), calls=%async_computation | async-start | bytes 262144 | tf_op jit(solution)/shard_map/all_to_all | solution.py:365
  32.9 0.0 copy-done
  32.9 1.7 %own_sums.1 = (f32[3,8,128]{2,1,0:T(8,128)}, f32[2,8,128]{2,1,0:T(8,128)}) custom-call(f32[16,5,8,128]{3,2,1,0:T(8,128)} %copy-done), custom_call_target="tpu_custom_call" | custom-call | flops 1000 | bytes 348160 | tf_op jit(solution)/shard_map/own_sums/pallas_call | solution.py:346
  34.5 1.3 %collective-permute-start.2 = (f32[2,8,128]{2,1,0:T(8,128)}, f32[2,8,128]{2,1,0:T(8,128)S(1)}, u32[]{:S(2)}, u32[]{:S(2)}) collective-permute-start(f32[2,8,128]{2,1,0:T(8,128)} %get-tuple-element.12.rows), channel_id=1, source_target_pairs={{16,0},{32,16},{48,32},{64,48},{80,64},{96,80},{112,96},{128,112},... | collective-permute-start | bytes 24584 | tf_op jit(solution)/shard_map/ppermute | solution.py:361
  35.8 4.0 %collective-permute-start.1 = (f32[2,8,128]{2,1,0:T(8,128)}, f32[2,8,128]{2,1,0:T(8,128)S(1)}, u32[]{:S(2)}, u32[]{:S(2)}) collective-permute-start(f32[2,8,128]{2,1,0:T(8,128)} %get-tuple-element.12.rows), channel_id=1, source_target_pairs={{0,16},{16,32},{32,48},{48,64},{64,80},{80,96},{96,112},{112,128},... | collective-permute-start | bytes 24584 | tf_op jit(solution)/shard_map/ppermute | solution.py:361
  39.8 1.9 %all-to-all-done.got = f32[16,2,8,128]{3,2,1,0:T(8,128)S(1)} async-done(((f32[16,2,8,128]{3,2,1,0:T(8,128)}), f32[16,2,8,128]{3,2,1,0:T(8,128)S(1)}, u32[]{:S(2)}, u32[]{:S(2)}) %all-to-all-start) | async-done | bytes 131104 | tf_op jit(solution)/shard_map/all_to_all | solution.py:365
  41.8 0.0 copy-start.2
  41.8 0.0 collective-permute-done.2.after
  41.8 0.0 copy-start.4
  41.8 0.0 collective-permute-done.1.before
  41.8 0.0 copy-start.5
  41.8 0.6 copy-done.2
  42.4 0.0 copy-done.4
  42.4 0.0 copy-done.5
  42.4 1.6 %own_gradient.1.own = f32[2,8,128]{2,1,0:T(8,128)} custom-call(f32[16,2,8,128]{3,2,1,0:T(8,128)} %copy-done.2, f32[3,8,128]{2,1,0:T(8,128)} %get-tuple-element.11.sums, f32[2,8,128]{2,1,0:T(8,128)} %get-tuple-element.12.rows, f32[2,8,128]{2,1,0:T(8,128)} %copy-done.5, f32[2,8,128]{2,1,0:T(8,128)} %copy-done.4), custom_call_target="tpu_custom_call" | custom-call | flops 1000 | bytes 176128 | tf_op jit(solution)/shard_map/own_gradient/pallas_call | solution.py:346
  44.0 1.3 %collective-permute-start.4 = (f32[2,8,128]{2,1,0:T(8,128)}, f32[2,8,128]{2,1,0:T(8,128)S(1)}, u32[]{:S(2)}, u32[]{:S(2)}) collective-permute-start(f32[2,8,128]{2,1,0:T(8,128)} %own_gradient.1.own), channel_id=1, source_target_pairs={{16,0},{32,16},{48,32},{64,48},{80,64},{96,80},{112,96},{128,112},... | collective-permute-start | bytes 24584 | tf_op jit(solution)/shard_map/ppermute | solution.py:361
  45.3 4.0 %collective-permute-start.3 = (f32[2,8,128]{2,1,0:T(8,128)}, f32[2,8,128]{2,1,0:T(8,128)S(1)}, u32[]{:S(2)}, u32[]{:S(2)}) collective-permute-start(f32[2,8,128]{2,1,0:T(8,128)} %own_gradient.1.own), channel_id=1, source_target_pairs={{0,16},{16,32},{32,48},{48,64},{64,80},{80,96},{96,112},{112,128},... | collective-permute-start | bytes 24584 | tf_op jit(solution)/shard_map/ppermute | solution.py:361
  49.3 0.0 collective-permute-done.4.after
  49.3 0.0 copy-start.6
  49.3 1.0 collective-permute-done.3.before
  50.3 0.0 copy-done.6
  50.3 0.0 copy-start.7
  50.3 0.6 copy-done.7
  50.9 1.4 %copies.1 = f32[16,2,8,128]{3,2,1,0:T(8,128)} custom-call(f32[2,8,128]{2,1,0:T(8,128)} %own_gradient.1.own, f32[2,8,128]{2,1,0:T(8,128)} %copy-done.7, f32[2,8,128]{2,1,0:T(8,128)} %copy-done.6), custom_call_target="tpu_custom_call" | custom-call | flops 1000 | bytes 155648 | tf_op jit(solution)/shard_map/copies/pallas_call | solution.py:346
  52.3 17.8 %all_to_all.25.got = f32[16,2,8,128]{3,2,1,0:T(8,128)} all-to-all(f32[16,2,8,128]{3,2,1,0:T(8,128)} %copies.1), channel_id=1, replica_groups=mesh['slab'=32,'mode'=16] {'mode'}, dimensions={0} | all-to-all | bytes 262144 | tf_op jit(solution)/shard_map/all_to_all | solution.py:365
  70.0 3.3 %first_round.1 = (f32[32,8,128]{2,1,0:T(8,128)}, f32[32,8,128]{2,1,0:T(8,128)}, f32[32,8,128]{2,1,0:T(8,128)}, f32[2,8,128]{2,1,0:T(8,128)}, f32[32,1,128]{2,1,0:T(1,128)}) custom-call(f32[16,2,8,128]{3,2,1,0:T(8,128)} %all_to_all.25.got, f32[16,5,8,128]{3,2,1,0:T(8,128)} %copy-done), custom_call_target="tpu_custom_call" | custom-call | flops 1000 | bytes 876544 | tf_op jit(solution)/shard_map/first_round/pallas_call | solution.py:346
  73.3 27.2 %all_to_all.26.got = f32[32,1,128]{2,1,0:T(1,128)} all-to-all(f32[32,1,128]{2,1,0:T(1,128)} %get-tuple-element.13), channel_id=1, replica_groups=mesh['slab'=32,'mode'=16] {'slab'}, dimensions={0} | all-to-all | bytes 32768 | tf_op jit(solution)/shard_map/all_to_all | solution.py:365
  100.5 3.4 %second_round.1 = (f32[32,1,128]{2,1,0:T(1,128)}, f32[8,128]{1,0:T(8,128)}) custom-call(f32[32,1,128]{2,1,0:T(1,128)} %all_to_all.26.got, f32[32,8,128]{2,1,0:T(8,128)} %get-tuple-element.14.gain, f32[32,8,128]{2,1,0:T(8,128)} %get-tuple-element.15.least, f32[32,8,128]{2,1,0:T(8,128)} %get-tuple-element.16.most), custom_call_target="tpu_custom_call" | custom-call | flops 1000 | bytes 430080 | tf_op jit(solution)/shard_map/second_round/pallas_call | solution.py:346
  103.9 13.0 %all_to_all.27.got = f32[32,1,128]{2,1,0:T(1,128)} all-to-all(f32[32,1,128]{2,1,0:T(1,128)} %get-tuple-element.17), channel_id=1, replica_groups=mesh['slab'=32,'mode'=16] {'slab'}, dimensions={0} | all-to-all | bytes 32768 | tf_op jit(solution)/shard_map/all_to_all | solution.py:365
  116.8 1.5 %last_update.1 = (f32[2,8,128]{2,1,0:T(8,128)}, f32[2,8,128]{2,1,0:T(8,128)}) custom-call(f32[32,1,128]{2,1,0:T(1,128)} %all_to_all.27.got, f32[8,128]{1,0:T(8,128)} %get-tuple-element.18.state, f32[2,8,128]{2,1,0:T(8,128)} %get-tuple-element.19.own, f32[2,8,128]{2,1,0:T(8,128)} %design.3), custom_call_target="tpu_custom_call" | custom-call | flops 1000 | bytes 53248 | tf_op jit(solution)/shard_map/last_update/pallas_call | solution.py:346
  (1 shorter events, 0.0 us)
Async XLA Ops:
  3.5 10.3 %copy-start.1 = (f32[1,3,2,128,128]{4,3,2,1,0:T(8,128)S(1)}, f32[1,3,2,128,128]{4,3,2,1,0:T(8,128)}, u32[]{:S(2)}) copy-start(f32[1,3,2,128,128]{4,3,2,1,0:T(8,128)} %modes.3) | copy-start | bytes 1179652
  3.5 23.6 %all-to-all-start.1 = ((f32[16,5,8,128]{3,2,1,0:T(8,128)}), f32[16,5,8,128]{3,2,1,0:T(8,128)S(1)}, u32[]{:S(2)}, u32[]{:S(2)}) async-start(f32[16,5,8,128]{3,2,1,0:T(8,128)} %first_layer.1), calls=%async_computation.1 | async-start | bytes 655360 | tf_op jit(solution)/shard_map/all_to_all | solution.py:365
  13.9 8.1 %collective-permute-start = (f32[1,3,128,128]{3,2,1,0:T(8,128)S(1)}, f32[1,3,128,128]{3,2,1,0:T(8,128)S(1)}, u32[]{:S(2)}, u32[]{:S(2)}) collective-permute-start(f32[1,3,128,128]{3,2,1,0:T(8,128)S(1)} %slice_bitcast_fusion), channel_id=1, source_target_pairs={{16,0},{32,16},{48,32},{64,48},{80,64},{96,80},{112,96},{128,112},... | collective-permute-start | bytes 589832 | tf_op jit(solution)/shard_map/ppermute | solution.py:379
  22.0 0.7 copy-start.3
  27.1 5.8 %copy-start = (f32[16,5,8,128]{3,2,1,0:T(8,128)}, f32[16,5,8,128]{3,2,1,0:T(8,128)S(1)}, u32[]{:S(2)}) copy-start(f32[16,5,8,128]{3,2,1,0:T(8,128)S(1)} %all-to-all-done.1.got.early) | copy-start | bytes 983044
  27.1 14.6 %all-to-all-start = ((f32[16,2,8,128]{3,2,1,0:T(8,128)}), f32[16,2,8,128]{3,2,1,0:T(8,128)S(1)}, u32[]{:S(2)}, u32[]{:S(2)}) async-start(f32[16,2,8,128]{3,2,1,0:T(8,128)} %second_layer.1), calls=%async_computation | async-start | bytes 262144 | tf_op jit(solution)/shard_map/all_to_all | solution.py:365
  34.5 7.2 %collective-permute-start.2 = (f32[2,8,128]{2,1,0:T(8,128)}, f32[2,8,128]{2,1,0:T(8,128)S(1)}, u32[]{:S(2)}, u32[]{:S(2)}) collective-permute-start(f32[2,8,128]{2,1,0:T(8,128)} %get-tuple-element.12.rows), channel_id=1, source_target_pairs={{16,0},{32,16},{48,32},{64,48},{80,64},{96,80},{112,96},{128,112},... | collective-permute-start | bytes 24584 | tf_op jit(solution)/shard_map/ppermute | solution.py:361
  35.8 5.9 %collective-permute-start.1 = (f32[2,8,128]{2,1,0:T(8,128)}, f32[2,8,128]{2,1,0:T(8,128)S(1)}, u32[]{:S(2)}, u32[]{:S(2)}) collective-permute-start(f32[2,8,128]{2,1,0:T(8,128)} %get-tuple-element.12.rows), channel_id=1, source_target_pairs={{0,16},{16,32},{32,48},{48,64},{64,80},{80,96},{96,112},{112,128},... | collective-permute-start | bytes 24584 | tf_op jit(solution)/shard_map/ppermute | solution.py:361
  41.8 0.6 copy-start.2
  41.8 0.6 copy-start.4
  41.8 0.6 copy-start.5
  44.0 5.3 %collective-permute-start.4 = (f32[2,8,128]{2,1,0:T(8,128)}, f32[2,8,128]{2,1,0:T(8,128)S(1)}, u32[]{:S(2)}, u32[]{:S(2)}) collective-permute-start(f32[2,8,128]{2,1,0:T(8,128)} %own_gradient.1.own), channel_id=1, source_target_pairs={{16,0},{32,16},{48,32},{64,48},{80,64},{96,80},{112,96},{128,112},... | collective-permute-start | bytes 24584 | tf_op jit(solution)/shard_map/ppermute | solution.py:361
  45.3 5.0 %collective-permute-start.3 = (f32[2,8,128]{2,1,0:T(8,128)}, f32[2,8,128]{2,1,0:T(8,128)S(1)}, u32[]{:S(2)}, u32[]{:S(2)}) collective-permute-start(f32[2,8,128]{2,1,0:T(8,128)} %own_gradient.1.own), channel_id=1, source_target_pairs={{0,16},{16,32},{32,48},{48,64},{64,80},{80,96},{96,112},{112,128},... | collective-permute-start | bytes 24584 | tf_op jit(solution)/shard_map/ppermute | solution.py:361
  49.3 1.0 copy-start.6
  50.3 0.6 copy-start.7

commit v2 on v1

--- a/solution.py
+++ b/solution.py
@@ -7,6 +7,7 @@
 from jax.experimental import pallas as pl
 from jax.experimental.pallas import tpu as pltpu
 from jax.sharding import PartitionSpec as P
+
 
 FR = 3
 KS_SHARP = 2.0
@@ -20,6 +21,7 @@
 COARSE = (LEVEL_HIGH - LEVEL_LOW) / FAN
 FINE = COARSE / FAN
 SUB, LANE = 8, 128
+GRANT = 8 * 1024 * 1024
 F32 = jnp.float32
 VMEM = pl.BlockSpec(memory_space=pltpu.VMEM)
 SMEM = pl.BlockSpec(memory_space=pltpu.SMEM)
@@ -149,7 +151,22 @@
         out[r, 4] = weight
 
 
-def second_layer(modes, plane, eigen, out, pairs):
+def shifted_rows(v, o):
+    rows = iota(v.shape, 0)
+    moved = pltpu.roll(v, (-o) % SUB, 0)
+    return jnp.where((rows + o >= 0) & (rows + o < SUB), moved, 0.0)
+
+
+def edge_rows(first, second):
+    zero = jnp.zeros((4, LANE), F32)
+    up, down = [], []
+    for f in (first, second):
+        up += [2.0 * f[7:8] + f[6:7], f[7:8]]
+        down += [f[0:1], 2.0 * f[0:1] + f[1:2]]
+    return jnp.concatenate([*up, zero], 0), jnp.concatenate([zero, *down], 0)
+
+
+def second_layer(modes, plane, eigen, design, before, after, out, rows, pairs, *, mode):
     def store(r, stiff, mass):
         out[r, 0] = stiff
         out[r, 1] = mass
@@ -157,28 +174,17 @@
     def load(c, a):
         return plane[0, c] if a else modes[0, c, 1]
 
-    forms(load, eigen[0], store, pairs, out.shape[0])
-
-
-def own_sums(got, sums, rows_out, padded, *, mode):
-    tiles = got.shape[0]
     m = lax.axis_index(mode)
-    for k, at in enumerate((0, 1, 4)):
-        total = got[0, at]
-        for r in range(1, tiles):
-            total = total + got[r, at]
-        sums[k] = total
+    tiles = out.shape[0]
+    pair = across_x(design, before, after)
+    up, down = edge_rows(*pair)
     for l in (0, 1):
-        padded[l, :SUB] = jnp.zeros((SUB, LANE), F32)
-        padded[l, (tiles + 1) * SUB :] = jnp.zeros((SUB, LANE), F32)
-        for r in range(tiles):
-            padded[l, (r + 1) * SUB : (r + 2) * SUB] = got[r, 2 + l]
-    for l in (0, 1):
-        total = None
-        for o in range(1 - FR, FR):
-            t = float(FR - abs(o)) * padded[l, pl.ds(m * SUB + SUB + o, SUB)]
-            total = t if total is None else total + t
-        rows_out[l] = tent_lanes(total)
+        rows[l] = pair[l]
+    for r in range(tiles):
+        to_next = jnp.where(m + 1 == r, F32(1.0), F32(0.0))
+        to_last = jnp.where(m - 1 == r, F32(1.0), F32(0.0))
+        out[r, 2] = up * to_next + down * to_last
+    forms(load, eigen[0], store, pairs, tiles)
 
 
 def across_x(own, before, after):
@@ -187,27 +193,34 @@
     return first, second
 
 
-def own_gradient(got, sums, rows, before, after, out, *, slab, mode, sizes):
+def over_modes(got, at):
+    total = got[0, at]
+    for r in range(1, got.shape[0]):
+        total = total + got[r, at]
+    return total
+
+
+def own_gradient(early, late, rows, out, *, slab, mode, sizes):
     total_x, total_y, total_z = sizes
-    tiles = got.shape[0]
     s, m = lax.axis_index(slab), lax.axis_index(mode)
-    later = []
-    for at in (0, 1):
-        total = got[0, at]
-        for r in range(1, tiles):
-            total = total + got[r, at]
-        later.append(total)
-    stiff = (sums[0], later[0])
-    mass = (sums[1], later[1])
+    stiff = (over_modes(early, 0), over_modes(late, 0))
+    mass = (over_modes(early, 1), over_modes(late, 1))
+    inverse_weight = 1.0 / over_modes(early, 4)
+    edges = over_modes(late, 2)
     inverse_yz = along(m * SUB + iota((SUB, LANE), 0), total_y, edge_tables(total_y)[0]) * along(
         iota((SUB, LANE), 1), total_z, edge_tables(total_z)[0]
     )
-    filtered = across_x(rows, before, after)
-    inverse_weight = 1.0 / sums[2]
     for l in (0, 1):
+        own = rows[l]
+        near = jnp.concatenate(
+            [edges[2 * l : 2 * l + 2], jnp.zeros((4, LANE), F32), edges[4 + 2 * l : 6 + 2 * l]], 0
+        )
+        filtered = near
+        for o in range(1 - FR, FR):
+            filtered = filtered + float(FR - abs(o)) * (shifted_rows(own, o) if o else own)
         x = jnp.full((SUB, LANE), 2 * s + l, jnp.int32)
         inverse = inverse_yz * along(x, total_x, edge_tables(total_x)[0])
-        density = filtered[l] * inverse
+        density = tent_lanes(filtered) * inverse
         slope = (PENALTY * (1.0 - FLOOR_MODULUS)) * density * density
         out[l] = tent_lanes((slope * stiff[l] - mass[l]) * inverse_weight * inverse)
 
@@ -339,7 +352,7 @@
         sens_out[l] = s
 
 
-def call(kernel, outs, operands, specs=None, scratch=(), flops=1000, name=None):
+def call(kernel, outs, operands, specs=None, scratch=(), flops=1000):
     outs = [jax.ShapeDtypeStruct(o, F32) for o in outs]
     size = sum(4 * int(np.prod(o.shape)) for o in (*outs, *operands))
     single = len(outs) == 1
@@ -350,7 +363,7 @@
         out_specs=VMEM if single else [VMEM] * len(outs),
         scratch_shapes=[pltpu.VMEM(s, F32) for s in scratch],
         cost_estimate=pl.CostEstimate(flops=flops, bytes_accessed=size, transcendentals=0),
-        name=name,
+        compiler_params=pltpu.CompilerParams(vmem_limit_bytes=GRANT),
     )(*operands)
 
 
@@ -358,7 +371,9 @@
     count = lax.axis_size(axis)
     up = [(i, i + 1) for i in range(count - 1)]
     down = [(j, i) for i, j in up]
-    return lax.ppermute(value, axis, up), lax.ppermute(value, axis, down)
+    before = lax.ppermute(value, axis, up)
+    after = lax.ppermute(value, axis, down)
+    return before, after
 
 
 def exchange(value, axis):
@@ -377,6 +392,7 @@
 
     down = [(i + 1, i) for i in range(slabs - 1)]
     plane = lax.ppermute(mode_shapes[:, :, 0], slab, down)
+    before, after = neighbours(design, slab)
     early = call(
         first_layer,
         [(modes, 5, SUB, LANE)],
@@ -384,35 +400,20 @@
         specs=[VMEM, SMEM, VMEM],
         scratch=[pairs],
         flops=5_000_000,
-        name="first_layer",
     )
     early = exchange(early, mode)
-    late = call(
-        second_layer,
-        [(modes, 2, SUB, LANE)],
-        [mode_shapes, plane, eigenvalues],
-        specs=[VMEM, VMEM, SMEM],
+    late, rows = call(
+        functools.partial(second_layer, mode=mode),
+        [(modes, 3, SUB, LANE), block],
+        [mode_shapes, plane, eigenvalues, design, before, after],
+        specs=[VMEM, VMEM, SMEM, VMEM, VMEM, VMEM],
         scratch=[pairs],
         flops=5_000_000,
-        name="second_layer",
     )
     late = exchange(late, mode)
-    sums, rows = call(
-        functools.partial(own_sums, mode=mode),
-        [(3, SUB, LANE), block],
-        [early],
-        scratch=[padded],
-        name="own_sums",
-    )
-    before, after = neighbours(rows, slab)
-    gradient = call(
-        functools.partial(own_gradient, **place),
-        [block],
-        [late, sums, rows, before, after],
-        name="own_gradient",
-    )
+    gradient = call(functools.partial(own_gradient, **place), [block], [early, late, rows])
     before, after = neighbours(gradient, slab)
-    copies = call(gradient_copies, [(modes, *block)], [gradient, before, after], name="copies")
+    copies = call(gradient_copies, [(modes, *block)], [gradient, before, after])
     whole = exchange(copies, mode)
     vectors = 2 * modes
     gain, least, most, own, sent = call(
@@ -420,7 +421,6 @@
         [(vectors, SUB, LANE)] * 3 + [block, (slabs, 1, LANE)],
         [whole, early],
         scratch=[padded, (FAN, LANE)],
-        name="first_round",
     )
     got = exchange(sent, slab)
     sent, state = call(
@@ -428,15 +428,9 @@
         [(slabs, 1, LANE), (SUB, LANE)],
         [got, gain, least, most],
         scratch=[(FAN, LANE)],
-        name="second_round",
     )
     got = exchange(sent, slab)
-    return call(
-        functools.partial(last_update, **place),
-        [block, block],
-        [got, state, own, design],
-        name="last_update",
-    )
+    return call(functools.partial(last_update, **place), [block, block], [got, state, own, design])
 
 
 def solution(mesh):

time: 119 us -> 110 us (0.924)
  Pallas kernels: 17.4 us -> 6.09 us
  blocking collectives: 57.9 us -> 65.2 us
  starting transfers between devices: 27.9 us -> 24.4 us
    pallas_call x8 -> x7, Pallas kernels: 17.4 us -> 6.09 us  [call(): pl.pallas_call(kernel, out_shape=outs[0] if single else outs, in_specs=sp...]
    all_to_all x3 -> x4, blocking collectives: 57.9 us -> 65.2 us  [exchange(): return lax.all_to_all(value, axis, 0, 0, tiled=True)]
    ppermute x1, waiting for transfers between devices: 6.83 us -> 0.01 us  [local(): plane = lax.ppermute(mode_shapes[:, :, 0], slab, down)]
    all_to_all x2 -> x1, starting transfers between devices: 16.1 us -> 9.96 us  [exchange(): return lax.all_to_all(value, axis, 0, 0, tiled=True)]
    all_to_all x2 -> x1, waiting for transfers between devices: 4.14 us -> 9.72 us  [exchange(): return lax.all_to_all(value, axis, 0, 0, tiled=True)]
    ppermute x4, starting transfers between devices: 10.5 us -> 13.2 us  [the longest x2 10.6 us: neighbours(): before = lax.ppermute(value, axis, up)]
    unnamed x16 -> x6, local copies, waits for them, and re-layouts: 1.91 us -> 0.71 us
  transfers between devices with their start and end apart: 7 -> 6, of which waited for: 4 -> 3; matrix products, arithmetic and copies ran while one was open for 0% -> 0% of each run, Pallas kernels for 3% -> 0%
where the time goes in v2:
time: 110 us
  blocking collectives  65.2 us (59%)
  starting transfers between devices  24.4 us (22%)
  waiting for transfers between devices  10.8 us (10%)
  Pallas kernels  6.09 us (6%)
  local copies, waits for them, and re-layouts  1.71 us (2%)
  between operations  1.37 us (1%)
    all_to_all x4, blocking collectives, exchange(): return lax.all_to_all(value, axis, 0, 0, tiled=True)  65.2 us
    ppermute x2, starting transfers between devices, neighbours(): before = lax.ppermute(value, axis, up)  10.6 us
    all_to_all x1, starting transfers between devices, exchange(): return lax.all_to_all(value, axis, 0, 0, tiled=True)  9.96 us
    all_to_all x1, waiting for transfers between devices, exchange(): return lax.all_to_all(value, axis, 0, 0, tiled=True)  9.72 us
    pallas_call x7, Pallas kernels, call(): pl.pallas_call(kernel, out_shape=outs[0] if single else outs, in_specs=sp...  6.09 us
    ppermute x2, starting transfers between devices, neighbours(): after = lax.ppermute(value, axis, down)  2.58 us
  transfers between devices with their start and end apart: 6, of which 3 were waited for; matrix products, arithmetic and copies ran while one was open for 0% of the time, Pallas kernels for 0%

profile of v2, /device:TPU:1, one launch (start us, length us, event | category | flops | bytes accessed | tf_op | source)
XLA Modules:
  0.0 109.7 jit_solution(7104935266976047985)
XLA Ops:
  0.6 0.0 copy-start
  0.6 1.0 slice_bitcast_fusion
  1.6 1.3 %collective-permute-start = (f32[1,3,128,128]{3,2,1,0:T(8,128)S(1)}, f32[1,3,128,128]{3,2,1,0:T(8,128)S(1)}, u32[]{:S(2)}, u32[]{:S(2)}) collective-permute-start(f32[1,3,128,128]{3,2,1,0:T(8,128)S(1)} %slice_bitcast_fusion), channel_id=1, source_target_pairs={{16,0},{32,16},{48,32},{64,48},{80,64},{96,80},{112,96},{128,112},... | collective-permute-start | bytes 589832 | tf_op jit(solution)/shard_map/ppermute | solution.py:394
  2.9 1.3 %collective-permute-start.2 = (f32[2,8,128]{2,1,0:T(8,128)}, f32[2,8,128]{2,1,0:T(8,128)S(1)}, u32[]{:S(2)}, u32[]{:S(2)}) collective-permute-start(f32[2,8,128]{2,1,0:T(8,128)} %design.5), channel_id=1, source_target_pairs={{16,0},{32,16},{48,32},{64,48},{80,64},{96,80},{112,96},{128,112},... | collective-permute-start | bytes 24584 | tf_op jit(solution)/shard_map/ppermute | solution.py:375
  4.2 6.1 %collective-permute-start.1 = (f32[2,8,128]{2,1,0:T(8,128)}, f32[2,8,128]{2,1,0:T(8,128)S(1)}, u32[]{:S(2)}, u32[]{:S(2)}) collective-permute-start(f32[2,8,128]{2,1,0:T(8,128)} %design.5), channel_id=1, source_target_pairs={{0,16},{16,32},{32,48},{48,64},{64,80},{80,96},{96,112},{112,128},... | collective-permute-start | bytes 24584 | tf_op jit(solution)/shard_map/ppermute | solution.py:374
  11.0 0.0 collective-permute-done.2.after
  11.0 0.3 collective-permute-done.1.before
  11.3 0.0 collective-permute-done.plane
  11.3 0.0 copy-done
  11.3 0.0 copy-start.1
  11.3 0.7 copy-done.1
  12.0 1.2 %shard_map.51 = (f32[16,3,8,128]{3,2,1,0:T(8,128)}, f32[2,8,128]{2,1,0:T(8,128)S(1)}) custom-call(f32[1,3,2,128,128]{4,3,2,1,0:T(8,128)S(1)} %copy-done, f32[1,3,128,128]{3,2,1,0:T(8,128)S(1)} %collective-permute-done.plane, f32[1]{0:T(128)S(6)} %copy.7.eigen, f32[2,8,128]{2,1,0:T(8,128)S(1)} %copy-done.1, f32[2,8,128]{2,1,0:T(8,128)S(1)} %collective-permute-done.1.before, ...), custom_call_target="tpu_custom_call" | custom-call | flops 5000000 | bytes 819204 | tf_op jit(solution)/shard_map/pallas_call | solution.py:359
  13.2 0.0 copy-start.2
  13.2 10.0 %all-to-all-start.1 = ((f32[16,3,8,128]{3,2,1,0:T(8,128)}), f32[16,3,8,128]{3,2,1,0:T(8,128)S(1)}, u32[]{:S(2)}, u32[]{:S(2)}) async-start(f32[16,3,8,128]{3,2,1,0:T(8,128)} %get-tuple-element.11), calls=%async_computation.1 | async-start | bytes 393216 | tf_op jit(solution)/shard_map/all_to_all | solution.py:380
  23.2 0.0 copy-done.2
  23.2 0.5 shard_map.50
  23.7 9.7 %all-to-all-done.1.late = f32[16,3,8,128]{3,2,1,0:T(8,128)S(1)} async-done(((f32[16,3,8,128]{3,2,1,0:T(8,128)}), f32[16,3,8,128]{3,2,1,0:T(8,128)S(1)}, u32[]{:S(2)}, u32[]{:S(2)}) %all-to-all-start.1) | async-done | bytes 196640 | tf_op jit(solution)/shard_map/all_to_all | solution.py:380
  33.5 15.7 %all_to_all.25.early = f32[16,5,8,128]{3,2,1,0:T(8,128)S(1)} all-to-all(f32[16,5,8,128]{3,2,1,0:T(8,128)S(1)} %shard_map.50), channel_id=1, replica_groups=mesh['slab'=32,'mode'=16] {'mode'}, dimensions={0} | all-to-all | bytes 655360 | tf_op jit(solution)/shard_map/all_to_all | solution.py:380
  49.1 0.2 shard_map.52.own
  49.3 1.3 %collective-permute-start.4 = (f32[2,8,128]{2,1,0:T(8,128)S(1)}, f32[2,8,128]{2,1,0:T(8,128)S(1)}, u32[]{:S(2)}, u32[]{:S(2)}) collective-permute-start(f32[2,8,128]{2,1,0:T(8,128)S(1)} %shard_map.52.own), channel_id=1, source_target_pairs={{16,0},{32,16},{48,32},{64,48},{80,64},{96,80},{112,96},{128,112},... | collective-permute-start | bytes 24584 | tf_op jit(solution)/shard_map/ppermute | solution.py:375
  50.6 4.5 %collective-permute-start.3 = (f32[2,8,128]{2,1,0:T(8,128)S(1)}, f32[2,8,128]{2,1,0:T(8,128)S(1)}, u32[]{:S(2)}, u32[]{:S(2)}) collective-permute-start(f32[2,8,128]{2,1,0:T(8,128)S(1)} %shard_map.52.own), channel_id=1, source_target_pairs={{0,16},{16,32},{32,48},{48,64},{64,80},{80,96},{96,112},{112,128},... | collective-permute-start | bytes 24584 | tf_op jit(solution)/shard_map/ppermute | solution.py:374
  55.2 0.0 collective-permute-done.4.after
  55.2 0.8 collective-permute-done.3.before
  56.0 12.5 %all_to_all.26.got = f32[16,2,8,128]{3,2,1,0:T(8,128)S(1)} all-to-all(f32[16,2,8,128]{3,2,1,0:T(8,128)S(1)} %shard_map.53), channel_id=1, replica_groups=mesh['slab'=32,'mode'=16] {'mode'}, dimensions={0} | all-to-all | bytes 262144 | tf_op jit(solution)/shard_map/all_to_all | solution.py:380
  68.5 1.6 %shard_map.54 = (f32[32,8,128]{2,1,0:T(8,128)S(1)}, f32[32,8,128]{2,1,0:T(8,128)S(1)}, f32[32,8,128]{2,1,0:T(8,128)S(1)}, f32[2,8,128]{2,1,0:T(8,128)S(1)}, f32[32,1,128]{2,1,0:T(1,128)S(1)}) custom-call(f32[16,2,8,128]{3,2,1,0:T(8,128)S(1)} %all_to_all.26.got, f32[16,5,8,128]{3,2,1,0:T(8,128)S(1)} %all_to_all.25.early), custom_call_target="tpu_custom_call" | custom-call | flops 1000 | bytes 876544 | tf_op jit(solution)/shard_map/pallas_call | solution.py:359
  70.1 25.4 %all_to_all.27.got = f32[32,1,128]{2,1,0:T(1,128)S(1)} all-to-all(f32[32,1,128]{2,1,0:T(1,128)S(1)} %get-tuple-element.13), channel_id=1, replica_groups=mesh['slab'=32,'mode'=16] {'slab'}, dimensions={0} | all-to-all | bytes 32768 | tf_op jit(solution)/shard_map/all_to_all | solution.py:380
  95.5 1.7 %shard_map.55 = (f32[32,1,128]{2,1,0:T(1,128)S(1)}, f32[8,128]{1,0:T(8,128)S(1)}) custom-call(f32[32,1,128]{2,1,0:T(1,128)S(1)} %all_to_all.27.got, f32[32,8,128]{2,1,0:T(8,128)S(1)} %get-tuple-element.14.gain, f32[32,8,128]{2,1,0:T(8,128)S(1)} %get-tuple-element.15.least, f32[32,8,128]{2,1,0:T(8,128)S(1)} %get-tuple-element.16.most), custom_call_target="tpu_custom_call" | custom-call | flops 1000 | bytes 430080 | tf_op jit(solution)/shard_map/pallas_call | solution.py:359
  97.2 11.7 %all_to_all.28.got = f32[32,1,128]{2,1,0:T(1,128)S(1)} all-to-all(f32[32,1,128]{2,1,0:T(1,128)S(1)} %get-tuple-element.17), channel_id=1, replica_groups=mesh['slab'=32,'mode'=16] {'slab'}, dimensions={0} | all-to-all | bytes 32768 | tf_op jit(solution)/shard_map/all_to_all | solution.py:380
  108.9 0.8 shard_map.56
  (1 shorter events, 0.0 us)
Async XLA Ops:
  0.6 10.7 %copy-start = (f32[1,3,2,128,128]{4,3,2,1,0:T(8,128)S(1)}, f32[1,3,2,128,128]{4,3,2,1,0:T(8,128)}, u32[]{:S(2)}) copy-start(f32[1,3,2,128,128]{4,3,2,1,0:T(8,128)} %modes.3) | copy-start | bytes 1179652
  1.6 9.7 %collective-permute-start = (f32[1,3,128,128]{3,2,1,0:T(8,128)S(1)}, f32[1,3,128,128]{3,2,1,0:T(8,128)S(1)}, u32[]{:S(2)}, u32[]{:S(2)}) collective-permute-start(f32[1,3,128,128]{3,2,1,0:T(8,128)S(1)} %slice_bitcast_fusion), channel_id=1, source_target_pairs={{16,0},{32,16},{48,32},{64,48},{80,64},{96,80},{112,96},{128,112},... | collective-permute-start | bytes 589832 | tf_op jit(solution)/shard_map/ppermute | solution.py:394
  2.9 8.0 %collective-permute-start.2 = (f32[2,8,128]{2,1,0:T(8,128)}, f32[2,8,128]{2,1,0:T(8,128)S(1)}, u32[]{:S(2)}, u32[]{:S(2)}) collective-permute-start(f32[2,8,128]{2,1,0:T(8,128)} %design.5), channel_id=1, source_target_pairs={{16,0},{32,16},{48,32},{64,48},{80,64},{96,80},{112,96},{128,112},... | collective-permute-start | bytes 24584 | tf_op jit(solution)/shard_map/ppermute | solution.py:375
  4.2 7.1 %collective-permute-start.1 = (f32[2,8,128]{2,1,0:T(8,128)}, f32[2,8,128]{2,1,0:T(8,128)S(1)}, u32[]{:S(2)}, u32[]{:S(2)}) collective-permute-start(f32[2,8,128]{2,1,0:T(8,128)} %design.5), channel_id=1, source_target_pairs={{0,16},{16,32},{32,48},{48,64},{64,80},{80,96},{96,112},{112,128},... | collective-permute-start | bytes 24584 | tf_op jit(solution)/shard_map/ppermute | solution.py:374
  11.3 0.7 copy-start.1
  13.2 10.0 %copy-start.2 = (f32[2,8,128]{2,1,0:T(8,128)S(1)}, f32[2,8,128]{2,1,0:T(8,128)}, u32[]{:S(2)}) copy-start(f32[2,8,128]{2,1,0:T(8,128)} %design.5) | copy-start | bytes 24580
  13.2 20.2 %all-to-all-start.1 = ((f32[16,3,8,128]{3,2,1,0:T(8,128)}), f32[16,3,8,128]{3,2,1,0:T(8,128)S(1)}, u32[]{:S(2)}, u32[]{:S(2)}) async-start(f32[16,3,8,128]{3,2,1,0:T(8,128)} %get-tuple-element.11), calls=%async_computation.1 | async-start | bytes 393216 | tf_op jit(solution)/shard_map/all_to_all | solution.py:380
  49.3 5.8 %collective-permute-start.4 = (f32[2,8,128]{2,1,0:T(8,128)S(1)}, f32[2,8,128]{2,1,0:T(8,128)S(1)}, u32[]{:S(2)}, u32[]{:S(2)}) collective-permute-start(f32[2,8,128]{2,1,0:T(8,128)S(1)} %shard_map.52.own), channel_id=1, source_target_pairs={{16,0},{32,16},{48,32},{64,48},{80,64},{96,80},{112,96},{128,112},... | collective-permute-start | bytes 24584 | tf_op jit(solution)/shard_map/ppermute | solution.py:375
  50.6 5.3 %collective-permute-start.3 = (f32[2,8,128]{2,1,0:T(8,128)S(1)}, f32[2,8,128]{2,1,0:T(8,128)S(1)}, u32[]{:S(2)}, u32[]{:S(2)}) collective-permute-start(f32[2,8,128]{2,1,0:T(8,128)S(1)} %shard_map.52.own), channel_id=1, source_target_pairs={{0,16},{16,32},{32,48},{48,64},{64,80},{80,96},{96,112},{112,128},... | collective-permute-start | bytes 24584 | tf_op jit(solution)/shard_map/ppermute | solution.py:374

commit v3 on v2

--- a/solution.py
+++ b/solution.py
@@ -146,9 +146,9 @@
     tiles = out.shape[0]
     weight = forms(lambda c, a: modes[0, c, a], eigen[0], store, pairs, tiles)
     for r in range(tiles):
-        out[r, 2] = design[0]
-        out[r, 3] = design[1]
-        out[r, 4] = weight
+        out[r, 4] = design[0]
+        out[r, 5] = design[1]
+        out[r, 6] = weight
 
 
 def shifted_rows(v, o):
@@ -166,30 +166,34 @@
     return jnp.concatenate([*up, zero], 0), jnp.concatenate([zero, *down], 0)
 
 
-def second_layer(modes, plane, eigen, design, before, after, out, rows, pairs, *, mode):
+def second_layer(modes, plane, eigen, design, even, odd, _, out, rows, pairs, *, slab, mode):
     def store(r, stiff, mass):
-        out[r, 0] = stiff
-        out[r, 1] = mass
+        out[r, 2] = stiff
+        out[r, 3] = mass
 
     def load(c, a):
         return plane[0, c] if a else modes[0, c, 1]
 
     m = lax.axis_index(mode)
     tiles = out.shape[0]
-    pair = across_x(design, before, after)
+    pair = across_x(design, even, odd, slab)
     up, down = edge_rows(*pair)
     for l in (0, 1):
         rows[l] = pair[l]
     for r in range(tiles):
         to_next = jnp.where(m + 1 == r, F32(1.0), F32(0.0))
         to_last = jnp.where(m - 1 == r, F32(1.0), F32(0.0))
-        out[r, 2] = up * to_next + down * to_last
+        out[r, 7] = up * to_next + down * to_last
     forms(load, eigen[0], store, pairs, tiles)
 
 
-def across_x(own, before, after):
-    first = before[0] + 2.0 * before[1] + 3.0 * own[0] + 2.0 * own[1] + after[0]
-    second = before[1] + 2.0 * own[0] + 3.0 * own[1] + 2.0 * after[0] + after[1]
+def across_x(own, even, odd, slab):
+    is_even = lax.rem(lax.axis_index(slab), 2) == 0
+    own_0, own_1, even_0, even_1, odd_0, odd_1 = own[0], own[1], even[0], even[1], odd[0], odd[1]
+    before_0, before_1 = jnp.where(is_even, odd_0, even_0), jnp.where(is_even, odd_1, even_1)
+    after_0, after_1 = jnp.where(is_even, even_0, odd_0), jnp.where(is_even, even_1, odd_1)
+    first = before_0 + 2.0 * before_1 + 3.0 * own_0 + 2.0 * own_1 + after_0
+    second = before_1 + 2.0 * own_0 + 3.0 * own_1 + 2.0 * after_0 + after_1
     return first, second
 
 
@@ -200,13 +204,13 @@
     return total
 
 
-def own_gradient(early, late, rows, out, *, slab, mode, sizes):
+def own_gradient(got, rows, out, *, slab, mode, sizes):
     total_x, total_y, total_z = sizes
     s, m = lax.axis_index(slab), lax.axis_index(mode)
-    stiff = (over_modes(early, 0), over_modes(late, 0))
-    mass = (over_modes(early, 1), over_modes(late, 1))
-    inverse_weight = 1.0 / over_modes(early, 4)
-    edges = over_modes(late, 2)
+    stiff = (over_modes(got, 0), over_modes(got, 2))
+    mass = (over_modes(got, 1), over_modes(got, 3))
+    inverse_weight = 1.0 / over_modes(got, 6)
+    edges = over_modes(got, 7)
     inverse_yz = along(m * SUB + iota((SUB, LANE), 0), total_y, edge_tables(total_y)[0]) * along(
         iota((SUB, LANE), 1), total_z, edge_tables(total_z)[0]
     )
@@ -225,8 +229,8 @@
         out[l] = tent_lanes((slope * stiff[l] - mass[l]) * inverse_weight * inverse)
 
 
-def gradient_copies(own, before, after, out):
-    pair = across_x(own, before, after)
+def gradient_copies(own, even, odd, out, *, slab):
+    pair = across_x(own, even, odd, slab)
     for r in range(out.shape[0]):
         out[r, 0] = pair[0]
         out[r, 1] = pair[1]
@@ -284,7 +288,7 @@
                 t = float(FR - abs(o)) * padded[l, start : start + SUB]
                 total = t if total is None else total + t
             measure = xz[l] * along(r * SUB + iota((SUB, LANE), 0), total_y, edge_tables(total_y)[1])
-            design = early[r, 2 + l]
+            design = early[r, 4 + l]
             at = l * tiles + r
             gain[at] = design * jnp.sqrt(jnp.maximum(total, 0.0) * measure)
             least[at] = jnp.maximum(design - MOVE_LIMIT, 0.0) * measure
@@ -352,7 +356,7 @@
         sens_out[l] = s
 
 
-def call(kernel, outs, operands, specs=None, scratch=(), flops=1000):
+def call(kernel, outs, operands, specs=None, scratch=(), flops=1000, alias=None):
     outs = [jax.ShapeDtypeStruct(o, F32) for o in outs]
     size = sum(4 * int(np.prod(o.shape)) for o in (*outs, *operands))
     single = len(outs) == 1
@@ -363,17 +367,16 @@
         out_specs=VMEM if single else [VMEM] * len(outs),
         scratch_shapes=[pltpu.VMEM(s, F32) for s in scratch],
         cost_estimate=pl.CostEstimate(flops=flops, bytes_accessed=size, transcendentals=0),
+        input_output_aliases=alias or {},
         compiler_params=pltpu.CompilerParams(vmem_limit_bytes=GRANT),
     )(*operands)
 
 
 def neighbours(value, axis):
     count = lax.axis_size(axis)
-    up = [(i, i + 1) for i in range(count - 1)]
-    down = [(j, i) for i, j in up]
-    before = lax.ppermute(value, axis, up)
-    after = lax.ppermute(value, axis, down)
-    return before, after
+    even = lax.ppermute(value, axis, [(i, i ^ 1) for i in range(count)])
+    odd = lax.ppermute(value, axis, [(i, ((i + 1) ^ 1) - 1) for i in range(1, count - 1)])
+    return even, odd
 
 
 def exchange(value, axis):
@@ -392,28 +395,30 @@
 
     down = [(i + 1, i) for i in range(slabs - 1)]
     plane = lax.ppermute(mode_shapes[:, :, 0], slab, down)
-    before, after = neighbours(design, slab)
-    early = call(
+    even, odd = neighbours(design, slab)
+    sent = call(
         first_layer,
-        [(modes, 5, SUB, LANE)],
+        [(modes, 8, SUB, LANE)],
         [mode_shapes, eigenvalues, design],
         specs=[VMEM, SMEM, VMEM],
         scratch=[pairs],
         flops=5_000_000,
     )
-    early = exchange(early, mode)
-    late, rows = call(
-        functools.partial(second_layer, mode=mode),
-        [(modes, 3, SUB, LANE), block],
-        [mode_shapes, plane, eigenvalues, design, before, after],
-        specs=[VMEM, VMEM, SMEM, VMEM, VMEM, VMEM],
+    sent, rows = call(
+        functools.partial(second_layer, slab=slab, mode=mode),
+        [(modes, 8, SUB, LANE), block],
+        [mode_shapes, plane, eigenvalues, design, even, odd, sent],
+        specs=[VMEM, VMEM, SMEM, VMEM, VMEM, VMEM, VMEM],
         scratch=[pairs],
         flops=5_000_000,
-    )
-    late = exchange(late, mode)
-    gradient = call(functools.partial(own_gradient, **place), [block], [early, late, rows])
-    before, after = neighbours(gradient, slab)
-    copies = call(gradient_copies, [(modes, *block)], [gradient, before, after])
+        alias={6: 0},
+    )
+    early = exchange(sent, mode)
+    gradient = call(functools.partial(own_gradient, **place), [block], [early, rows])
+    even, odd = neighbours(gradient, slab)
+    copies = call(
+        functools.partial(gradient_copies, slab=slab), [(modes, *block)], [gradient, even, odd]
+    )
     whole = exchange(copies, mode)
     vectors = 2 * modes
     gain, least, most, own, sent = call(

time: 110 us -> 99.5 us (0.905)
  waiting for transfers between devices: 10.8 us -> 1.03 us
  starting transfers between devices: 24.4 us -> 19.9 us
  blocking collectives: 65.2 us -> 69.5 us
    all_to_all x1 -> x0, starting transfers between devices: 9.96 us -> none  [exchange(): return lax.all_to_all(value, axis, 0, 0, tiled=True)]
    all_to_all x1 -> x0, waiting for transfers between devices: 9.72 us -> none  [exchange(): return lax.all_to_all(value, axis, 0, 0, tiled=True)]
    ppermute x4, starting transfers between devices: 13.2 us -> 18.7 us  [the longest x2 17.3 us: neighbours(): even = lax.ppermute(value, axis, [(i, i ^ 1) for i in range(count)])]
    all_to_all x4, blocking collectives: 65.2 us -> 69.5 us  [exchange(): return lax.all_to_all(value, axis, 0, 0, tiled=True)]
  transfers between devices with their start and end apart: 6 -> 5, of which waited for: 3 -> 1; matrix products, arithmetic and copies ran while one was open for 0% -> 0% of each run, Pallas kernels for 0% -> 1%
where the time goes in v3:
time: 99.5 us; the launch traced here: 99 us
  blocking collectives  69.5 us (70%)
  starting transfers between devices  19.9 us (20%)
  Pallas kernels  5.41 us (5%)
  local copies, waits for them, and re-layouts  1.71 us (2%)
  between operations  1.4 us (1%)
  waiting for transfers between devices  1.03 us (1%)
    all_to_all x4, blocking collectives, exchange(): return lax.all_to_all(value, axis, 0, 0, tiled=True)  69.5 us
    ppermute x2, starting transfers between devices, neighbours(): even = lax.ppermute(value, axis, [(i, i ^ 1) for i in range(count)])  17.3 us
    pallas_call x7, Pallas kernels, call(): pl.pallas_call(kernel, out_shape=outs[0] if single else outs, in_specs=sp...  5.41 us
  transfers between devices with their start and end apart: 5, of which 1 were waited for; matrix products, arithmetic and copies ran while one was open for 0% of the time, Pallas kernels for 1%

profile of v3, /device:TPU:1, one launch (start us, length us, event | category | flops | bytes accessed | tf_op | source)
XLA Modules:
  0.0 99.0 jit_solution(14600903282565692254)
XLA Ops:
  0.6 0.0 copy-start
  0.6 1.0 %slice_bitcast_fusion = f32[1,3,128,128]{3,2,1,0:T(8,128)S(1)} fusion(f32[1,3,2,128,128]{4,3,2,1,0:T(8,128)} %modes.3), kind=kLoop, calls=%fused_computation | loop fusion | bytes 393216 | tf_op jit(solution)/shard_map/squeeze | solution.py:397
  1.6 1.3 %collective-permute-start = (f32[1,3,128,128]{3,2,1,0:T(8,128)S(1)}, f32[1,3,128,128]{3,2,1,0:T(8,128)S(1)}, u32[]{:S(2)}, u32[]{:S(2)}) collective-permute-start(f32[1,3,128,128]{3,2,1,0:T(8,128)S(1)} %slice_bitcast_fusion), channel_id=1, source_target_pairs={{16,0},{32,16},{48,32},{64,48},{80,64},{96,80},{112,96},{128,112},... | collective-permute-start | bytes 589832 | tf_op jit(solution)/shard_map/ppermute | solution.py:397
  2.9 0.7 collective-permute-start.2
  3.6 8.8 %collective-permute-start.1 = (f32[2,8,128]{2,1,0:T(8,128)}, f32[2,8,128]{2,1,0:T(8,128)S(1)}, u32[]{:S(2)}, u32[]{:S(2)}) collective-permute-start(f32[2,8,128]{2,1,0:T(8,128)} %design.5), channel_id=1, source_target_pairs={{0,16},{16,0},{32,48},{48,32},{64,80},{80,64},{96,112},{112,96},{1... | collective-permute-start | bytes 24584 | tf_op jit(solution)/shard_map/ppermute | solution.py:377
  13.1 0.0 copy-done
  13.1 0.0 copy-start.1
  13.1 0.7 copy-done.1
  13.8 0.5 shard_map.50._
  14.3 0.0 collective-permute-done.2.odd
  14.3 0.0 collective-permute-done.1.even
  14.3 0.0 collective-permute-done.plane
  14.4 0.5 shard_map.51
  14.9 25.3 %all_to_all.20.got.early = f32[16,8,8,128]{3,2,1,0:T(8,128)S(1)} all-to-all(f32[16,8,8,128]{3,2,1,0:T(8,128)S(1)} %get-tuple-element.11), channel_id=1, replica_groups=mesh['slab'=32,'mode'=16] {'mode'}, dimensions={0} | all-to-all | bytes 1048576 | tf_op jit(solution)/shard_map/all_to_all | solution.py:383
  40.2 0.2 shard_map.52.own
  40.4 0.7 collective-permute-start.4
  41.1 8.6 %collective-permute-start.3 = (f32[2,8,128]{2,1,0:T(8,128)S(1)}, f32[2,8,128]{2,1,0:T(8,128)S(1)}, u32[]{:S(2)}, u32[]{:S(2)}) collective-permute-start(f32[2,8,128]{2,1,0:T(8,128)S(1)} %shard_map.52.own), channel_id=1, source_target_pairs={{0,16},{16,0},{32,48},{48,32},{64,80},{80,64},{96,112},{112,96},{1... | collective-permute-start | bytes 24584 | tf_op jit(solution)/shard_map/ppermute | solution.py:377
  49.6 0.0 collective-permute-done.4.odd
  49.6 1.0 %collective-permute-done.3.even = f32[2,8,128]{2,1,0:T(8,128)S(1)} collective-permute-done((f32[2,8,128]{2,1,0:T(8,128)S(1)}, f32[2,8,128]{2,1,0:T(8,128)S(1)}, u32[]{:S(2)}, u32[]{:S(2)}) %collective-permute-start.3) | collective-permute-done | bytes 8224 | tf_op jit(solution)/shard_map/ppermute | solution.py:377
  50.7 12.8 %all_to_all.21.got = f32[16,2,8,128]{3,2,1,0:T(8,128)S(1)} all-to-all(f32[16,2,8,128]{3,2,1,0:T(8,128)S(1)} %shard_map.53), channel_id=1, replica_groups=mesh['slab'=32,'mode'=16] {'mode'}, dimensions={0} | all-to-all | bytes 262144 | tf_op jit(solution)/shard_map/all_to_all | solution.py:383
  63.5 1.6 %shard_map.54 = (f32[32,8,128]{2,1,0:T(8,128)S(1)}, f32[32,8,128]{2,1,0:T(8,128)S(1)}, f32[32,8,128]{2,1,0:T(8,128)S(1)}, f32[2,8,128]{2,1,0:T(8,128)S(1)}, f32[32,1,128]{2,1,0:T(1,128)S(1)}) custom-call(f32[16,2,8,128]{3,2,1,0:T(8,128)S(1)} %all_to_all.21.got, f32[16,8,8,128]{3,2,1,0:T(8,128)S(1)} %all_to_all.20.got.early), custom_call_target="tpu_custom_call" | custom-call | flops 1000 | bytes 1073152 | tf_op jit(solution)/shard_map/pallas_call | solution.py:363
  65.1 19.7 %all_to_all.22.got = f32[32,1,128]{2,1,0:T(1,128)S(1)} all-to-all(f32[32,1,128]{2,1,0:T(1,128)S(1)} %get-tuple-element.13), channel_id=1, replica_groups=mesh['slab'=32,'mode'=16] {'slab'}, dimensions={0} | all-to-all | bytes 32768 | tf_op jit(solution)/shard_map/all_to_all | solution.py:383
  84.8 0.0 copy-start.2
  84.8 1.7 %shard_map.55 = (f32[32,1,128]{2,1,0:T(1,128)S(1)}, f32[8,128]{1,0:T(8,128)S(1)}) custom-call(f32[32,1,128]{2,1,0:T(1,128)S(1)} %all_to_all.22.got, f32[32,8,128]{2,1,0:T(8,128)S(1)} %get-tuple-element.14.gain, f32[32,8,128]{2,1,0:T(8,128)S(1)} %get-tuple-element.15.least, f32[32,8,128]{2,1,0:T(8,128)S(1)} %get-tuple-element.16.most), custom_call_target="tpu_custom_call" | custom-call | flops 1000 | bytes 430080 | tf_op jit(solution)/shard_map/pallas_call | solution.py:363
  86.6 11.7 %all_to_all.23.got = f32[32,1,128]{2,1,0:T(1,128)S(1)} all-to-all(f32[32,1,128]{2,1,0:T(1,128)S(1)} %get-tuple-element.17), channel_id=1, replica_groups=mesh['slab'=32,'mode'=16] {'slab'}, dimensions={0} | all-to-all | bytes 32768 | tf_op jit(solution)/shard_map/all_to_all | solution.py:383
  98.2 0.0 copy-done.2
  98.2 0.8 shard_map.56
  (1 shorter events, 0.0 us)
Async XLA Ops:
  0.6 12.4 %copy-start = (f32[1,3,2,128,128]{4,3,2,1,0:T(8,128)S(1)}, f32[1,3,2,128,128]{4,3,2,1,0:T(8,128)}, u32[]{:S(2)}) copy-start(f32[1,3,2,128,128]{4,3,2,1,0:T(8,128)} %modes.3) | copy-start | bytes 1179652
  1.6 12.7 %collective-permute-start = (f32[1,3,128,128]{3,2,1,0:T(8,128)S(1)}, f32[1,3,128,128]{3,2,1,0:T(8,128)S(1)}, u32[]{:S(2)}, u32[]{:S(2)}) collective-permute-start(f32[1,3,128,128]{3,2,1,0:T(8,128)S(1)} %slice_bitcast_fusion), channel_id=1, source_target_pairs={{16,0},{32,16},{48,32},{64,48},{80,64},{96,80},{112,96},{128,112},... | collective-permute-start | bytes 589832 | tf_op jit(solution)/shard_map/ppermute | solution.py:397
  2.9 11.4 %collective-permute-start.2 = (f32[2,8,128]{2,1,0:T(8,128)}, f32[2,8,128]{2,1,0:T(8,128)S(1)}, u32[]{:S(2)}, u32[]{:S(2)}) collective-permute-start(f32[2,8,128]{2,1,0:T(8,128)} %design.5), channel_id=1, source_target_pairs={{16,32},{32,16},{48,64},{64,48},{80,96},{96,80},{112,128},{128,112... | collective-permute-start | bytes 24584 | tf_op jit(solution)/shard_map/ppermute | solution.py:378
  3.6 10.7 %collective-permute-start.1 = (f32[2,8,128]{2,1,0:T(8,128)}, f32[2,8,128]{2,1,0:T(8,128)S(1)}, u32[]{:S(2)}, u32[]{:S(2)}) collective-permute-start(f32[2,8,128]{2,1,0:T(8,128)} %design.5), channel_id=1, source_target_pairs={{0,16},{16,0},{32,48},{48,32},{64,80},{80,64},{96,112},{112,96},{1... | collective-permute-start | bytes 24584 | tf_op jit(solution)/shard_map/ppermute | solution.py:377
  13.1 0.7 copy-start.1
  40.4 9.2 %collective-permute-start.4 = (f32[2,8,128]{2,1,0:T(8,128)S(1)}, f32[2,8,128]{2,1,0:T(8,128)S(1)}, u32[]{:S(2)}, u32[]{:S(2)}) collective-permute-start(f32[2,8,128]{2,1,0:T(8,128)S(1)} %shard_map.52.own), channel_id=1, source_target_pairs={{16,32},{32,16},{48,64},{64,48},{80,96},{96,80},{112,128},{128,112... | collective-permute-start | bytes 24584 | tf_op jit(solution)/shard_map/ppermute | solution.py:378
  41.1 9.6 %collective-permute-start.3 = (f32[2,8,128]{2,1,0:T(8,128)S(1)}, f32[2,8,128]{2,1,0:T(8,128)S(1)}, u32[]{:S(2)}, u32[]{:S(2)}) collective-permute-start(f32[2,8,128]{2,1,0:T(8,128)S(1)} %shard_map.52.own), channel_id=1, source_target_pairs={{0,16},{16,0},{32,48},{48,32},{64,80},{80,64},{96,112},{112,96},{1... | collective-permute-start | bytes 24584 | tf_op jit(solution)/shard_map/ppermute | solution.py:377
  84.8 13.4 %copy-start.2 = (f32[2,8,128]{2,1,0:T(8,128)S(1)}, f32[2,8,128]{2,1,0:T(8,128)}, u32[]{:S(2)}) copy-start(f32[2,8,128]{2,1,0:T(8,128)} %design.5) | copy-start | bytes 24580

commit v4 on v3

--- a/solution.py
+++ b/solution.py
@@ -138,17 +138,22 @@
     return weight
 
 
-def first_layer(modes, eigen, design, out, pairs):
+def tail_rows(packed, k):
+    start = packed.shape[0] - (2 - k) * SUB
+    return packed[start : start + SUB]
+
+
+def first_layer(modes, eigen, packed, out, pairs):
     def store(r, stiff, mass):
         out[r, 0] = stiff
         out[r, 1] = mass
 
     tiles = out.shape[0]
-    weight = forms(lambda c, a: modes[0, c, a], eigen[0], store, pairs, tiles)
+    forms(lambda c, a: modes[0, c, a], eigen[0], store, pairs, tiles)
+    design = tail_rows(packed, 0), tail_rows(packed, 1)
     for r in range(tiles):
         out[r, 4] = design[0]
         out[r, 5] = design[1]
-        out[r, 6] = weight
 
 
 def shifted_rows(v, o):
@@ -158,42 +163,41 @@
 
 
 def edge_rows(first, second):
-    zero = jnp.zeros((4, LANE), F32)
     up, down = [], []
     for f in (first, second):
         up += [2.0 * f[7:8] + f[6:7], f[7:8]]
         down += [f[0:1], 2.0 * f[0:1] + f[1:2]]
-    return jnp.concatenate([*up, zero], 0), jnp.concatenate([zero, *down], 0)
-
-
-def second_layer(modes, plane, eigen, design, even, odd, _, out, rows, pairs, *, slab, mode):
+    return jnp.concatenate(up, 0), jnp.concatenate(down, 0)
+
+
+def second_layer(modes, eigen, packed, got, before, _, out, rows, pairs, *, mode):
     def store(r, stiff, mass):
         out[r, 2] = stiff
         out[r, 3] = mass
 
+    tiles = out.shape[0]
+    span = tiles * SUB
+
     def load(c, a):
-        return plane[0, c] if a else modes[0, c, 1]
+        return got[c * span : (c + 1) * span] if a else modes[0, c, 1]
 
     m = lax.axis_index(mode)
-    tiles = out.shape[0]
-    pair = across_x(design, even, odd, slab)
+    own = tail_rows(packed, 0), tail_rows(packed, 1)
+    after = tail_rows(got, 0), tail_rows(got, 1)
+    pair = across_x(own, before, after)
     up, down = edge_rows(*pair)
     for l in (0, 1):
         rows[l] = pair[l]
+    weight = forms(load, eigen[0], store, pairs, tiles)
+    half = SUB // 2
     for r in range(tiles):
-        to_next = jnp.where(m + 1 == r, F32(1.0), F32(0.0))
-        to_last = jnp.where(m - 1 == r, F32(1.0), F32(0.0))
-        out[r, 7] = up * to_next + down * to_last
-    forms(load, eigen[0], store, pairs, tiles)
-
-
-def across_x(own, even, odd, slab):
-    is_even = lax.rem(lax.axis_index(slab), 2) == 0
-    own_0, own_1, even_0, even_1, odd_0, odd_1 = own[0], own[1], even[0], even[1], odd[0], odd[1]
-    before_0, before_1 = jnp.where(is_even, odd_0, even_0), jnp.where(is_even, odd_1, even_1)
-    after_0, after_1 = jnp.where(is_even, even_0, odd_0), jnp.where(is_even, even_1, odd_1)
-    first = before_0 + 2.0 * before_1 + 3.0 * own_0 + 2.0 * own_1 + after_0
-    second = before_1 + 2.0 * own_0 + 3.0 * own_1 + 2.0 * after_0 + after_1
+        out[r, 6, :half] = jnp.where(m + 1 == r, up, weight[:half])
+        out[r, 6, half:] = jnp.where(m - 1 == r, down, weight[half:])
+
+
+def across_x(own, before, after):
+    first = before[0] + 2.0 * before[1] + 3.0 * own[0] + 2.0 * own[1] + after[0]
+    second = before[1] + 2.0 * own[0] + 3.0 * own[1] + 2.0 * after[0] + after[1]
     return first, second
 
 
@@ -209,15 +213,22 @@
     s, m = lax.axis_index(slab), lax.axis_index(mode)
     stiff = (over_modes(got, 0), over_modes(got, 2))
     mass = (over_modes(got, 1), over_modes(got, 3))
-    inverse_weight = 1.0 / over_modes(got, 6)
-    edges = over_modes(got, 7)
+    tiles = got.shape[0]
+    half = SUB // 2
+    weight = None
+    for r in range(tiles):
+        w = jnp.where(m - 1 == r, got[r, 6, half : half + 1], got[r, 6, :1])
+        weight = w if weight is None else weight + w
+    inverse_weight = 1.0 / jnp.broadcast_to(weight, (SUB, LANE))
+    from_last = jnp.where(m > 0, got[jnp.maximum(m - 1, 0), 6, :half], 0.0)
+    from_next = jnp.where(m < tiles - 1, got[jnp.minimum(m + 1, tiles - 1), 6, half:], 0.0)
     inverse_yz = along(m * SUB + iota((SUB, LANE), 0), total_y, edge_tables(total_y)[0]) * along(
         iota((SUB, LANE), 1), total_z, edge_tables(total_z)[0]
     )
     for l in (0, 1):
         own = rows[l]
         near = jnp.concatenate(
-            [edges[2 * l : 2 * l + 2], jnp.zeros((4, LANE), F32), edges[4 + 2 * l : 6 + 2 * l]], 0
+            [from_last[2 * l : 2 * l + 2], jnp.zeros((4, LANE), F32), from_next[2 * l : 2 * l + 2]], 0
         )
         filtered = near
         for o in range(1 - FR, FR):
@@ -229,8 +240,8 @@
         out[l] = tent_lanes((slope * stiff[l] - mass[l]) * inverse_weight * inverse)
 
 
-def gradient_copies(own, even, odd, out, *, slab):
-    pair = across_x(own, even, odd, slab)
+def gradient_copies(own, before, after, out):
+    pair = across_x(own, before, after)
     for r in range(out.shape[0]):
         out[r, 0] = pair[0]
         out[r, 1] = pair[1]
@@ -372,11 +383,14 @@
     )(*operands)
 
 
-def neighbours(value, axis):
+def from_before(value, axis):
     count = lax.axis_size(axis)
-    even = lax.ppermute(value, axis, [(i, i ^ 1) for i in range(count)])
-    odd = lax.ppermute(value, axis, [(i, ((i + 1) ^ 1) - 1) for i in range(1, count - 1)])
-    return even, odd
+    return lax.ppermute(value, axis, [(i, i + 1) for i in range(count - 1)])
+
+
+def from_after(value, axis):
+    count = lax.axis_size(axis)
+    return lax.ppermute(value, axis, [(i + 1, i) for i in range(count - 1)])
 
 
 def exchange(value, axis):
@@ -393,32 +407,31 @@
     padded = (2, total_y + 2 * SUB, LANE)
     place = dict(slab=slab, mode=mode, sizes=sizes)
 
-    down = [(i + 1, i) for i in range(slabs - 1)]
-    plane = lax.ppermute(mode_shapes[:, :, 0], slab, down)
-    even, odd = neighbours(design, slab)
+    packed = jnp.concatenate([mode_shapes[0, :, 0].reshape(-1, LANE), design.reshape(-1, LANE)], 0)
+    got = from_after(packed, slab)
+    before = from_before(design, slab)
     sent = call(
         first_layer,
-        [(modes, 8, SUB, LANE)],
-        [mode_shapes, eigenvalues, design],
+        [(modes, 7, SUB, LANE)],
+        [mode_shapes, eigenvalues, packed],
         specs=[VMEM, SMEM, VMEM],
         scratch=[pairs],
         flops=5_000_000,
     )
     sent, rows = call(
-        functools.partial(second_layer, slab=slab, mode=mode),
-        [(modes, 8, SUB, LANE), block],
-        [mode_shapes, plane, eigenvalues, design, even, odd, sent],
-        specs=[VMEM, VMEM, SMEM, VMEM, VMEM, VMEM, VMEM],
+        functools.partial(second_layer, mode=mode),
+        [(modes, 7, SUB, LANE), block],
+        [mode_shapes, eigenvalues, packed, got, before, sent],
+        specs=[VMEM, SMEM, VMEM, VMEM, VMEM, VMEM],
         scratch=[pairs],
         flops=5_000_000,
-        alias={6: 0},
+        alias={5: 0},
     )
     early = exchange(sent, mode)
     gradient = call(functools.partial(own_gradient, **place), [block], [early, rows])
-    even, odd = neighbours(gradient, slab)
-    copies = call(
-        functools.partial(gradient_copies, slab=slab), [(modes, *block)], [gradient, even, odd]
-    )
+    after = from_after(gradient, slab)
+    before = from_before(gradient, slab)
+    copies = call(gradient_copies, [(modes, *block)], [gradient, before, after])
     whole = exchange(copies, mode)
     vectors = 2 * modes
     gain, least, most, own, sent = call(

time: 99.5 us -> 97.6 us (0.981)
  starting transfers between devices: 19.9 us -> 12.6 us
  blocking collectives: 69.5 us -> 75.1 us
    ppermute x5 -> x4, starting transfers between devices: 19.9 us -> 12.6 us  [the longest x2 10.1 us: from_before(): return lax.ppermute(value, axis, [(i, i + 1) for i in range(count - 1)])]
    all_to_all x4, blocking collectives: 69.5 us -> 75.1 us  [exchange(): return lax.all_to_all(value, axis, 0, 0, tiled=True)]
    squeeze x1 -> x0, local copies, waits for them, and re-layouts: 1.01 us -> none  [local(): plane = lax.ppermute(mode_shapes[:, :, 0], slab, down)]
  transfers between devices with their start and end apart: 5 -> 4, of which waited for: 1 -> 1; matrix products, arithmetic and copies ran while one was open for 0% -> 0% of each run, Pallas kernels for 1% -> 1%
where the time goes in v4:
time: 97.6 us; the launch traced here: 97.1 us
  blocking collectives  75.1 us (77%)
  starting transfers between devices  12.6 us (13%)
  Pallas kernels  5.44 us (6%)
  between operations  1.39 us (1%)
    all_to_all x4, blocking collectives, exchange(): return lax.all_to_all(value, axis, 0, 0, tiled=True)  75.1 us
    ppermute x2, starting transfers between devices, from_before(): return lax.ppermute(value, axis, [(i, i + 1) for i in range(count - 1)])  10.1 us
    pallas_call x7, Pallas kernels, call(): pl.pallas_call(kernel, out_shape=outs[0] if single else outs, in_specs=sp...  5.44 us
    ppermute x2, starting transfers between devices, from_after(): return lax.ppermute(value, axis, [(i + 1, i) for i in range(count - 1)])  2.58 us
  transfers between devices with their start and end apart: 4, of which 1 were waited for; matrix products, arithmetic and copies ran while one was open for 0% of the time, Pallas kernels for 1%

profile of v4, /device:TPU:1, one launch (start us, length us, event | category | flops | bytes accessed | tf_op | source)
XLA Modules:
  0.0 97.1 jit_solution(15905500889076149033)
XLA Ops:
  0.6 0.0 slice-start
  0.6 0.0 copy-start
  0.6 0.9 slice-done
  1.6 0.0 copy-start.1
  1.6 0.8 pad_maximum_fusion.packed
  2.3 1.3 %collective-permute-start = (f32[400,128]{1,0:T(8,128)S(1)}, f32[400,128]{1,0:T(8,128)S(1)}, u32[]{:S(2)}, u32[]{:S(2)}) collective-permute-start(f32[400,128]{1,0:T(8,128)S(1)} %pad_maximum_fusion.packed), channel_id=1, source_target_pairs={{16,0},{32,16},{48,32},{64,48},{80,64},{96,80},{112,96},{128,112},... | collective-permute-start | bytes 614408 | tf_op jit(solution)/shard_map/ppermute | solution.py:393
  3.6 0.0 copy-done.1
  3.7 5.4 %collective-permute-start.1 = (f32[2,8,128]{2,1,0:T(8,128)S(1)}, f32[2,8,128]{2,1,0:T(8,128)S(1)}, u32[]{:S(2)}, u32[]{:S(2)}) collective-permute-start(f32[2,8,128]{2,1,0:T(8,128)S(1)} %copy-done.1), channel_id=1, source_target_pairs={{0,16},{16,32},{32,48},{48,64},{64,80},{80,96},{96,112},{112,128},... | collective-permute-start | bytes 24584 | tf_op jit(solution)/shard_map/ppermute | solution.py:388
  9.8 0.0 copy-done
  9.8 0.5 shard_map.50._
  10.3 0.0 collective-permute-done.1.before
  10.3 0.0 collective-permute-done.got
  10.3 0.6 shard_map.51
  10.9 25.6 %all_to_all.20.got.early = f32[16,7,8,128]{3,2,1,0:T(8,128)S(1)} all-to-all(f32[16,7,8,128]{3,2,1,0:T(8,128)S(1)} %get-tuple-element.11), channel_id=1, replica_groups=mesh['slab'=32,'mode'=16] {'mode'}, dimensions={0} | all-to-all | bytes 917504 | tf_op jit(solution)/shard_map/all_to_all | solution.py:397
  36.5 0.2 shard_map.52.own
  36.7 1.3 %collective-permute-start.3 = (f32[2,8,128]{2,1,0:T(8,128)S(1)}, f32[2,8,128]{2,1,0:T(8,128)S(1)}, u32[]{:S(2)}, u32[]{:S(2)}) collective-permute-start(f32[2,8,128]{2,1,0:T(8,128)S(1)} %shard_map.52.own), channel_id=1, source_target_pairs={{16,0},{32,16},{48,32},{64,48},{80,64},{96,80},{112,96},{128,112},... | collective-permute-start | bytes 24584 | tf_op jit(solution)/shard_map/ppermute | solution.py:393
  38.0 4.6 %collective-permute-start.2 = (f32[2,8,128]{2,1,0:T(8,128)S(1)}, f32[2,8,128]{2,1,0:T(8,128)S(1)}, u32[]{:S(2)}, u32[]{:S(2)}) collective-permute-start(f32[2,8,128]{2,1,0:T(8,128)S(1)} %shard_map.52.own), channel_id=1, source_target_pairs={{0,16},{16,32},{32,48},{48,64},{64,80},{80,96},{96,112},{112,128},... | collective-permute-start | bytes 24584 | tf_op jit(solution)/shard_map/ppermute | solution.py:388
  42.6 0.0 collective-permute-done.3.after
  42.6 0.8 collective-permute-done.2.before
  43.4 12.5 %all_to_all.21.got = f32[16,2,8,128]{3,2,1,0:T(8,128)S(1)} all-to-all(f32[16,2,8,128]{3,2,1,0:T(8,128)S(1)} %shard_map.53), channel_id=1, replica_groups=mesh['slab'=32,'mode'=16] {'mode'}, dimensions={0} | all-to-all | bytes 262144 | tf_op jit(solution)/shard_map/all_to_all | solution.py:397
  55.9 1.6 %shard_map.54 = (f32[32,8,128]{2,1,0:T(8,128)S(1)}, f32[32,8,128]{2,1,0:T(8,128)S(1)}, f32[32,8,128]{2,1,0:T(8,128)S(1)}, f32[2,8,128]{2,1,0:T(8,128)S(1)}, f32[32,1,128]{2,1,0:T(1,128)S(1)}) custom-call(f32[16,2,8,128]{3,2,1,0:T(8,128)S(1)} %all_to_all.21.got, f32[16,7,8,128]{3,2,1,0:T(8,128)S(1)} %all_to_all.20.got.early), custom_call_target="tpu_custom_call" | custom-call | flops 1000 | bytes 1007616 | tf_op jit(solution)/shard_map/pallas_call | solution.py:374
  57.5 25.4 %all_to_all.22.got = f32[32,1,128]{2,1,0:T(1,128)S(1)} all-to-all(f32[32,1,128]{2,1,0:T(1,128)S(1)} %get-tuple-element.13), channel_id=1, replica_groups=mesh['slab'=32,'mode'=16] {'slab'}, dimensions={0} | all-to-all | bytes 32768 | tf_op jit(solution)/shard_map/all_to_all | solution.py:397
  82.9 1.8 %shard_map.55 = (f32[32,1,128]{2,1,0:T(1,128)S(1)}, f32[8,128]{1,0:T(8,128)S(1)}) custom-call(f32[32,1,128]{2,1,0:T(1,128)S(1)} %all_to_all.22.got, f32[32,8,128]{2,1,0:T(8,128)S(1)} %get-tuple-element.14.gain, f32[32,8,128]{2,1,0:T(8,128)S(1)} %get-tuple-element.15.least, f32[32,8,128]{2,1,0:T(8,128)S(1)} %get-tuple-element.16.most), custom_call_target="tpu_custom_call" | custom-call | flops 1000 | bytes 430080 | tf_op jit(solution)/shard_map/pallas_call | solution.py:374
  84.6 11.7 %all_to_all.23.got = f32[32,1,128]{2,1,0:T(1,128)S(1)} all-to-all(f32[32,1,128]{2,1,0:T(1,128)S(1)} %get-tuple-element.17), channel_id=1, replica_groups=mesh['slab'=32,'mode'=16] {'slab'}, dimensions={0} | all-to-all | bytes 32768 | tf_op jit(solution)/shard_map/all_to_all | solution.py:397
  96.3 0.8 shard_map.56
  (1 shorter events, 0.0 us)
Async XLA Ops:
  0.6 0.9 slice-start
  0.6 9.1 %copy-start = (f32[1,3,2,128,128]{4,3,2,1,0:T(8,128)S(1)}, f32[1,3,2,128,128]{4,3,2,1,0:T(8,128)}, u32[]{:S(2)}) copy-start(f32[1,3,2,128,128]{4,3,2,1,0:T(8,128)} %modes.3) | copy-start | bytes 1179652
  1.6 2.1 %copy-start.1 = (f32[2,8,128]{2,1,0:T(8,128)S(1)}, f32[2,8,128]{2,1,0:T(8,128)}, u32[]{:S(2)}) copy-start(f32[2,8,128]{2,1,0:T(8,128)} %design.1) | copy-start | bytes 24580
  2.3 8.0 %collective-permute-start = (f32[400,128]{1,0:T(8,128)S(1)}, f32[400,128]{1,0:T(8,128)S(1)}, u32[]{:S(2)}, u32[]{:S(2)}) collective-permute-start(f32[400,128]{1,0:T(8,128)S(1)} %pad_maximum_fusion.packed), channel_id=1, source_target_pairs={{16,0},{32,16},{48,32},{64,48},{80,64},{96,80},{112,96},{128,112},... | collective-permute-start | bytes 614408 | tf_op jit(solution)/shard_map/ppermute | solution.py:393
  3.7 6.7 %collective-permute-start.1 = (f32[2,8,128]{2,1,0:T(8,128)S(1)}, f32[2,8,128]{2,1,0:T(8,128)S(1)}, u32[]{:S(2)}, u32[]{:S(2)}) collective-permute-start(f32[2,8,128]{2,1,0:T(8,128)S(1)} %copy-done.1), channel_id=1, source_target_pairs={{0,16},{16,32},{32,48},{48,64},{64,80},{80,96},{96,112},{112,128},... | collective-permute-start | bytes 24584 | tf_op jit(solution)/shard_map/ppermute | solution.py:388
  36.7 5.9 %collective-permute-start.3 = (f32[2,8,128]{2,1,0:T(8,128)S(1)}, f32[2,8,128]{2,1,0:T(8,128)S(1)}, u32[]{:S(2)}, u32[]{:S(2)}) collective-permute-start(f32[2,8,128]{2,1,0:T(8,128)S(1)} %shard_map.52.own), channel_id=1, source_target_pairs={{16,0},{32,16},{48,32},{64,48},{80,64},{96,80},{112,96},{128,112},... | collective-permute-start | bytes 24584 | tf_op jit(solution)/shard_map/ppermute | solution.py:393
  38.0 5.4 %collective-permute-start.2 = (f32[2,8,128]{2,1,0:T(8,128)S(1)}, f32[2,8,128]{2,1,0:T(8,128)S(1)}, u32[]{:S(2)}, u32[]{:S(2)}) collective-permute-start(f32[2,8,128]{2,1,0:T(8,128)S(1)} %shard_map.52.own), channel_id=1, source_target_pairs={{0,16},{16,32},{32,48},{48,64},{64,80},{80,96},{96,112},{112,128},... | collective-permute-start | bytes 24584 | tf_op jit(solution)/shard_map/ppermute | solution.py:388

commit v5 on v4

--- a/solution.py
+++ b/solution.py
@@ -268,7 +268,7 @@
             )
 
         zeros = tuple(jnp.zeros((SUB, LANE), F32) for _ in chunk)
-        totals = lax.fori_loop(0, count, body, zeros, unroll=4)
+        totals = lax.fori_loop(0, count, body, zeros, unroll=16)
         for i, t in enumerate(totals):
             parts[start + i : start + i + 1] = jnp.sum(t, axis=0, keepdims=True)
 
@@ -280,8 +280,25 @@
     return jnp.sum(spread, axis=0, keepdims=True)
 
 
-def first_round(got, early, gain, least, most, own, out, padded, parts, *, slab, mode, sizes):
+def bounds(early, least, most, goals, measures, *, slab, sizes):
     total_x, total_y, total_z = sizes
+    tiles = early.shape[0]
+    xz = measure_xz(slab, total_x, total_z)
+    goal = jnp.zeros((SUB, LANE), F32)
+    for r in range(tiles):
+        y = along(r * SUB + iota((SUB, LANE), 0), total_y, edge_tables(total_y)[1])
+        for l in (0, 1):
+            measure = xz[l] * y
+            design = early[r, 4 + l]
+            at = l * tiles + r
+            least[at] = jnp.maximum(design - MOVE_LIMIT, 0.0) * measure
+            most[at] = jnp.minimum(design + MOVE_LIMIT, 1.0) * measure
+            measures[at] = measure
+            goal = goal + design * measure
+    goals[0:1] = jnp.sum(goal, axis=0, keepdims=True)
+
+
+def first_round(got, early, least, most, goals, measures, gain, own, out, padded, parts, *, mode):
     tiles = got.shape[0]
     m = lax.axis_index(mode)
     for l in (0, 1):
@@ -289,8 +306,6 @@
         padded[l, (tiles + 1) * SUB :] = jnp.zeros((SUB, LANE), F32)
         for r in range(tiles):
             padded[l, (r + 1) * SUB : (r + 2) * SUB] = got[r, l]
-    xz = measure_xz(slab, total_x, total_z)
-    goal = jnp.zeros((SUB, LANE), F32)
     for l in (0, 1):
         for r in range(tiles):
             total = None
@@ -298,13 +313,8 @@
                 start = (r + 1) * SUB + o
                 t = float(FR - abs(o)) * padded[l, start : start + SUB]
                 total = t if total is None else total + t
-            measure = xz[l] * along(r * SUB + iota((SUB, LANE), 0), total_y, edge_tables(total_y)[1])
-            design = early[r, 4 + l]
             at = l * tiles + r
-            gain[at] = design * jnp.sqrt(jnp.maximum(total, 0.0) * measure)
-            least[at] = jnp.maximum(design - MOVE_LIMIT, 0.0) * measure
-            most[at] = jnp.minimum(design + MOVE_LIMIT, 1.0) * measure
-            goal = goal + design * measure
+            gain[at] = early[r, 4 + l] * jnp.sqrt(jnp.maximum(total, 0.0) * measures[at])
         total = None
         for o in range(1 - FR, FR):
             t = float(FR - abs(o)) * padded[l, pl.ds(m * SUB + SUB + o, SUB)]
@@ -312,7 +322,7 @@
         own[l] = total
     levels = [float(np.exp(-0.5 * (LEVEL_LOW + COARSE * (i + 1)))) for i in range(FAN - 1)]
     volumes(levels, gain, least, most, parts)
-    parts[FAN - 1 : FAN] = jnp.sum(goal, axis=0, keepdims=True)
+    parts[FAN - 1 : FAN] = goals[0:1]
     row = lane_totals(parts)
     for k in range(out.shape[0]):
         out[k] = row
@@ -433,11 +443,17 @@
     before = from_before(gradient, slab)
     copies = call(gradient_copies, [(modes, *block)], [gradient, before, after])
     whole = exchange(copies, mode)
-    vectors = 2 * modes
-    gain, least, most, own, sent = call(
-        functools.partial(first_round, **place),
-        [(vectors, SUB, LANE)] * 3 + [block, (slabs, 1, LANE)],
-        [whole, early],
+    vectors = (2 * modes, SUB, LANE)
+    least, most, goals, measures = call(
+        functools.partial(bounds, slab=slab, sizes=sizes),
+        [vectors, vectors, (SUB, LANE), vectors],
+        [early],
+        flops=100_000,
+    )
+    gain, own, sent = call(
+        functools.partial(first_round, mode=mode),
+        [vectors, block, (slabs, 1, LANE)],
+        [whole, early, least, most, goals, measures],
         scratch=[padded, (FAN, LANE)],
     )
     got = exchange(sent, slab)

time: 97.6 us -> 98.1 us (level)
  blocking collectives: 75.1 us -> 62.7 us
  waiting for transfers between devices: 0.77 us -> 9.6 us
  starting transfers between devices: 12.6 us -> 16.4 us
    all_to_all x4 -> x3, blocking collectives: 75.1 us -> 62.7 us  [exchange(): return lax.all_to_all(value, axis, 0, 0, tiled=True)]
    all_to_all x0 -> x1, waiting for transfers between devices: none -> 8.83 us  [exchange(): return lax.all_to_all(value, axis, 0, 0, tiled=True)]
    all_to_all x0 -> x1, starting transfers between devices: none -> 3.78 us  [exchange(): return lax.all_to_all(value, axis, 0, 0, tiled=True)]
    pallas_call x7 -> x8, Pallas kernels: 5.44 us -> 5.78 us  [call(): pl.pallas_call(kernel, out_shape=outs[0] if single else outs, in_specs=sp...]
  transfers between devices with their start and end apart: 4 -> 5, of which waited for: 1 -> 2; matrix products, arithmetic and copies ran while one was open for 0% -> 0% of each run, Pallas kernels for 1% -> 1%
where the time goes in v5:
time: 98.1 us; the launch traced here: 97.6 us
  blocking collectives  62.7 us (64%)
  starting transfers between devices  16.4 us (17%)
  waiting for transfers between devices  9.6 us (10%)
  Pallas kernels  5.78 us (6%)
  between operations  1.39 us (1%)
    all_to_all x3, blocking collectives, exchange(): return lax.all_to_all(value, axis, 0, 0, tiled=True)  62.7 us
    ppermute x2, starting transfers between devices, from_before(): return lax.ppermute(value, axis, [(i, i + 1) for i in range(count - 1)])  10.1 us
    all_to_all x1, waiting for transfers between devices, exchange(): return lax.all_to_all(value, axis, 0, 0, tiled=True)  8.83 us
    pallas_call x8, Pallas kernels, call(): pl.pallas_call(kernel, out_shape=outs[0] if single else outs, in_specs=sp...  5.78 us
    all_to_all x1, starting transfers between devices, exchange(): return lax.all_to_all(value, axis, 0, 0, tiled=True)  3.78 us
    ppermute x2, starting transfers between devices, from_after(): return lax.ppermute(value, axis, [(i + 1, i) for i in range(count - 1)])  2.58 us
  transfers between devices with their start and end apart: 5, of which 2 were waited for; matrix products, arithmetic and copies ran while one was open for 0% of the time, Pallas kernels for 1%

profile of v5, /device:TPU:1, one launch (start us, length us, event | category | flops | bytes accessed | tf_op | source)
XLA Modules:
  0.0 97.6 jit_solution(6675960078542701480)
XLA Ops:
  0.6 0.0 slice-start
  0.6 0.0 copy-start
  0.6 0.9 slice-done
  1.6 0.0 copy-start.1
  1.6 0.8 pad_maximum_fusion.packed
  2.3 1.3 %collective-permute-start = (f32[400,128]{1,0:T(8,128)S(1)}, f32[400,128]{1,0:T(8,128)S(1)}, u32[]{:S(2)}, u32[]{:S(2)}) collective-permute-start(f32[400,128]{1,0:T(8,128)S(1)} %pad_maximum_fusion.packed), channel_id=1, source_target_pairs={{16,0},{32,16},{48,32},{64,48},{80,64},{96,80},{112,96},{128,112},... | collective-permute-start | bytes 614408 | tf_op jit(solution)/shard_map/ppermute | solution.py:403
  3.6 0.0 copy-done.1
  3.7 5.4 %collective-permute-start.1 = (f32[2,8,128]{2,1,0:T(8,128)S(1)}, f32[2,8,128]{2,1,0:T(8,128)S(1)}, u32[]{:S(2)}, u32[]{:S(2)}) collective-permute-start(f32[2,8,128]{2,1,0:T(8,128)S(1)} %copy-done.1), channel_id=1, source_target_pairs={{0,16},{16,32},{32,48},{48,64},{64,80},{80,96},{96,112},{112,128},... | collective-permute-start | bytes 24584 | tf_op jit(solution)/shard_map/ppermute | solution.py:398
  9.8 0.0 copy-done
  9.8 0.5 shard_map.50._
  10.3 0.0 collective-permute-done.1.before
  10.3 0.0 collective-permute-done.got
  10.3 0.6 shard_map.51
  10.9 25.6 %all_to_all.20.got.early = f32[16,7,8,128]{3,2,1,0:T(8,128)S(1)} all-to-all(f32[16,7,8,128]{3,2,1,0:T(8,128)S(1)} %get-tuple-element.13), channel_id=1, replica_groups=mesh['slab'=32,'mode'=16] {'mode'}, dimensions={0} | all-to-all | bytes 917504 | tf_op jit(solution)/shard_map/all_to_all | solution.py:407
  36.5 0.2 shard_map.52.own
  36.7 1.3 %collective-permute-start.3 = (f32[2,8,128]{2,1,0:T(8,128)S(1)}, f32[2,8,128]{2,1,0:T(8,128)S(1)}, u32[]{:S(2)}, u32[]{:S(2)}) collective-permute-start(f32[2,8,128]{2,1,0:T(8,128)S(1)} %shard_map.52.own), channel_id=1, source_target_pairs={{16,0},{32,16},{48,32},{64,48},{80,64},{96,80},{112,96},{128,112},... | collective-permute-start | bytes 24584 | tf_op jit(solution)/shard_map/ppermute | solution.py:403
  38.0 4.6 %collective-permute-start.2 = (f32[2,8,128]{2,1,0:T(8,128)S(1)}, f32[2,8,128]{2,1,0:T(8,128)S(1)}, u32[]{:S(2)}, u32[]{:S(2)}) collective-permute-start(f32[2,8,128]{2,1,0:T(8,128)S(1)} %shard_map.52.own), channel_id=1, source_target_pairs={{0,16},{16,32},{32,48},{48,64},{64,80},{80,96},{96,112},{112,128},... | collective-permute-start | bytes 24584 | tf_op jit(solution)/shard_map/ppermute | solution.py:398
  42.6 0.0 collective-permute-done.3.after
  42.6 0.8 collective-permute-done.2.before
  43.4 0.7 shard_map.53
  44.1 3.8 %all-to-all-start.1 = ((f32[16,2,8,128]{3,2,1,0:T(8,128)}), f32[16,2,8,128]{3,2,1,0:T(8,128)S(1)}, u32[]{:S(2)}, u32[]{:S(2)}) async-start(f32[16,2,8,128]{3,2,1,0:T(8,128)} %shard_map.53), calls=%async_computation.1 | async-start | bytes 262144 | tf_op jit(solution)/shard_map/all_to_all | solution.py:407
  47.8 0.1 shard_map.54
  47.9 8.8 %all-to-all-done.1.got = f32[16,2,8,128]{3,2,1,0:T(8,128)S(1)} async-done(((f32[16,2,8,128]{3,2,1,0:T(8,128)}), f32[16,2,8,128]{3,2,1,0:T(8,128)S(1)}, u32[]{:S(2)}, u32[]{:S(2)}) %all-to-all-start.1) | async-done | bytes 131104 | tf_op jit(solution)/shard_map/all_to_all | solution.py:407
  56.7 1.4 %shard_map.55 = (f32[32,8,128]{2,1,0:T(8,128)S(1)}, f32[2,8,128]{2,1,0:T(8,128)S(1)}, f32[32,1,128]{2,1,0:T(1,128)S(1)}) custom-call(f32[16,2,8,128]{3,2,1,0:T(8,128)S(1)} %all-to-all-done.1.got, f32[16,7,8,128]{3,2,1,0:T(8,128)S(1)} %all_to_all.20.got.early, f32[32,8,128]{2,1,0:T(8,128)S(1)} %get-tuple-element.15.least, ...), custom_call_target="tpu_custom_call" | custom-call | flops 1000 | bytes 1142784 | tf_op jit(solution)/shard_map/pallas_call | solution.py:384
  58.1 25.4 %all_to_all.21.got = f32[32,1,128]{2,1,0:T(1,128)S(1)} all-to-all(f32[32,1,128]{2,1,0:T(1,128)S(1)} %get-tuple-element.19), channel_id=1, replica_groups=mesh['slab'=32,'mode'=16] {'slab'}, dimensions={0} | all-to-all | bytes 32768 | tf_op jit(solution)/shard_map/all_to_all | solution.py:407
  83.5 1.6 %shard_map.56 = (f32[32,1,128]{2,1,0:T(1,128)S(1)}, f32[8,128]{1,0:T(8,128)S(1)}) custom-call(f32[32,1,128]{2,1,0:T(1,128)S(1)} %all_to_all.21.got, f32[32,8,128]{2,1,0:T(8,128)S(1)} %get-tuple-element.20.gain, f32[32,8,128]{2,1,0:T(8,128)S(1)} %get-tuple-element.15.least, f32[32,8,128]{2,1,0:T(8,128)S(1)} %get-tuple-element.16.most), custom_call_target="tpu_custom_call" | custom-call | flops 1000 | bytes 430080 | tf_op jit(solution)/shard_map/pallas_call | solution.py:384
  85.1 11.6 %all_to_all.22.got = f32[32,1,128]{2,1,0:T(1,128)S(1)} all-to-all(f32[32,1,128]{2,1,0:T(1,128)S(1)} %get-tuple-element.21), channel_id=1, replica_groups=mesh['slab'=32,'mode'=16] {'slab'}, dimensions={0} | all-to-all | bytes 32768 | tf_op jit(solution)/shard_map/all_to_all | solution.py:407
  96.8 0.8 shard_map.57
Async XLA Ops:
  0.6 0.9 slice-start
  0.6 9.1 %copy-start = (f32[1,3,2,128,128]{4,3,2,1,0:T(8,128)S(1)}, f32[1,3,2,128,128]{4,3,2,1,0:T(8,128)}, u32[]{:S(2)}) copy-start(f32[1,3,2,128,128]{4,3,2,1,0:T(8,128)} %modes.3) | copy-start | bytes 1179652
  1.6 2.1 %copy-start.1 = (f32[2,8,128]{2,1,0:T(8,128)S(1)}, f32[2,8,128]{2,1,0:T(8,128)}, u32[]{:S(2)}) copy-start(f32[2,8,128]{2,1,0:T(8,128)} %design.1) | copy-start | bytes 24580
  2.3 8.0 %collective-permute-start = (f32[400,128]{1,0:T(8,128)S(1)}, f32[400,128]{1,0:T(8,128)S(1)}, u32[]{:S(2)}, u32[]{:S(2)}) collective-permute-start(f32[400,128]{1,0:T(8,128)S(1)} %pad_maximum_fusion.packed), channel_id=1, source_target_pairs={{16,0},{32,16},{48,32},{64,48},{80,64},{96,80},{112,96},{128,112},... | collective-permute-start | bytes 614408 | tf_op jit(solution)/shard_map/ppermute | solution.py:403
  3.7 6.7 %collective-permute-start.1 = (f32[2,8,128]{2,1,0:T(8,128)S(1)}, f32[2,8,128]{2,1,0:T(8,128)S(1)}, u32[]{:S(2)}, u32[]{:S(2)}) collective-permute-start(f32[2,8,128]{2,1,0:T(8,128)S(1)} %copy-done.1), channel_id=1, source_target_pairs={{0,16},{16,32},{32,48},{48,64},{64,80},{80,96},{96,112},{112,128},... | collective-permute-start | bytes 24584 | tf_op jit(solution)/shard_map/ppermute | solution.py:398
  36.7 5.9 %collective-permute-start.3 = (f32[2,8,128]{2,1,0:T(8,128)S(1)}, f32[2,8,128]{2,1,0:T(8,128)S(1)}, u32[]{:S(2)}, u32[]{:S(2)}) collective-permute-start(f32[2,8,128]{2,1,0:T(8,128)S(1)} %shard_map.52.own), channel_id=1, source_target_pairs={{16,0},{32,16},{48,32},{64,48},{80,64},{96,80},{112,96},{128,112},... | collective-permute-start | bytes 24584 | tf_op jit(solution)/shard_map/ppermute | solution.py:403
  38.0 5.4 %collective-permute-start.2 = (f32[2,8,128]{2,1,0:T(8,128)S(1)}, f32[2,8,128]{2,1,0:T(8,128)S(1)}, u32[]{:S(2)}, u32[]{:S(2)}) collective-permute-start(f32[2,8,128]{2,1,0:T(8,128)S(1)} %shard_map.52.own), channel_id=1, source_target_pairs={{0,16},{16,32},{32,48},{48,64},{64,80},{80,96},{96,112},{112,128},... | collective-permute-start | bytes 24584 | tf_op jit(solution)/shard_map/ppermute | solution.py:398
  44.1 12.7 %all-to-all-start.1 = ((f32[16,2,8,128]{3,2,1,0:T(8,128)}), f32[16,2,8,128]{3,2,1,0:T(8,128)S(1)}, u32[]{:S(2)}, u32[]{:S(2)}) async-start(f32[16,2,8,128]{3,2,1,0:T(8,128)} %shard_map.53), calls=%async_computation.1 | async-start | bytes 262144 | tf_op jit(solution)/shard_map/all_to_all | solution.py:407

commit v6 on v5

--- a/solution.py
+++ b/solution.py
@@ -138,22 +138,12 @@
     return weight
 
 
-def tail_rows(packed, k):
-    start = packed.shape[0] - (2 - k) * SUB
-    return packed[start : start + SUB]
-
-
-def first_layer(modes, eigen, packed, out, pairs):
+def first_layer(modes, eigen, out, pairs):
     def store(r, stiff, mass):
         out[r, 0] = stiff
         out[r, 1] = mass
 
-    tiles = out.shape[0]
-    forms(lambda c, a: modes[0, c, a], eigen[0], store, pairs, tiles)
-    design = tail_rows(packed, 0), tail_rows(packed, 1)
-    for r in range(tiles):
-        out[r, 4] = design[0]
-        out[r, 5] = design[1]
+    forms(lambda c, a: modes[0, c, a], eigen[0], store, pairs, out.shape[0])
 
 
 def shifted_rows(v, o):
@@ -170,27 +160,25 @@
     return jnp.concatenate(up, 0), jnp.concatenate(down, 0)
 
 
-def second_layer(modes, eigen, packed, got, before, _, out, rows, pairs, *, mode):
+def second_layer(modes, eigen, plane, design, before, after, _, out, rows, pairs, *, mode):
     def store(r, stiff, mass):
         out[r, 2] = stiff
         out[r, 3] = mass
 
+    def load(c, a):
+        return plane[c] if a else modes[0, c, 1]
+
+    m = lax.axis_index(mode)
     tiles = out.shape[0]
-    span = tiles * SUB
-
-    def load(c, a):
-        return got[c * span : (c + 1) * span] if a else modes[0, c, 1]
-
-    m = lax.axis_index(mode)
-    own = tail_rows(packed, 0), tail_rows(packed, 1)
-    after = tail_rows(got, 0), tail_rows(got, 1)
-    pair = across_x(own, before, after)
+    pair = across_x(design, before, after)
     up, down = edge_rows(*pair)
     for l in (0, 1):
         rows[l] = pair[l]
     weight = forms(load, eigen[0], store, pairs, tiles)
     half = SUB // 2
     for r in range(tiles):
+        out[r, 4] = design[0]
+        out[r, 5] = design[1]
         out[r, 6, :half] = jnp.where(m + 1 == r, up, weight[:half])
         out[r, 6, half:] = jnp.where(m - 1 == r, down, weight[half:])
 
@@ -417,25 +405,25 @@
     padded = (2, total_y + 2 * SUB, LANE)
     place = dict(slab=slab, mode=mode, sizes=sizes)
 
-    packed = jnp.concatenate([mode_shapes[0, :, 0].reshape(-1, LANE), design.reshape(-1, LANE)], 0)
-    got = from_after(packed, slab)
+    plane = from_after(mode_shapes[0, :, 0], slab)
+    after = from_after(design, slab)
     before = from_before(design, slab)
     sent = call(
         first_layer,
         [(modes, 7, SUB, LANE)],
-        [mode_shapes, eigenvalues, packed],
-        specs=[VMEM, SMEM, VMEM],
+        [mode_shapes, eigenvalues],
+        specs=[VMEM, SMEM],
         scratch=[pairs],
         flops=5_000_000,
     )
     sent, rows = call(
         functools.partial(second_layer, mode=mode),
         [(modes, 7, SUB, LANE), block],
-        [mode_shapes, eigenvalues, packed, got, before, sent],
-        specs=[VMEM, SMEM, VMEM, VMEM, VMEM, VMEM],
+        [mode_shapes, eigenvalues, plane, design, before, after, sent],
+        specs=[VMEM, SMEM, VMEM, VMEM, VMEM, VMEM, VMEM],
         scratch=[pairs],
         flops=5_000_000,
-        alias={5: 0},
+        alias={6: 0},
     )
     early = exchange(sent, mode)
     gradient = call(functools.partial(own_gradient, **place), [block], [early, rows])

time: 98.1 us -> 98.9 us (level)
  starting transfers between devices: 16.4 us -> 18.2 us
    ppermute x2 -> x3, starting transfers between devices: 2.58 us -> 3.87 us  [from_after(): return lax.ppermute(value, axis, [(i + 1, i) for i in range(count - 1)])]
    squeeze x0 -> x1, local copies, waits for them, and re-layouts: none -> 1.01 us  [local(): plane = from_after(mode_shapes[0, :, 0], slab)]
  transfers between devices with their start and end apart: 5 -> 6, of which waited for: 2 -> 2; matrix products, arithmetic and copies ran while one was open for 0% -> 0% of each run, Pallas kernels for 1% -> 1%
where the time goes in v6:
time: 98.9 us; the launch traced here: 98.3 us
  blocking collectives  62.2 us (63%)
  starting transfers between devices  18.2 us (18%)
  waiting for transfers between devices  9.6 us (10%)
  Pallas kernels  5.77 us (6%)
  between operations  1.4 us (1%)
  local copies, waits for them, and re-layouts  1.14 us (1%)
    all_to_all x3, blocking collectives, exchange(): return lax.all_to_all(value, axis, 0, 0, tiled=True)  62.2 us
    ppermute x2, starting transfers between devices, from_before(): return lax.ppermute(value, axis, [(i, i + 1) for i in range(count - 1)])  10.6 us
    all_to_all x1, waiting for transfers between devices, exchange(): return lax.all_to_all(value, axis, 0, 0, tiled=True)  8.83 us
    pallas_call x8, Pallas kernels, call(): pl.pallas_call(kernel, out_shape=outs[0] if single else outs, in_specs=sp...  5.77 us
    ppermute x3, starting transfers between devices, from_after(): return lax.ppermute(value, axis, [(i + 1, i) for i in range(count - 1)])  3.87 us
    all_to_all x1, starting transfers between devices, exchange(): return lax.all_to_all(value, axis, 0, 0, tiled=True)  3.74 us
  transfers between devices with their start and end apart: 6, of which 2 were waited for; matrix products, arithmetic and copies ran while one was open for 0% of the time, Pallas kernels for 1%

profile of v6, /device:TPU:1, one launch (start us, length us, event | category | flops | bytes accessed | tf_op | source)
XLA Modules:
  0.0 98.3 jit_solution(896763857314941139)
XLA Ops:
  0.6 0.0 copy-start
  0.6 1.0 %slice_bitcast_fusion = f32[3,128,128]{2,1,0:T(8,128)S(1)} fusion(f32[1,3,2,128,128]{4,3,2,1,0:T(8,128)} %modes.3), kind=kLoop, calls=%fused_computation | loop fusion | bytes 393216 | tf_op jit(solution)/shard_map/squeeze | solution.py:408
  1.6 1.3 %collective-permute-start = (f32[3,128,128]{2,1,0:T(8,128)S(1)}, f32[3,128,128]{2,1,0:T(8,128)S(1)}, u32[]{:S(2)}, u32[]{:S(2)}) collective-permute-start(f32[3,128,128]{2,1,0:T(8,128)S(1)} %slice_bitcast_fusion), channel_id=1, source_target_pairs={{16,0},{32,16},{48,32},{64,48},{80,64},{96,80},{112,96},{128,112},... | collective-permute-start | bytes 589832 | tf_op jit(solution)/shard_map/ppermute | solution.py:391
  2.9 1.3 %collective-permute-start.2 = (f32[2,8,128]{2,1,0:T(8,128)}, f32[2,8,128]{2,1,0:T(8,128)S(1)}, u32[]{:S(2)}, u32[]{:S(2)}) collective-permute-start(f32[2,8,128]{2,1,0:T(8,128)} %design.3), channel_id=1, source_target_pairs={{16,0},{32,16},{48,32},{64,48},{80,64},{96,80},{112,96},{128,112},... | collective-permute-start | bytes 24584 | tf_op jit(solution)/shard_map/ppermute | solution.py:391
  4.2 6.1 %collective-permute-start.1 = (f32[2,8,128]{2,1,0:T(8,128)}, f32[2,8,128]{2,1,0:T(8,128)S(1)}, u32[]{:S(2)}, u32[]{:S(2)}) collective-permute-start(f32[2,8,128]{2,1,0:T(8,128)} %design.3), channel_id=1, source_target_pairs={{0,16},{16,32},{32,48},{48,64},{64,80},{80,96},{96,112},{112,128},... | collective-permute-start | bytes 24584 | tf_op jit(solution)/shard_map/ppermute | solution.py:386
  11.0 0.0 copy-done
  11.0 0.0 copy-start.1
  11.0 0.5 shard_map.50._
  11.5 0.0 collective-permute-done.2.after
  11.5 0.0 collective-permute-done.1.before
  11.6 0.0 collective-permute-done.plane
  11.6 0.1 copy-done.1
  11.7 0.6 shard_map.51
  12.3 24.5 %all_to_all.20.got.early = f32[16,7,8,128]{3,2,1,0:T(8,128)S(1)} all-to-all(f32[16,7,8,128]{3,2,1,0:T(8,128)S(1)} %get-tuple-element.13), channel_id=1, replica_groups=mesh['slab'=32,'mode'=16] {'mode'}, dimensions={0} | all-to-all | bytes 917504 | tf_op jit(solution)/shard_map/all_to_all | solution.py:395
  36.8 0.2 shard_map.52.own
  37.0 1.3 %collective-permute-start.4 = (f32[2,8,128]{2,1,0:T(8,128)S(1)}, f32[2,8,128]{2,1,0:T(8,128)S(1)}, u32[]{:S(2)}, u32[]{:S(2)}) collective-permute-start(f32[2,8,128]{2,1,0:T(8,128)S(1)} %shard_map.52.own), channel_id=1, source_target_pairs={{16,0},{32,16},{48,32},{64,48},{80,64},{96,80},{112,96},{128,112},... | collective-permute-start | bytes 24584 | tf_op jit(solution)/shard_map/ppermute | solution.py:391
  38.3 4.5 %collective-permute-start.3 = (f32[2,8,128]{2,1,0:T(8,128)S(1)}, f32[2,8,128]{2,1,0:T(8,128)S(1)}, u32[]{:S(2)}, u32[]{:S(2)}) collective-permute-start(f32[2,8,128]{2,1,0:T(8,128)S(1)} %shard_map.52.own), channel_id=1, source_target_pairs={{0,16},{16,32},{32,48},{48,64},{64,80},{80,96},{96,112},{112,128},... | collective-permute-start | bytes 24584 | tf_op jit(solution)/shard_map/ppermute | solution.py:386
  42.8 0.0 collective-permute-done.4.after
  42.8 0.8 collective-permute-done.3.before
  43.6 0.7 shard_map.53
  44.2 3.7 %all-to-all-start.1 = ((f32[16,2,8,128]{3,2,1,0:T(8,128)}), f32[16,2,8,128]{3,2,1,0:T(8,128)S(1)}, u32[]{:S(2)}, u32[]{:S(2)}) async-start(f32[16,2,8,128]{3,2,1,0:T(8,128)} %shard_map.53), calls=%async_computation.1 | async-start | bytes 262144 | tf_op jit(solution)/shard_map/all_to_all | solution.py:395
  48.0 0.1 shard_map.54
  48.0 8.8 %all-to-all-done.1.got = f32[16,2,8,128]{3,2,1,0:T(8,128)S(1)} async-done(((f32[16,2,8,128]{3,2,1,0:T(8,128)}), f32[16,2,8,128]{3,2,1,0:T(8,128)S(1)}, u32[]{:S(2)}, u32[]{:S(2)}) %all-to-all-start.1) | async-done | bytes 131104 | tf_op jit(solution)/shard_map/all_to_all | solution.py:395
  56.9 1.4 %shard_map.55 = (f32[32,8,128]{2,1,0:T(8,128)S(1)}, f32[2,8,128]{2,1,0:T(8,128)S(1)}, f32[32,1,128]{2,1,0:T(1,128)S(1)}) custom-call(f32[16,2,8,128]{3,2,1,0:T(8,128)S(1)} %all-to-all-done.1.got, f32[16,7,8,128]{3,2,1,0:T(8,128)S(1)} %all_to_all.20.got.early, f32[32,8,128]{2,1,0:T(8,128)S(1)} %get-tuple-element.15.least, ...), custom_call_target="tpu_custom_call" | custom-call | flops 1000 | bytes 1142784 | tf_op jit(solution)/shard_map/pallas_call | solution.py:372
  58.2 26.0 %all_to_all.21.got = f32[32,1,128]{2,1,0:T(1,128)S(1)} all-to-all(f32[32,1,128]{2,1,0:T(1,128)S(1)} %get-tuple-element.19), channel_id=1, replica_groups=mesh['slab'=32,'mode'=16] {'slab'}, dimensions={0} | all-to-all | bytes 32768 | tf_op jit(solution)/shard_map/all_to_all | solution.py:395
  84.2 1.6 %shard_map.56 = (f32[32,1,128]{2,1,0:T(1,128)S(1)}, f32[8,128]{1,0:T(8,128)S(1)}) custom-call(f32[32,1,128]{2,1,0:T(1,128)S(1)} %all_to_all.21.got, f32[32,8,128]{2,1,0:T(8,128)S(1)} %get-tuple-element.20.gain, f32[32,8,128]{2,1,0:T(8,128)S(1)} %get-tuple-element.15.least, f32[32,8,128]{2,1,0:T(8,128)S(1)} %get-tuple-element.16.most), custom_call_target="tpu_custom_call" | custom-call | flops 1000 | bytes 430080 | tf_op jit(solution)/shard_map/pallas_call | solution.py:372
  85.9 11.6 %all_to_all.22.got = f32[32,1,128]{2,1,0:T(1,128)S(1)} all-to-all(f32[32,1,128]{2,1,0:T(1,128)S(1)} %get-tuple-element.21), channel_id=1, replica_groups=mesh['slab'=32,'mode'=16] {'slab'}, dimensions={0} | all-to-all | bytes 32768 | tf_op jit(solution)/shard_map/all_to_all | solution.py:395
  97.5 0.8 shard_map.57
Async XLA Ops:
  0.6 10.4 %copy-start = (f32[1,3,2,128,128]{4,3,2,1,0:T(8,128)S(1)}, f32[1,3,2,128,128]{4,3,2,1,0:T(8,128)}, u32[]{:S(2)}) copy-start(f32[1,3,2,128,128]{4,3,2,1,0:T(8,128)} %modes.3) | copy-start | bytes 1179652
  1.6 9.9 %collective-permute-start = (f32[3,128,128]{2,1,0:T(8,128)S(1)}, f32[3,128,128]{2,1,0:T(8,128)S(1)}, u32[]{:S(2)}, u32[]{:S(2)}) collective-permute-start(f32[3,128,128]{2,1,0:T(8,128)S(1)} %slice_bitcast_fusion), channel_id=1, source_target_pairs={{16,0},{32,16},{48,32},{64,48},{80,64},{96,80},{112,96},{128,112},... | collective-permute-start | bytes 589832 | tf_op jit(solution)/shard_map/ppermute | solution.py:391
  2.9 8.6 %collective-permute-start.2 = (f32[2,8,128]{2,1,0:T(8,128)}, f32[2,8,128]{2,1,0:T(8,128)S(1)}, u32[]{:S(2)}, u32[]{:S(2)}) collective-permute-start(f32[2,8,128]{2,1,0:T(8,128)} %design.3), channel_id=1, source_target_pairs={{16,0},{32,16},{48,32},{64,48},{80,64},{96,80},{112,96},{128,112},... | collective-permute-start | bytes 24584 | tf_op jit(solution)/shard_map/ppermute | solution.py:391
  4.2 7.3 %collective-permute-start.1 = (f32[2,8,128]{2,1,0:T(8,128)}, f32[2,8,128]{2,1,0:T(8,128)S(1)}, u32[]{:S(2)}, u32[]{:S(2)}) collective-permute-start(f32[2,8,128]{2,1,0:T(8,128)} %design.3), channel_id=1, source_target_pairs={{0,16},{16,32},{32,48},{48,64},{64,80},{80,96},{96,112},{112,128},... | collective-permute-start | bytes 24584 | tf_op jit(solution)/shard_map/ppermute | solution.py:386
  11.0 0.7 copy-start.1
  37.0 5.8 %collective-permute-start.4 = (f32[2,8,128]{2,1,0:T(8,128)S(1)}, f32[2,8,128]{2,1,0:T(8,128)S(1)}, u32[]{:S(2)}, u32[]{:S(2)}) collective-permute-start(f32[2,8,128]{2,1,0:T(8,128)S(1)} %shard_map.52.own), channel_id=1, source_target_pairs={{16,0},{32,16},{48,32},{64,48},{80,64},{96,80},{112,96},{128,112},... | collective-permute-start | bytes 24584 | tf_op jit(solution)/shard_map/ppermute | solution.py:391
  38.3 5.3 %collective-permute-start.3 = (f32[2,8,128]{2,1,0:T(8,128)S(1)}, f32[2,8,128]{2,1,0:T(8,128)S(1)}, u32[]{:S(2)}, u32[]{:S(2)}) collective-permute-start(f32[2,8,128]{2,1,0:T(8,128)S(1)} %shard_map.52.own), channel_id=1, source_target_pairs={{0,16},{16,32},{32,48},{48,64},{64,80},{80,96},{96,112},{112,128},... | collective-permute-start | bytes 24584 | tf_op jit(solution)/shard_map/ppermute | solution.py:386
  44.2 12.6 %all-to-all-start.1 = ((f32[16,2,8,128]{3,2,1,0:T(8,128)}), f32[16,2,8,128]{3,2,1,0:T(8,128)S(1)}, u32[]{:S(2)}, u32[]{:S(2)}) async-start(f32[16,2,8,128]{3,2,1,0:T(8,128)} %shard_map.53), calls=%async_computation.1 | async-start | bytes 262144 | tf_op jit(solution)/shard_map/all_to_all | solution.py:395

commit v7 on v5

--- a/solution.py
+++ b/solution.py
@@ -240,7 +240,10 @@
         out[l] = tent_lanes((slope * stiff[l] - mass[l]) * inverse_weight * inverse)
 
 
-def gradient_copies(own, before, after, out):
+def gradient_copies(own, even, odd, out, *, slab):
+    is_even = lax.rem(lax.axis_index(slab), 2) == 0
+    before = [jnp.where(is_even, odd[l], even[l]) for l in (0, 1)]
+    after = [jnp.where(is_even, even[l], odd[l]) for l in (0, 1)]
     pair = across_x(own, before, after)
     for r in range(out.shape[0]):
         out[r, 0] = pair[0]
@@ -403,6 +406,13 @@
     return lax.ppermute(value, axis, [(i + 1, i) for i in range(count - 1)])
 
 
+def swapped(value, axis, first):
+    pairs = []
+    for i in range(first, lax.axis_size(axis) - 1, 2):
+        pairs += [(i, i + 1), (i + 1, i)]
+    return lax.ppermute(value, axis, pairs)
+
+
 def exchange(value, axis):
     return lax.all_to_all(value, axis, 0, 0, tiled=True)
 
@@ -439,9 +449,11 @@
     )
     early = exchange(sent, mode)
     gradient = call(functools.partial(own_gradient, **place), [block], [early, rows])
-    after = from_after(gradient, slab)
-    before = from_before(gradient, slab)
-    copies = call(gradient_copies, [(modes, *block)], [gradient, before, after])
+    even = swapped(gradient, slab, 0)
+    odd = swapped(gradient, slab, 1)
+    copies = call(
+        functools.partial(gradient_copies, slab=slab), [(modes, *block)], [gradient, even, odd]
+    )
     whole = exchange(copies, mode)
     vectors = (2 * modes, SUB, LANE)
     least, most, goals, measures = call(

time: 98.1 us -> 98.3 us (level)
  blocking collectives: 62.7 us -> 60.3 us
  starting transfers between devices: 16.4 us -> 18.8 us
    ppermute x0 -> x2, starting transfers between devices: none -> 7.99 us  [swapped(): return lax.ppermute(value, axis, pairs)]
    ppermute x2 -> x1, starting transfers between devices: 10.1 us -> 5.44 us  [from_before(): return lax.ppermute(value, axis, [(i, i + 1) for i in range(count - 1)])]
    all_to_all x3, blocking collectives: 62.7 us -> 60.3 us  [exchange(): return lax.all_to_all(value, axis, 0, 0, tiled=True)]
    ppermute x2 -> x1, starting transfers between devices: 2.58 us -> 1.29 us  [from_after(): return lax.ppermute(value, axis, [(i + 1, i) for i in range(count - 1)])]
    ppermute x0 -> x2, waiting for transfers between devices: none -> 1.02 us  [swapped(): return lax.ppermute(value, axis, pairs)]
where the time goes in v7:
time: 98.3 us; the launch traced here: 97.8 us
  blocking collectives  60.3 us (61%)
  starting transfers between devices  18.8 us (19%)
  waiting for transfers between devices  9.85 us (10%)
  Pallas kernels  5.78 us (6%)
  between operations  1.39 us (1%)
    all_to_all x3, blocking collectives, exchange(): return lax.all_to_all(value, axis, 0, 0, tiled=True)  60.3 us
    all_to_all x1, waiting for transfers between devices, exchange(): return lax.all_to_all(value, axis, 0, 0, tiled=True)  8.83 us
    ppermute x2, starting transfers between devices, swapped(): return lax.ppermute(value, axis, pairs)  7.99 us
    pallas_call x8, Pallas kernels, call(): pl.pallas_call(kernel, out_shape=outs[0] if single else outs, in_specs=sp...  5.78 us
    ppermute x1, starting transfers between devices, from_before(): return lax.ppermute(value, axis, [(i, i + 1) for i in range(count - 1)])  5.44 us
    all_to_all x1, starting transfers between devices, exchange(): return lax.all_to_all(value, axis, 0, 0, tiled=True)  4.08 us
  transfers between devices with their start and end apart: 5, of which 2 were waited for; matrix products, arithmetic and copies ran while one was open for 0% of the time, Pallas kernels for 1%

profile of v7, /device:TPU:1, one launch (start us, length us, event | category | flops | bytes accessed | tf_op | source)
XLA Modules:
  0.0 97.8 jit_solution(684349411515655267)
XLA Ops:
  0.6 0.0 slice-start
  0.6 0.0 copy-start
  0.6 0.9 slice-done
  1.6 0.0 copy-start.1
  1.6 0.8 pad_maximum_fusion.packed
  2.3 1.3 %collective-permute-start = (f32[400,128]{1,0:T(8,128)S(1)}, f32[400,128]{1,0:T(8,128)S(1)}, u32[]{:S(2)}, u32[]{:S(2)}) collective-permute-start(f32[400,128]{1,0:T(8,128)S(1)} %pad_maximum_fusion.packed), channel_id=1, source_target_pairs={{16,0},{32,16},{48,32},{64,48},{80,64},{96,80},{112,96},{128,112},... | collective-permute-start | bytes 614408 | tf_op jit(solution)/shard_map/ppermute | solution.py:406
  3.6 0.0 copy-done.1
  3.7 5.4 %collective-permute-start.1 = (f32[2,8,128]{2,1,0:T(8,128)S(1)}, f32[2,8,128]{2,1,0:T(8,128)S(1)}, u32[]{:S(2)}, u32[]{:S(2)}) collective-permute-start(f32[2,8,128]{2,1,0:T(8,128)S(1)} %copy-done.1), channel_id=1, source_target_pairs={{0,16},{16,32},{32,48},{48,64},{64,80},{80,96},{96,112},{112,128},... | collective-permute-start | bytes 24584 | tf_op jit(solution)/shard_map/ppermute | solution.py:401
  9.8 0.0 copy-done
  9.8 0.5 shard_map.50._
  10.3 0.0 collective-permute-done.1.before
  10.3 0.0 collective-permute-done.got
  10.3 0.6 shard_map.51
  10.9 25.6 %all_to_all.20.got.early = f32[16,7,8,128]{3,2,1,0:T(8,128)S(1)} all-to-all(f32[16,7,8,128]{3,2,1,0:T(8,128)S(1)} %get-tuple-element.13), channel_id=1, replica_groups=mesh['slab'=32,'mode'=16] {'mode'}, dimensions={0} | all-to-all | bytes 917504 | tf_op jit(solution)/shard_map/all_to_all | solution.py:417
  36.5 0.2 shard_map.52.own
  36.7 0.7 collective-permute-start.3
  37.4 7.3 %collective-permute-start.2 = (f32[2,8,128]{2,1,0:T(8,128)S(1)}, f32[2,8,128]{2,1,0:T(8,128)S(1)}, u32[]{:S(2)}, u32[]{:S(2)}) collective-permute-start(f32[2,8,128]{2,1,0:T(8,128)S(1)} %shard_map.52.own), channel_id=1, source_target_pairs={{0,16},{16,0},{32,48},{48,32},{64,80},{80,64},{96,112},{112,96},{1... | collective-permute-start | bytes 24584 | tf_op jit(solution)/shard_map/ppermute | solution.py:413
  44.7 0.0 collective-permute-done.3.odd
  44.7 1.0 %collective-permute-done.2.even = f32[2,8,128]{2,1,0:T(8,128)S(1)} collective-permute-done((f32[2,8,128]{2,1,0:T(8,128)S(1)}, f32[2,8,128]{2,1,0:T(8,128)S(1)}, u32[]{:S(2)}, u32[]{:S(2)}) %collective-permute-start.2) | collective-permute-done | bytes 8224 | tf_op jit(solution)/shard_map/ppermute | solution.py:413
  45.7 0.7 shard_map.53
  46.4 4.1 %all-to-all-start.1 = ((f32[16,2,8,128]{3,2,1,0:T(8,128)}), f32[16,2,8,128]{3,2,1,0:T(8,128)S(1)}, u32[]{:S(2)}, u32[]{:S(2)}) async-start(f32[16,2,8,128]{3,2,1,0:T(8,128)} %shard_map.53), calls=%async_computation.1 | async-start | bytes 262144 | tf_op jit(solution)/shard_map/all_to_all | solution.py:417
  50.5 0.1 shard_map.54
  50.5 8.8 %all-to-all-done.1.got = f32[16,2,8,128]{3,2,1,0:T(8,128)S(1)} async-done(((f32[16,2,8,128]{3,2,1,0:T(8,128)}), f32[16,2,8,128]{3,2,1,0:T(8,128)S(1)}, u32[]{:S(2)}, u32[]{:S(2)}) %all-to-all-start.1) | async-done | bytes 131104 | tf_op jit(solution)/shard_map/all_to_all | solution.py:417
  59.4 1.4 %shard_map.55 = (f32[32,8,128]{2,1,0:T(8,128)S(1)}, f32[2,8,128]{2,1,0:T(8,128)S(1)}, f32[32,1,128]{2,1,0:T(1,128)S(1)}) custom-call(f32[16,2,8,128]{3,2,1,0:T(8,128)S(1)} %all-to-all-done.1.got, f32[16,7,8,128]{3,2,1,0:T(8,128)S(1)} %all_to_all.20.got.early, f32[32,8,128]{2,1,0:T(8,128)S(1)} %get-tuple-element.15.least, ...), custom_call_target="tpu_custom_call" | custom-call | flops 1000 | bytes 1142784 | tf_op jit(solution)/shard_map/pallas_call | solution.py:387
  60.7 23.0 %all_to_all.21.got = f32[32,1,128]{2,1,0:T(1,128)S(1)} all-to-all(f32[32,1,128]{2,1,0:T(1,128)S(1)} %get-tuple-element.19), channel_id=1, replica_groups=mesh['slab'=32,'mode'=16] {'slab'}, dimensions={0} | all-to-all | bytes 32768 | tf_op jit(solution)/shard_map/all_to_all | solution.py:417
  83.7 1.6 %shard_map.56 = (f32[32,1,128]{2,1,0:T(1,128)S(1)}, f32[8,128]{1,0:T(8,128)S(1)}) custom-call(f32[32,1,128]{2,1,0:T(1,128)S(1)} %all_to_all.21.got, f32[32,8,128]{2,1,0:T(8,128)S(1)} %get-tuple-element.20.gain, f32[32,8,128]{2,1,0:T(8,128)S(1)} %get-tuple-element.15.least, f32[32,8,128]{2,1,0:T(8,128)S(1)} %get-tuple-element.16.most), custom_call_target="tpu_custom_call" | custom-call | flops 1000 | bytes 430080 | tf_op jit(solution)/shard_map/pallas_call | solution.py:387
  85.3 11.6 %all_to_all.22.got = f32[32,1,128]{2,1,0:T(1,128)S(1)} all-to-all(f32[32,1,128]{2,1,0:T(1,128)S(1)} %get-tuple-element.21), channel_id=1, replica_groups=mesh['slab'=32,'mode'=16] {'slab'}, dimensions={0} | all-to-all | bytes 32768 | tf_op jit(solution)/shard_map/all_to_all | solution.py:417
  97.0 0.8 shard_map.57
Async XLA Ops:
  0.6 0.9 slice-start
  0.6 9.1 %copy-start = (f32[1,3,2,128,128]{4,3,2,1,0:T(8,128)S(1)}, f32[1,3,2,128,128]{4,3,2,1,0:T(8,128)}, u32[]{:S(2)}) copy-start(f32[1,3,2,128,128]{4,3,2,1,0:T(8,128)} %modes.3) | copy-start | bytes 1179652
  1.6 2.1 %copy-start.1 = (f32[2,8,128]{2,1,0:T(8,128)S(1)}, f32[2,8,128]{2,1,0:T(8,128)}, u32[]{:S(2)}) copy-start(f32[2,8,128]{2,1,0:T(8,128)} %design.1) | copy-start | bytes 24580
  2.3 8.0 %collective-permute-start = (f32[400,128]{1,0:T(8,128)S(1)}, f32[400,128]{1,0:T(8,128)S(1)}, u32[]{:S(2)}, u32[]{:S(2)}) collective-permute-start(f32[400,128]{1,0:T(8,128)S(1)} %pad_maximum_fusion.packed), channel_id=1, source_target_pairs={{16,0},{32,16},{48,32},{64,48},{80,64},{96,80},{112,96},{128,112},... | collective-permute-start | bytes 614408 | tf_op jit(solution)/shard_map/ppermute | solution.py:406
  3.7 6.7 %collective-permute-start.1 = (f32[2,8,128]{2,1,0:T(8,128)S(1)}, f32[2,8,128]{2,1,0:T(8,128)S(1)}, u32[]{:S(2)}, u32[]{:S(2)}) collective-permute-start(f32[2,8,128]{2,1,0:T(8,128)S(1)} %copy-done.1), channel_id=1, source_target_pairs={{0,16},{16,32},{32,48},{48,64},{64,80},{80,96},{96,112},{112,128},... | collective-permute-start | bytes 24584 | tf_op jit(solution)/shard_map/ppermute | solution.py:401
  36.7 8.0 %collective-permute-start.3 = (f32[2,8,128]{2,1,0:T(8,128)S(1)}, f32[2,8,128]{2,1,0:T(8,128)S(1)}, u32[]{:S(2)}, u32[]{:S(2)}) collective-permute-start(f32[2,8,128]{2,1,0:T(8,128)S(1)} %shard_map.52.own), channel_id=1, source_target_pairs={{16,32},{32,16},{48,64},{64,48},{80,96},{96,80},{112,128},{128,112... | collective-permute-start | bytes 24584 | tf_op jit(solution)/shard_map/ppermute | solution.py:413
  37.4 8.4 %collective-permute-start.2 = (f32[2,8,128]{2,1,0:T(8,128)S(1)}, f32[2,8,128]{2,1,0:T(8,128)S(1)}, u32[]{:S(2)}, u32[]{:S(2)}) collective-permute-start(f32[2,8,128]{2,1,0:T(8,128)S(1)} %shard_map.52.own), channel_id=1, source_target_pairs={{0,16},{16,0},{32,48},{48,32},{64,80},{80,64},{96,112},{112,96},{1... | collective-permute-start | bytes 24584 | tf_op jit(solution)/shard_map/ppermute | solution.py:413
  46.4 13.0 %all-to-all-start.1 = ((f32[16,2,8,128]{3,2,1,0:T(8,128)}), f32[16,2,8,128]{3,2,1,0:T(8,128)S(1)}, u32[]{:S(2)}, u32[]{:S(2)}) async-start(f32[16,2,8,128]{3,2,1,0:T(8,128)} %shard_map.53), calls=%async_computation.1 | async-start | bytes 262144 | tf_op jit(solution)/shard_map/all_to_all | solution.py:417

commit v8 on v7

--- a/solution.py
+++ b/solution.py
@@ -138,6 +138,23 @@
     return weight
 
 
+def pack(modes, design, out, sems):
+    planes, rows = modes.shape[1], modes.shape[3]
+    copies = [
+        pltpu.make_async_copy(modes.at[0, c, 0], out.at[pl.ds(c * rows, rows)], sems.at[c])
+        for c in range(planes)
+    ]
+    for l in (0, 1):
+        start = planes * rows + l * SUB
+        copies.append(
+            pltpu.make_async_copy(design.at[l], out.at[pl.ds(start, SUB)], sems.at[planes + l])
+        )
+    for copy in copies:
+        copy.start()
+    for copy in copies:
+        copy.wait()
+
+
 def tail_rows(packed, k):
     start = packed.shape[0] - (2 - k) * SUB
     return packed[start : start + SUB]
@@ -427,7 +444,18 @@
     padded = (2, total_y + 2 * SUB, LANE)
     place = dict(slab=slab, mode=mode, sizes=sizes)
 
-    packed = jnp.concatenate([mode_shapes[0, :, 0].reshape(-1, LANE), design.reshape(-1, LANE)], 0)
+    packed = pl.pallas_call(
+        pack,
+        out_shape=jax.ShapeDtypeStruct((3 * total_y + 2 * SUB, LANE), F32),
+        in_specs=[pl.BlockSpec(memory_space=pltpu.HBM)] * 2,
+        out_specs=VMEM,
+        scratch_shapes=[pltpu.SemaphoreType.DMA((5,))],
+        compiler_params=pltpu.CompilerParams(vmem_limit_bytes=GRANT),
+        name="pack",
+    )(
+        pltpu.with_memory_space_constraint(mode_shapes, pltpu.HBM),
+        pltpu.with_memory_space_constraint(design, pltpu.HBM),
+    )
     got = from_after(packed, slab)
     before = from_before(design, slab)
     sent = call(

time: 98.3 us -> 97.6 us (level)
  Pallas kernels: 5.78 us -> 6.77 us
    pallas_call x0 -> x1, Pallas kernels: none -> 1 us  [local(): pl.pallas_call(pack, out_shape=jax.ShapeDtypeStruct((3 * total_y + 2 * SU...]
where the time goes in v8:
time: 97.6 us; the launch traced here: 97.1 us
  blocking collectives  60.3 us (62%)
  starting transfers between devices  18.8 us (19%)
  waiting for transfers between devices  9.85 us (10%)
  Pallas kernels  6.77 us (7%)
  between operations  1.4 us (1%)
    all_to_all x3, blocking collectives, exchange(): return lax.all_to_all(value, axis, 0, 0, tiled=True)  60.3 us
    all_to_all x1, waiting for transfers between devices, exchange(): return lax.all_to_all(value, axis, 0, 0, tiled=True)  8.83 us
    ppermute x2, starting transfers between devices, swapped(): return lax.ppermute(value, axis, pairs)  7.99 us
    pallas_call x8, Pallas kernels, call(): pl.pallas_call(kernel, out_shape=outs[0] if single else outs, in_specs=sp...  5.77 us
    ppermute x1, starting transfers between devices, from_before(): return lax.ppermute(value, axis, [(i, i + 1) for i in range(count - 1)])  5.44 us
    all_to_all x1, starting transfers between devices, exchange(): return lax.all_to_all(value, axis, 0, 0, tiled=True)  4.08 us
  transfers between devices with their start and end apart: 5, of which 2 were waited for; matrix products, arithmetic and copies ran while one was open for 0% of the time, Pallas kernels for 1%

profile of v8, /device:TPU:1, one launch (start us, length us, event | category | flops | bytes accessed | tf_op | source)
XLA Modules:
  0.0 97.1 jit_solution(6345328287174449524)
XLA Ops:
  0.6 0.0 copy-start
  0.6 0.0 copy-start.1
  0.6 1.0 %pack.1.packed = f32[400,128]{1,0:T(8,128)S(1)} custom-call(f32[1,3,2,128,128]{4,3,2,1,0:T(8,128)} %modes.5, f32[2,8,128]{2,1,0:T(8,128)} %design.3), custom_call_target="tpu_custom_call" | custom-call | tf_op jit(solution)/shard_map/pack/pallas_call | solution.py:447
  1.7 1.3 %collective-permute-start = (f32[400,128]{1,0:T(8,128)S(1)}, f32[400,128]{1,0:T(8,128)S(1)}, u32[]{:S(2)}, u32[]{:S(2)}) collective-permute-start(f32[400,128]{1,0:T(8,128)S(1)} %pack.1.packed), channel_id=1, source_target_pairs={{16,0},{32,16},{48,32},{64,48},{80,64},{96,80},{112,96},{128,112},... | collective-permute-start | bytes 614408 | tf_op jit(solution)/shard_map/ppermute | solution.py:423
  3.0 0.0 copy-done.1
  3.0 5.4 %collective-permute-start.1 = (f32[2,8,128]{2,1,0:T(8,128)S(1)}, f32[2,8,128]{2,1,0:T(8,128)S(1)}, u32[]{:S(2)}, u32[]{:S(2)}) collective-permute-start(f32[2,8,128]{2,1,0:T(8,128)S(1)} %copy-done.1), channel_id=1, source_target_pairs={{0,16},{16,32},{32,48},{48,64},{64,80},{80,96},{96,112},{112,128},... | collective-permute-start | bytes 24584 | tf_op jit(solution)/shard_map/ppermute | solution.py:418
  9.1 0.0 copy-done
  9.1 0.5 shard_map.50._
  9.6 0.0 collective-permute-done.1.before
  9.6 0.0 collective-permute-done.got
  9.6 0.6 shard_map.51
  10.2 25.6 %all_to_all.20.got.early = f32[16,7,8,128]{3,2,1,0:T(8,128)S(1)} all-to-all(f32[16,7,8,128]{3,2,1,0:T(8,128)S(1)} %get-tuple-element.13), channel_id=1, replica_groups=mesh['slab'=32,'mode'=16] {'mode'}, dimensions={0} | all-to-all | bytes 917504 | tf_op jit(solution)/shard_map/all_to_all | solution.py:434
  35.8 0.2 shard_map.52.own
  36.0 0.7 collective-permute-start.3
  36.7 7.3 %collective-permute-start.2 = (f32[2,8,128]{2,1,0:T(8,128)S(1)}, f32[2,8,128]{2,1,0:T(8,128)S(1)}, u32[]{:S(2)}, u32[]{:S(2)}) collective-permute-start(f32[2,8,128]{2,1,0:T(8,128)S(1)} %shard_map.52.own), channel_id=1, source_target_pairs={{0,16},{16,0},{32,48},{48,32},{64,80},{80,64},{96,112},{112,96},{1... | collective-permute-start | bytes 24584 | tf_op jit(solution)/shard_map/ppermute | solution.py:430
  44.0 0.0 collective-permute-done.3.odd
  44.0 1.0 %collective-permute-done.2.even = f32[2,8,128]{2,1,0:T(8,128)S(1)} collective-permute-done((f32[2,8,128]{2,1,0:T(8,128)S(1)}, f32[2,8,128]{2,1,0:T(8,128)S(1)}, u32[]{:S(2)}, u32[]{:S(2)}) %collective-permute-start.2) | collective-permute-done | bytes 8224 | tf_op jit(solution)/shard_map/ppermute | solution.py:430
  45.0 0.7 shard_map.53
  45.7 4.1 %all-to-all-start.1 = ((f32[16,2,8,128]{3,2,1,0:T(8,128)}), f32[16,2,8,128]{3,2,1,0:T(8,128)S(1)}, u32[]{:S(2)}, u32[]{:S(2)}) async-start(f32[16,2,8,128]{3,2,1,0:T(8,128)} %shard_map.53), calls=%async_computation.1 | async-start | bytes 262144 | tf_op jit(solution)/shard_map/all_to_all | solution.py:434
  49.8 0.1 shard_map.54
  49.8 8.8 %all-to-all-done.1.got = f32[16,2,8,128]{3,2,1,0:T(8,128)S(1)} async-done(((f32[16,2,8,128]{3,2,1,0:T(8,128)}), f32[16,2,8,128]{3,2,1,0:T(8,128)S(1)}, u32[]{:S(2)}, u32[]{:S(2)}) %all-to-all-start.1) | async-done | bytes 131104 | tf_op jit(solution)/shard_map/all_to_all | solution.py:434
  58.7 1.4 %shard_map.55 = (f32[32,8,128]{2,1,0:T(8,128)S(1)}, f32[2,8,128]{2,1,0:T(8,128)S(1)}, f32[32,1,128]{2,1,0:T(1,128)S(1)}) custom-call(f32[16,2,8,128]{3,2,1,0:T(8,128)S(1)} %all-to-all-done.1.got, f32[16,7,8,128]{3,2,1,0:T(8,128)S(1)} %all_to_all.20.got.early, f32[32,8,128]{2,1,0:T(8,128)S(1)} %get-tuple-element.15.least, ...), custom_call_target="tpu_custom_call" | custom-call | flops 1000 | bytes 1142784 | tf_op jit(solution)/shard_map/pallas_call | solution.py:404
  60.0 23.0 %all_to_all.21.got = f32[32,1,128]{2,1,0:T(1,128)S(1)} all-to-all(f32[32,1,128]{2,1,0:T(1,128)S(1)} %get-tuple-element.19), channel_id=1, replica_groups=mesh['slab'=32,'mode'=16] {'slab'}, dimensions={0} | all-to-all | bytes 32768 | tf_op jit(solution)/shard_map/all_to_all | solution.py:434
  83.0 1.6 %shard_map.56 = (f32[32,1,128]{2,1,0:T(1,128)S(1)}, f32[8,128]{1,0:T(8,128)S(1)}) custom-call(f32[32,1,128]{2,1,0:T(1,128)S(1)} %all_to_all.21.got, f32[32,8,128]{2,1,0:T(8,128)S(1)} %get-tuple-element.20.gain, f32[32,8,128]{2,1,0:T(8,128)S(1)} %get-tuple-element.15.least, f32[32,8,128]{2,1,0:T(8,128)S(1)} %get-tuple-element.16.most), custom_call_target="tpu_custom_call" | custom-call | flops 1000 | bytes 430080 | tf_op jit(solution)/shard_map/pallas_call | solution.py:404
  84.6 11.6 %all_to_all.22.got = f32[32,1,128]{2,1,0:T(1,128)S(1)} all-to-all(f32[32,1,128]{2,1,0:T(1,128)S(1)} %get-tuple-element.21), channel_id=1, replica_groups=mesh['slab'=32,'mode'=16] {'slab'}, dimensions={0} | all-to-all | bytes 32768 | tf_op jit(solution)/shard_map/all_to_all | solution.py:434
  96.3 0.8 shard_map.57
Async XLA Ops:
  0.6 8.4 %copy-start = (f32[1,3,2,128,128]{4,3,2,1,0:T(8,128)S(1)}, f32[1,3,2,128,128]{4,3,2,1,0:T(8,128)}, u32[]{:S(2)}) copy-start(f32[1,3,2,128,128]{4,3,2,1,0:T(8,128)} %modes.5) | copy-start | bytes 1179652
  0.6 2.3 %copy-start.1 = (f32[2,8,128]{2,1,0:T(8,128)S(1)}, f32[2,8,128]{2,1,0:T(8,128)}, u32[]{:S(2)}) copy-start(f32[2,8,128]{2,1,0:T(8,128)} %design.3) | copy-start | bytes 24580
  1.7 8.0 %collective-permute-start = (f32[400,128]{1,0:T(8,128)S(1)}, f32[400,128]{1,0:T(8,128)S(1)}, u32[]{:S(2)}, u32[]{:S(2)}) collective-permute-start(f32[400,128]{1,0:T(8,128)S(1)} %pack.1.packed), channel_id=1, source_target_pairs={{16,0},{32,16},{48,32},{64,48},{80,64},{96,80},{112,96},{128,112},... | collective-permute-start | bytes 614408 | tf_op jit(solution)/shard_map/ppermute | solution.py:423
  3.0 6.7 %collective-permute-start.1 = (f32[2,8,128]{2,1,0:T(8,128)S(1)}, f32[2,8,128]{2,1,0:T(8,128)S(1)}, u32[]{:S(2)}, u32[]{:S(2)}) collective-permute-start(f32[2,8,128]{2,1,0:T(8,128)S(1)} %copy-done.1), channel_id=1, source_target_pairs={{0,16},{16,32},{32,48},{48,64},{64,80},{80,96},{96,112},{112,128},... | collective-permute-start | bytes 24584 | tf_op jit(solution)/shard_map/ppermute | solution.py:418
  36.0 8.0 %collective-permute-start.3 = (f32[2,8,128]{2,1,0:T(8,128)S(1)}, f32[2,8,128]{2,1,0:T(8,128)S(1)}, u32[]{:S(2)}, u32[]{:S(2)}) collective-permute-start(f32[2,8,128]{2,1,0:T(8,128)S(1)} %shard_map.52.own), channel_id=1, source_target_pairs={{16,32},{32,16},{48,64},{64,48},{80,96},{96,80},{112,128},{128,112... | collective-permute-start | bytes 24584 | tf_op jit(solution)/shard_map/ppermute | solution.py:430
  36.7 8.4 %collective-permute-start.2 = (f32[2,8,128]{2,1,0:T(8,128)S(1)}, f32[2,8,128]{2,1,0:T(8,128)S(1)}, u32[]{:S(2)}, u32[]{:S(2)}) collective-permute-start(f32[2,8,128]{2,1,0:T(8,128)S(1)} %shard_map.52.own), channel_id=1, source_target_pairs={{0,16},{16,0},{32,48},{48,32},{64,80},{80,64},{96,112},{112,96},{1... | collective-permute-start | bytes 24584 | tf_op jit(solution)/shard_map/ppermute | solution.py:430
  45.7 13.0 %all-to-all-start.1 = ((f32[16,2,8,128]{3,2,1,0:T(8,128)}), f32[16,2,8,128]{3,2,1,0:T(8,128)S(1)}, u32[]{:S(2)}, u32[]{:S(2)}) async-start(f32[16,2,8,128]{3,2,1,0:T(8,128)} %shard_map.53), calls=%async_computation.1 | async-start | bytes 262144 | tf_op jit(solution)/shard_map/all_to_all | solution.py:434

commit v9 on v8

--- a/solution.py
+++ b/solution.py
@@ -138,17 +138,15 @@
     return weight
 
 
-def pack(modes, design, out, sems):
+def pack(modes, design, out, upper, sems):
     planes, rows = modes.shape[1], modes.shape[3]
+    pieces = [(modes.at[0, c, 0], out, c * rows, rows) for c in range(planes)]
+    pieces += [(design.at[l], out, planes * rows + l * SUB, SUB) for l in (0, 1)]
+    pieces += [(modes.at[0, c, 1], upper, c * rows, rows) for c in range(planes)]
     copies = [
-        pltpu.make_async_copy(modes.at[0, c, 0], out.at[pl.ds(c * rows, rows)], sems.at[c])
-        for c in range(planes)
+        pltpu.make_async_copy(source, to.at[pl.ds(start, size)], sems.at[k])
+        for k, (source, to, start, size) in enumerate(pieces)
     ]
-    for l in (0, 1):
-        start = planes * rows + l * SUB
-        copies.append(
-            pltpu.make_async_copy(design.at[l], out.at[pl.ds(start, SUB)], sems.at[planes + l])
-        )
     for copy in copies:
         copy.start()
     for copy in copies:
@@ -160,13 +158,22 @@
     return packed[start : start + SUB]
 
 
-def first_layer(modes, eigen, packed, out, pairs):
+def plane_rows(packed, c, rows):
+    return packed[c * rows : (c + 1) * rows]
+
+
+def first_layer(packed, upper, eigen, out, pairs):
     def store(r, stiff, mass):
         out[r, 0] = stiff
         out[r, 1] = mass
 
     tiles = out.shape[0]
-    forms(lambda c, a: modes[0, c, a], eigen[0], store, pairs, tiles)
+    span = tiles * SUB
+
+    def load(c, a):
+        return plane_rows(upper if a else packed, c, span)
+
+    forms(load, eigen[0], store, pairs, tiles)
     design = tail_rows(packed, 0), tail_rows(packed, 1)
     for r in range(tiles):
         out[r, 4] = design[0]
@@ -187,7 +194,7 @@
     return jnp.concatenate(up, 0), jnp.concatenate(down, 0)
 
 
-def second_layer(modes, eigen, packed, got, before, _, out, rows, pairs, *, mode):
+def second_layer(packed, upper, eigen, got, before, _, out, rows, pairs, *, mode):
     def store(r, stiff, mass):
         out[r, 2] = stiff
         out[r, 3] = mass
@@ -196,7 +203,7 @@
     span = tiles * SUB
 
     def load(c, a):
-        return got[c * span : (c + 1) * span] if a else modes[0, c, 1]
+        return plane_rows(got if a else upper, c, span)
 
     m = lax.axis_index(mode)
     own = tail_rows(packed, 0), tail_rows(packed, 1)
@@ -444,12 +451,15 @@
     padded = (2, total_y + 2 * SUB, LANE)
     place = dict(slab=slab, mode=mode, sizes=sizes)
 
-    packed = pl.pallas_call(
+    packed, upper = pl.pallas_call(
         pack,
-        out_shape=jax.ShapeDtypeStruct((3 * total_y + 2 * SUB, LANE), F32),
+        out_shape=[
+            jax.ShapeDtypeStruct((3 * total_y + 2 * SUB, LANE), F32),
+            jax.ShapeDtypeStruct((3 * total_y, LANE), F32),
+        ],
         in_specs=[pl.BlockSpec(memory_space=pltpu.HBM)] * 2,
-        out_specs=VMEM,
-        scratch_shapes=[pltpu.SemaphoreType.DMA((5,))],
+        out_specs=[VMEM] * 2,
+        scratch_shapes=[pltpu.SemaphoreType.DMA((8,))],
         compiler_params=pltpu.CompilerParams(vmem_limit_bytes=GRANT),
         name="pack",
     )(
@@ -461,16 +471,16 @@
     sent = call(
         first_layer,
         [(modes, 7, SUB, LANE)],
-        [mode_shapes, eigenvalues, packed],
-        specs=[VMEM, SMEM, VMEM],
+        [packed, upper, eigenvalues],
+        specs=[VMEM, VMEM, SMEM],
         scratch=[pairs],
         flops=5_000_000,
     )
     sent, rows = call(
         functools.partial(second_layer, mode=mode),
         [(modes, 7, SUB, LANE), block],
-        [mode_shapes, eigenvalues, packed, got, before, sent],
-        specs=[VMEM, SMEM, VMEM, VMEM, VMEM, VMEM],
+        [packed, upper, eigenvalues, got, before, sent],
+        specs=[VMEM, VMEM, SMEM, VMEM, VMEM, VMEM],
         scratch=[pairs],
         flops=5_000_000,
         alias={5: 0},

time: 97.6 us -> 97.7 us (level)
  no operation moved by 1% of the time
where the time goes in v9:
time: 97.7 us; the launch traced here: 97.2 us
  blocking collectives  60.3 us (62%)
  starting transfers between devices  18.8 us (19%)
  waiting for transfers between devices  9.85 us (10%)
  Pallas kernels  6.87 us (7%)
  between operations  1.38 us (1%)
    all_to_all x3, blocking collectives, exchange(): return lax.all_to_all(value, axis, 0, 0, tiled=True)  60.3 us
    all_to_all x1, waiting for transfers between devices, exchange(): return lax.all_to_all(value, axis, 0, 0, tiled=True)  8.83 us
    ppermute x2, starting transfers between devices, swapped(): return lax.ppermute(value, axis, pairs)  7.99 us
    pallas_call x8, Pallas kernels, call(): pl.pallas_call(kernel, out_shape=outs[0] if single else outs, in_specs=sp...  5.77 us
    ppermute x1, starting transfers between devices, from_before(): return lax.ppermute(value, axis, [(i, i + 1) for i in range(count - 1)])  5.44 us
    all_to_all x1, starting transfers between devices, exchange(): return lax.all_to_all(value, axis, 0, 0, tiled=True)  4.08 us
  transfers between devices with their start and end apart: 5, of which 2 were waited for; matrix products, arithmetic and copies ran while one was open for 0% of the time, Pallas kernels for 1%

profile of v9, /device:TPU:1, one launch (start us, length us, event | category | flops | bytes accessed | tf_op | source)
XLA Modules:
  0.0 97.2 jit_solution(7103493551327342617)
XLA Ops:
  0.6 0.0 copy-start
  0.6 1.1 %pack.1 = (f32[400,128]{1,0:T(8,128)S(1)}, f32[384,128]{1,0:T(8,128)S(1)}) custom-call(f32[1,3,2,128,128]{4,3,2,1,0:T(8,128)} %modes.1, f32[2,8,128]{2,1,0:T(8,128)} %design.3), custom_call_target="tpu_custom_call" | custom-call | tf_op jit(solution)/shard_map/pack/pallas_call | solution.py:454
  1.8 1.3 %collective-permute-start = (f32[400,128]{1,0:T(8,128)S(1)}, f32[400,128]{1,0:T(8,128)S(1)}, u32[]{:S(2)}, u32[]{:S(2)}) collective-permute-start(f32[400,128]{1,0:T(8,128)S(1)} %get-tuple-element.15.packed), channel_id=1, source_target_pairs={{16,0},{32,16},{48,32},{64,48},{80,64},{96,80},{112,96},{128,112},... | collective-permute-start | bytes 614408 | tf_op jit(solution)/shard_map/ppermute | solution.py:430
  3.1 0.0 copy-done
  3.1 5.4 %collective-permute-start.1 = (f32[2,8,128]{2,1,0:T(8,128)S(1)}, f32[2,8,128]{2,1,0:T(8,128)S(1)}, u32[]{:S(2)}, u32[]{:S(2)}) collective-permute-start(f32[2,8,128]{2,1,0:T(8,128)S(1)} %copy-done), channel_id=1, source_target_pairs={{0,16},{16,32},{32,48},{48,64},{64,80},{80,96},{96,112},{112,128},... | collective-permute-start | bytes 24584 | tf_op jit(solution)/shard_map/ppermute | solution.py:425
  9.2 0.5 shard_map.50._
  9.7 0.0 collective-permute-done.1.before
  9.7 0.0 collective-permute-done.got
  9.7 0.6 shard_map.51
  10.3 25.6 %all_to_all.20.got.early = f32[16,7,8,128]{3,2,1,0:T(8,128)S(1)} all-to-all(f32[16,7,8,128]{3,2,1,0:T(8,128)S(1)} %get-tuple-element.17), channel_id=1, replica_groups=mesh['slab'=32,'mode'=16] {'mode'}, dimensions={0} | all-to-all | bytes 917504 | tf_op jit(solution)/shard_map/all_to_all | solution.py:441
  35.9 0.2 shard_map.52.own
  36.1 0.7 collective-permute-start.3
  36.8 7.3 %collective-permute-start.2 = (f32[2,8,128]{2,1,0:T(8,128)S(1)}, f32[2,8,128]{2,1,0:T(8,128)S(1)}, u32[]{:S(2)}, u32[]{:S(2)}) collective-permute-start(f32[2,8,128]{2,1,0:T(8,128)S(1)} %shard_map.52.own), channel_id=1, source_target_pairs={{0,16},{16,0},{32,48},{48,32},{64,80},{80,64},{96,112},{112,96},{1... | collective-permute-start | bytes 24584 | tf_op jit(solution)/shard_map/ppermute | solution.py:437
  44.1 0.0 collective-permute-done.3.odd
  44.1 1.0 %collective-permute-done.2.even = f32[2,8,128]{2,1,0:T(8,128)S(1)} collective-permute-done((f32[2,8,128]{2,1,0:T(8,128)S(1)}, f32[2,8,128]{2,1,0:T(8,128)S(1)}, u32[]{:S(2)}, u32[]{:S(2)}) %collective-permute-start.2) | collective-permute-done | bytes 8224 | tf_op jit(solution)/shard_map/ppermute | solution.py:437
  45.1 0.7 shard_map.53
  45.8 4.1 %all-to-all-start.1 = ((f32[16,2,8,128]{3,2,1,0:T(8,128)}), f32[16,2,8,128]{3,2,1,0:T(8,128)S(1)}, u32[]{:S(2)}, u32[]{:S(2)}) async-start(f32[16,2,8,128]{3,2,1,0:T(8,128)} %shard_map.53), calls=%async_computation.1 | async-start | bytes 262144 | tf_op jit(solution)/shard_map/all_to_all | solution.py:441
  49.9 0.1 shard_map.54
  49.9 8.8 %all-to-all-done.1.got = f32[16,2,8,128]{3,2,1,0:T(8,128)S(1)} async-done(((f32[16,2,8,128]{3,2,1,0:T(8,128)}), f32[16,2,8,128]{3,2,1,0:T(8,128)S(1)}, u32[]{:S(2)}, u32[]{:S(2)}) %all-to-all-start.1) | async-done | bytes 131104 | tf_op jit(solution)/shard_map/all_to_all | solution.py:441
  58.8 1.4 %shard_map.55 = (f32[32,8,128]{2,1,0:T(8,128)S(1)}, f32[2,8,128]{2,1,0:T(8,128)S(1)}, f32[32,1,128]{2,1,0:T(1,128)S(1)}) custom-call(f32[16,2,8,128]{3,2,1,0:T(8,128)S(1)} %all-to-all-done.1.got, f32[16,7,8,128]{3,2,1,0:T(8,128)S(1)} %all_to_all.20.got.early, f32[32,8,128]{2,1,0:T(8,128)S(1)} %get-tuple-element.19.least, ...), custom_call_target="tpu_custom_call" | custom-call | flops 1000 | bytes 1142784 | tf_op jit(solution)/shard_map/pallas_call | solution.py:411
  60.1 23.0 %all_to_all.21.got = f32[32,1,128]{2,1,0:T(1,128)S(1)} all-to-all(f32[32,1,128]{2,1,0:T(1,128)S(1)} %get-tuple-element.23), channel_id=1, replica_groups=mesh['slab'=32,'mode'=16] {'slab'}, dimensions={0} | all-to-all | bytes 32768 | tf_op jit(solution)/shard_map/all_to_all | solution.py:441
  83.1 1.6 %shard_map.56 = (f32[32,1,128]{2,1,0:T(1,128)S(1)}, f32[8,128]{1,0:T(8,128)S(1)}) custom-call(f32[32,1,128]{2,1,0:T(1,128)S(1)} %all_to_all.21.got, f32[32,8,128]{2,1,0:T(8,128)S(1)} %get-tuple-element.24.gain, f32[32,8,128]{2,1,0:T(8,128)S(1)} %get-tuple-element.19.least, f32[32,8,128]{2,1,0:T(8,128)S(1)} %get-tuple-element.20.most), custom_call_target="tpu_custom_call" | custom-call | flops 1000 | bytes 430080 | tf_op jit(solution)/shard_map/pallas_call | solution.py:411
  84.7 11.6 %all_to_all.22.got = f32[32,1,128]{2,1,0:T(1,128)S(1)} all-to-all(f32[32,1,128]{2,1,0:T(1,128)S(1)} %get-tuple-element.25), channel_id=1, replica_groups=mesh['slab'=32,'mode'=16] {'slab'}, dimensions={0} | all-to-all | bytes 32768 | tf_op jit(solution)/shard_map/all_to_all | solution.py:441
  96.4 0.8 shard_map.57
Async XLA Ops:
  0.6 2.4 %copy-start = (f32[2,8,128]{2,1,0:T(8,128)S(1)}, f32[2,8,128]{2,1,0:T(8,128)}, u32[]{:S(2)}) copy-start(f32[2,8,128]{2,1,0:T(8,128)} %design.3) | copy-start | bytes 24580
  1.8 8.0 %collective-permute-start = (f32[400,128]{1,0:T(8,128)S(1)}, f32[400,128]{1,0:T(8,128)S(1)}, u32[]{:S(2)}, u32[]{:S(2)}) collective-permute-start(f32[400,128]{1,0:T(8,128)S(1)} %get-tuple-element.15.packed), channel_id=1, source_target_pairs={{16,0},{32,16},{48,32},{64,48},{80,64},{96,80},{112,96},{128,112},... | collective-permute-start | bytes 614408 | tf_op jit(solution)/shard_map/ppermute | solution.py:430
  3.1 6.6 %collective-permute-start.1 = (f32[2,8,128]{2,1,0:T(8,128)S(1)}, f32[2,8,128]{2,1,0:T(8,128)S(1)}, u32[]{:S(2)}, u32[]{:S(2)}) collective-permute-start(f32[2,8,128]{2,1,0:T(8,128)S(1)} %copy-done), channel_id=1, source_target_pairs={{0,16},{16,32},{32,48},{48,64},{64,80},{80,96},{96,112},{112,128},... | collective-permute-start | bytes 24584 | tf_op jit(solution)/shard_map/ppermute | solution.py:425
  36.1 8.0 %collective-permute-start.3 = (f32[2,8,128]{2,1,0:T(8,128)S(1)}, f32[2,8,128]{2,1,0:T(8,128)S(1)}, u32[]{:S(2)}, u32[]{:S(2)}) collective-permute-start(f32[2,8,128]{2,1,0:T(8,128)S(1)} %shard_map.52.own), channel_id=1, source_target_pairs={{16,32},{32,16},{48,64},{64,48},{80,96},{96,80},{112,128},{128,112... | collective-permute-start | bytes 24584 | tf_op jit(solution)/shard_map/ppermute | solution.py:437
  36.8 8.4 %collective-permute-start.2 = (f32[2,8,128]{2,1,0:T(8,128)S(1)}, f32[2,8,128]{2,1,0:T(8,128)S(1)}, u32[]{:S(2)}, u32[]{:S(2)}) collective-permute-start(f32[2,8,128]{2,1,0:T(8,128)S(1)} %shard_map.52.own), channel_id=1, source_target_pairs={{0,16},{16,0},{32,48},{48,32},{64,80},{80,64},{96,112},{112,96},{1... | collective-permute-start | bytes 24584 | tf_op jit(solution)/shard_map/ppermute | solution.py:437
  45.8 13.0 %all-to-all-start.1 = ((f32[16,2,8,128]{3,2,1,0:T(8,128)}), f32[16,2,8,128]{3,2,1,0:T(8,128)S(1)}, u32[]{:S(2)}, u32[]{:S(2)}) async-start(f32[16,2,8,128]{3,2,1,0:T(8,128)} %shard_map.53), calls=%async_computation.1 | async-start | bytes 262144 | tf_op jit(solution)/shard_map/all_to_all | solution.py:441

commit v10 on v9

--- a/solution.py
+++ b/solution.py
@@ -138,15 +138,18 @@
     return weight
 
 
-def pack(modes, design, out, upper, sems):
+def fetch(pieces, sems):
+    return [
+        pltpu.make_async_copy(source, to.at[pl.ds(start, size)], sems.at[k])
+        for k, (source, to, start, size) in enumerate(pieces)
+    ]
+
+
+def pack(modes, design, out, sems):
     planes, rows = modes.shape[1], modes.shape[3]
     pieces = [(modes.at[0, c, 0], out, c * rows, rows) for c in range(planes)]
     pieces += [(design.at[l], out, planes * rows + l * SUB, SUB) for l in (0, 1)]
-    pieces += [(modes.at[0, c, 1], upper, c * rows, rows) for c in range(planes)]
-    copies = [
-        pltpu.make_async_copy(source, to.at[pl.ds(start, size)], sems.at[k])
-        for k, (source, to, start, size) in enumerate(pieces)
-    ]
+    copies = fetch(pieces, sems)
     for copy in copies:
         copy.start()
     for copy in copies:
@@ -162,7 +165,18 @@
     return packed[c * rows : (c + 1) * rows]
 
 
-def first_layer(packed, upper, eigen, out, pairs):
+def first_layer(modes, packed, eigen, out, upper, pairs, sems):
+    planes, rows = modes.shape[1], modes.shape[3]
+    copies = fetch([(modes.at[0, c, 1], upper, c * rows, rows) for c in range(planes)], sems)
+    for copy in copies:
+        copy.start()
+    design = tail_rows(packed, 0), tail_rows(packed, 1)
+    for r in range(out.shape[0]):
+        out[r, 4] = design[0]
+        out[r, 5] = design[1]
+    for copy in copies:
+        copy.wait()
+
     def store(r, stiff, mass):
         out[r, 0] = stiff
         out[r, 1] = mass
@@ -174,10 +188,6 @@
         return plane_rows(upper if a else packed, c, span)
 
     forms(load, eigen[0], store, pairs, tiles)
-    design = tail_rows(packed, 0), tail_rows(packed, 1)
-    for r in range(tiles):
-        out[r, 4] = design[0]
-        out[r, 5] = design[1]
 
 
 def shifted_rows(v, o):
@@ -303,7 +313,8 @@
 def lane_totals(parts):
     column = jnp.sum(parts[...], axis=1, keepdims=True)
     shape = (FAN, LANE)
-    spread = jnp.where(iota(shape, 0) == iota(shape, 1), jnp.broadcast_to(column, shape), 0.0)
+    mine = iota(shape, 0) == jnp.minimum(iota(shape, 1), FAN - 1)
+    spread = jnp.where(mine, jnp.broadcast_to(column, shape), 0.0)
     return jnp.sum(spread, axis=0, keepdims=True)
 
 
@@ -356,14 +367,10 @@
 
 
 def added(got):
-    total = got[0]
-    for k in range(1, got.shape[0]):
-        total = total + got[k]
-    return total
-
-
-def at_lane(row, k):
-    return jnp.sum(jnp.where(iota(row.shape, 1) == k, row, 0.0), axis=1, keepdims=True)
+    rows = [got[k] for k in range(got.shape[0])]
+    while len(rows) > 1:
+        rows = [a + b for a, b in zip(rows[::2], rows[1::2])] + rows[len(rows) & ~1 :]
+    return rows[0]
 
 
 def cells_above(row, goal):
@@ -373,10 +380,10 @@
 
 def second_round(got, gain, least, most, out, state, parts):
     row = added(got)
-    goal = at_lane(row, FAN - 1)
+    goal = pltpu.roll(row, LANE - FAN, 1)
     low = LEVEL_LOW + COARSE * cells_above(row, goal)
     state[0:1] = jnp.broadcast_to(low, (1, LANE))
-    state[1:2] = jnp.broadcast_to(goal, (1, LANE))
+    state[1:2] = goal
     scale = jnp.exp(-0.5 * jnp.broadcast_to(low, (SUB, LANE)))
     levels = [scale * float(np.exp(-0.5 * FINE * (i + 1))) for i in range(FAN - 1)]
     volumes(levels, gain, least, most, parts)
@@ -390,7 +397,7 @@
     total_x, total_y, total_z = sizes
     m = lax.axis_index(mode)
     row = added(got)
-    goal = state[1:2, 0:1]
+    goal = state[1:2]
     level = state[0:1, 0:1] + FINE * (cells_above(row, goal) + 0.5)
     scale = jnp.exp(jnp.broadcast_to(level, (SUB, LANE)))
     y = along(m * SUB + iota((SUB, LANE), 0), total_y, edge_tables(total_y)[1])
@@ -451,31 +458,33 @@
     padded = (2, total_y + 2 * SUB, LANE)
     place = dict(slab=slab, mode=mode, sizes=sizes)
 
-    packed, upper = pl.pallas_call(
+    held = pltpu.with_memory_space_constraint(mode_shapes, pltpu.HBM)
+    params = pltpu.CompilerParams(vmem_limit_bytes=GRANT)
+    hbm = pl.BlockSpec(memory_space=pltpu.HBM)
+    packed = pl.pallas_call(
         pack,
+        out_shape=jax.ShapeDtypeStruct((3 * total_y + 2 * SUB, LANE), F32),
+        in_specs=[hbm, hbm],
+        out_specs=VMEM,
+        scratch_shapes=[pltpu.SemaphoreType.DMA((5,))],
+        compiler_params=params,
+        name="pack",
+    )(held, pltpu.with_memory_space_constraint(design, pltpu.HBM))
+    got = from_after(packed, slab)
+    before = from_before(design, slab)
+    sent, upper = pl.pallas_call(
+        first_layer,
         out_shape=[
-            jax.ShapeDtypeStruct((3 * total_y + 2 * SUB, LANE), F32),
+            jax.ShapeDtypeStruct((modes, 7, SUB, LANE), F32),
             jax.ShapeDtypeStruct((3 * total_y, LANE), F32),
         ],
-        in_specs=[pl.BlockSpec(memory_space=pltpu.HBM)] * 2,
-        out_specs=[VMEM] * 2,
-        scratch_shapes=[pltpu.SemaphoreType.DMA((8,))],
-        compiler_params=pltpu.CompilerParams(vmem_limit_bytes=GRANT),
-        name="pack",
-    )(
-        pltpu.with_memory_space_constraint(mode_shapes, pltpu.HBM),
-        pltpu.with_memory_space_constraint(design, pltpu.HBM),
-    )
-    got = from_after(packed, slab)
-    before = from_before(design, slab)
-    sent = call(
-        first_layer,
-        [(modes, 7, SUB, LANE)],
-        [packed, upper, eigenvalues],
-        specs=[VMEM, VMEM, SMEM],
-        scratch=[pairs],
-        flops=5_000_000,
-    )
+        in_specs=[hbm, VMEM, SMEM],
+        out_specs=[VMEM, VMEM],
+        scratch_shapes=[pltpu.VMEM(pairs, F32), pltpu.SemaphoreType.DMA((3,))],
+        cost_estimate=pl.CostEstimate(flops=5_000_000, bytes_accessed=600_000, transcendentals=0),
+        compiler_params=params,
+        name="first_layer",
+    )(held, packed, eigenvalues)
     sent, rows = call(
         functools.partial(second_layer, mode=mode),
         [(modes, 7, SUB, LANE), block],

time: 97.7 us -> 97.5 us (level)
    pallas_call x1 -> x2, Pallas kernels: 1.1 us -> 2.41 us  [the longest x1 1.45 us: local(): pl.pallas_call(first_layer, out_shape=[jax.ShapeDtypeStruct((modes, 7, SU...]
    pallas_call x8 -> x7, Pallas kernels: 5.77 us -> 5.15 us  [call(): pl.pallas_call(kernel, out_shape=outs[0] if single else outs, in_specs=sp...]
  transfers between devices with their start and end apart: 5 -> 5, of which waited for: 2 -> 2; matrix products, arithmetic and copies ran while one was open for 0% -> 0% of each run, Pallas kernels for 1% -> 2%
where the time goes in v10:
time: 97.5 us; the launch traced here: 97 us
  blocking collectives  59.4 us (61%)
  starting transfers between devices  18.8 us (19%)
  waiting for transfers between devices  9.85 us (10%)
  Pallas kernels  7.56 us (8%)
  between operations  1.38 us (1%)
    all_to_all x3, blocking collectives, exchange(): return lax.all_to_all(value, axis, 0, 0, tiled=True)  59.4 us
    all_to_all x1, waiting for transfers between devices, exchange(): return lax.all_to_all(value, axis, 0, 0, tiled=True)  8.83 us
    ppermute x2, starting transfers between devices, swapped(): return lax.ppermute(value, axis, pairs)  7.99 us
    ppermute x1, starting transfers between devices, from_before(): return lax.ppermute(value, axis, [(i, i + 1) for i in range(count - 1)])  5.44 us
    pallas_call x7, Pallas kernels, call(): pl.pallas_call(kernel, out_shape=outs[0] if single else outs, in_specs=sp...  5.15 us
    all_to_all x1, starting transfers between devices, exchange(): return lax.all_to_all(value, axis, 0, 0, tiled=True)  4.08 us
  transfers between devices with their start and end apart: 5, of which 2 were waited for; matrix products, arithmetic and copies ran while one was open for 0% of the time, Pallas kernels for 2%

profile of v10, /device:TPU:1, one launch (start us, length us, event | category | flops | bytes accessed | tf_op | source)
XLA Modules:
  0.0 97.0 jit_solution(1127678207236116916)
XLA Ops:
  0.6 0.0 copy-start
  0.6 1.0 pack.1.packed
  1.6 1.3 %collective-permute-start = (f32[400,128]{1,0:T(8,128)S(1)}, f32[400,128]{1,0:T(8,128)S(1)}, u32[]{:S(2)}, u32[]{:S(2)}) collective-permute-start(f32[400,128]{1,0:T(8,128)S(1)} %pack.1.packed), channel_id=1, source_target_pairs={{16,0},{32,16},{48,32},{64,48},{80,64},{96,80},{112,96},{128,112},... | collective-permute-start | bytes 614408 | tf_op jit(solution)/shard_map/ppermute | solution.py:437
  2.9 0.0 copy-done
  2.9 5.4 %collective-permute-start.1 = (f32[2,8,128]{2,1,0:T(8,128)S(1)}, f32[2,8,128]{2,1,0:T(8,128)S(1)}, u32[]{:S(2)}, u32[]{:S(2)}) collective-permute-start(f32[2,8,128]{2,1,0:T(8,128)S(1)} %copy-done), channel_id=1, source_target_pairs={{0,16},{16,32},{32,48},{48,64},{64,80},{80,96},{96,112},{112,128},... | collective-permute-start | bytes 24584 | tf_op jit(solution)/shard_map/ppermute | solution.py:432
  9.0 1.5 %first_layer.1 = (f32[16,7,8,128]{3,2,1,0:T(8,128)S(1)}, f32[384,128]{1,0:T(8,128)S(1)}) custom-call(f32[1,3,2,128,128]{4,3,2,1,0:T(8,128)} %modes.3, f32[400,128]{1,0:T(8,128)S(1)} %pack.1.packed, f32[1]{0:T(128)S(6)} %copy.7.eigen), custom_call_target="tpu_custom_call" | custom-call | flops 5000000 | bytes 600000 | tf_op jit(solution)/shard_map/first_layer/pallas_call | solution.py:475
  10.5 0.0 collective-permute-done.1.before
  10.5 0.0 collective-permute-done.got
  10.5 0.6 shard_map.50
  11.1 24.7 %all_to_all.20.got.early = f32[16,7,8,128]{3,2,1,0:T(8,128)S(1)} all-to-all(f32[16,7,8,128]{3,2,1,0:T(8,128)S(1)} %get-tuple-element.17), channel_id=1, replica_groups=mesh['slab'=32,'mode'=16] {'mode'}, dimensions={0} | all-to-all | bytes 917504 | tf_op jit(solution)/shard_map/all_to_all | solution.py:448
  35.8 0.2 shard_map.51.own
  36.0 0.7 collective-permute-start.3
  36.6 7.3 %collective-permute-start.2 = (f32[2,8,128]{2,1,0:T(8,128)S(1)}, f32[2,8,128]{2,1,0:T(8,128)S(1)}, u32[]{:S(2)}, u32[]{:S(2)}) collective-permute-start(f32[2,8,128]{2,1,0:T(8,128)S(1)} %shard_map.51.own), channel_id=1, source_target_pairs={{0,16},{16,0},{32,48},{48,32},{64,80},{80,64},{96,112},{112,96},{1... | collective-permute-start | bytes 24584 | tf_op jit(solution)/shard_map/ppermute | solution.py:444
  44.0 0.0 collective-permute-done.3.odd
  44.0 1.0 %collective-permute-done.2.even = f32[2,8,128]{2,1,0:T(8,128)S(1)} collective-permute-done((f32[2,8,128]{2,1,0:T(8,128)S(1)}, f32[2,8,128]{2,1,0:T(8,128)S(1)}, u32[]{:S(2)}, u32[]{:S(2)}) %collective-permute-start.2) | collective-permute-done | bytes 8224 | tf_op jit(solution)/shard_map/ppermute | solution.py:444
  45.0 0.7 shard_map.52
  45.6 4.1 %all-to-all-start.1 = ((f32[16,2,8,128]{3,2,1,0:T(8,128)}), f32[16,2,8,128]{3,2,1,0:T(8,128)S(1)}, u32[]{:S(2)}, u32[]{:S(2)}) async-start(f32[16,2,8,128]{3,2,1,0:T(8,128)} %shard_map.52), calls=%async_computation.1 | async-start | bytes 262144 | tf_op jit(solution)/shard_map/all_to_all | solution.py:448
  49.7 0.1 shard_map.53
  49.8 8.8 %all-to-all-done.1.got = f32[16,2,8,128]{3,2,1,0:T(8,128)S(1)} async-done(((f32[16,2,8,128]{3,2,1,0:T(8,128)}), f32[16,2,8,128]{3,2,1,0:T(8,128)S(1)}, u32[]{:S(2)}, u32[]{:S(2)}) %all-to-all-start.1) | async-done | bytes 131104 | tf_op jit(solution)/shard_map/all_to_all | solution.py:448
  58.6 1.4 %shard_map.54 = (f32[32,8,128]{2,1,0:T(8,128)S(1)}, f32[2,8,128]{2,1,0:T(8,128)S(1)}, f32[32,1,128]{2,1,0:T(1,128)S(1)}) custom-call(f32[16,2,8,128]{3,2,1,0:T(8,128)S(1)} %all-to-all-done.1.got, f32[16,7,8,128]{3,2,1,0:T(8,128)S(1)} %all_to_all.20.got.early, f32[32,8,128]{2,1,0:T(8,128)S(1)} %get-tuple-element.19.least, ...), custom_call_target="tpu_custom_call" | custom-call | flops 1000 | bytes 1142784 | tf_op jit(solution)/shard_map/pallas_call | solution.py:418
  60.0 23.0 %all_to_all.21.got = f32[32,1,128]{2,1,0:T(1,128)S(1)} all-to-all(f32[32,1,128]{2,1,0:T(1,128)S(1)} %get-tuple-element.23), channel_id=1, replica_groups=mesh['slab'=32,'mode'=16] {'slab'}, dimensions={0} | all-to-all | bytes 32768 | tf_op jit(solution)/shard_map/all_to_all | solution.py:448
  83.0 1.6 %shard_map.55 = (f32[32,1,128]{2,1,0:T(1,128)S(1)}, f32[8,128]{1,0:T(8,128)S(1)}) custom-call(f32[32,1,128]{2,1,0:T(1,128)S(1)} %all_to_all.21.got, f32[32,8,128]{2,1,0:T(8,128)S(1)} %get-tuple-element.24.gain, f32[32,8,128]{2,1,0:T(8,128)S(1)} %get-tuple-element.19.least, f32[32,8,128]{2,1,0:T(8,128)S(1)} %get-tuple-element.20.most), custom_call_target="tpu_custom_call" | custom-call | flops 1000 | bytes 430080 | tf_op jit(solution)/shard_map/pallas_call | solution.py:418
  84.6 11.6 %all_to_all.22.got = f32[32,1,128]{2,1,0:T(1,128)S(1)} all-to-all(f32[32,1,128]{2,1,0:T(1,128)S(1)} %get-tuple-element.25), channel_id=1, replica_groups=mesh['slab'=32,'mode'=16] {'slab'}, dimensions={0} | all-to-all | bytes 32768 | tf_op jit(solution)/shard_map/all_to_all | solution.py:448
  96.2 0.8 shard_map.56
Async XLA Ops:
  0.6 2.3 %copy-start = (f32[2,8,128]{2,1,0:T(8,128)S(1)}, f32[2,8,128]{2,1,0:T(8,128)}, u32[]{:S(2)}) copy-start(f32[2,8,128]{2,1,0:T(8,128)} %design.3) | copy-start | bytes 24580
  1.6 8.9 %collective-permute-start = (f32[400,128]{1,0:T(8,128)S(1)}, f32[400,128]{1,0:T(8,128)S(1)}, u32[]{:S(2)}, u32[]{:S(2)}) collective-permute-start(f32[400,128]{1,0:T(8,128)S(1)} %pack.1.packed), channel_id=1, source_target_pairs={{16,0},{32,16},{48,32},{64,48},{80,64},{96,80},{112,96},{128,112},... | collective-permute-start | bytes 614408 | tf_op jit(solution)/shard_map/ppermute | solution.py:437
  2.9 7.6 %collective-permute-start.1 = (f32[2,8,128]{2,1,0:T(8,128)S(1)}, f32[2,8,128]{2,1,0:T(8,128)S(1)}, u32[]{:S(2)}, u32[]{:S(2)}) collective-permute-start(f32[2,8,128]{2,1,0:T(8,128)S(1)} %copy-done), channel_id=1, source_target_pairs={{0,16},{16,32},{32,48},{48,64},{64,80},{80,96},{96,112},{112,128},... | collective-permute-start | bytes 24584 | tf_op jit(solution)/shard_map/ppermute | solution.py:432
  36.0 8.0 %collective-permute-start.3 = (f32[2,8,128]{2,1,0:T(8,128)S(1)}, f32[2,8,128]{2,1,0:T(8,128)S(1)}, u32[]{:S(2)}, u32[]{:S(2)}) collective-permute-start(f32[2,8,128]{2,1,0:T(8,128)S(1)} %shard_map.51.own), channel_id=1, source_target_pairs={{16,32},{32,16},{48,64},{64,48},{80,96},{96,80},{112,128},{128,112... | collective-permute-start | bytes 24584 | tf_op jit(solution)/shard_map/ppermute | solution.py:444
  36.6 8.4 %collective-permute-start.2 = (f32[2,8,128]{2,1,0:T(8,128)S(1)}, f32[2,8,128]{2,1,0:T(8,128)S(1)}, u32[]{:S(2)}, u32[]{:S(2)}) collective-permute-start(f32[2,8,128]{2,1,0:T(8,128)S(1)} %shard_map.51.own), channel_id=1, source_target_pairs={{0,16},{16,0},{32,48},{48,32},{64,80},{80,64},{96,112},{112,96},{1... | collective-permute-start | bytes 24584 | tf_op jit(solution)/shard_map/ppermute | solution.py:444
  45.6 13.0 %all-to-all-start.1 = ((f32[16,2,8,128]{3,2,1,0:T(8,128)}), f32[16,2,8,128]{3,2,1,0:T(8,128)S(1)}, u32[]{:S(2)}, u32[]{:S(2)}) async-start(f32[16,2,8,128]{3,2,1,0:T(8,128)} %shard_map.52), calls=%async_computation.1 | async-start | bytes 262144 | tf_op jit(solution)/shard_map/all_to_all | solution.py:448

commit v11 on v10

--- a/solution.py
+++ b/solution.py
@@ -170,10 +170,6 @@
     copies = fetch([(modes.at[0, c, 1], upper, c * rows, rows) for c in range(planes)], sems)
     for copy in copies:
         copy.start()
-    design = tail_rows(packed, 0), tail_rows(packed, 1)
-    for r in range(out.shape[0]):
-        out[r, 4] = design[0]
-        out[r, 5] = design[1]
     for copy in copies:
         copy.wait()
 
@@ -225,8 +221,8 @@
     weight = forms(load, eigen[0], store, pairs, tiles)
     half = SUB // 2
     for r in range(tiles):
-        out[r, 6, :half] = jnp.where(m + 1 == r, up, weight[:half])
-        out[r, 6, half:] = jnp.where(m - 1 == r, down, weight[half:])
+        out[r, 4, :half] = jnp.where(m + 1 == r, up, weight[:half])
+        out[r, 4, half:] = jnp.where(m - 1 == r, down, weight[half:])
 
 
 def across_x(own, before, after):
@@ -251,11 +247,11 @@
     half = SUB // 2
     weight = None
     for r in range(tiles):
-        w = jnp.where(m - 1 == r, got[r, 6, half : half + 1], got[r, 6, :1])
+        w = jnp.where(m - 1 == r, got[r, 4, half : half + 1], got[r, 4, :1])
         weight = w if weight is None else weight + w
     inverse_weight = 1.0 / jnp.broadcast_to(weight, (SUB, LANE))
-    from_last = jnp.where(m > 0, got[jnp.maximum(m - 1, 0), 6, :half], 0.0)
-    from_next = jnp.where(m < tiles - 1, got[jnp.minimum(m + 1, tiles - 1), 6, half:], 0.0)
+    from_last = jnp.where(m > 0, got[jnp.maximum(m - 1, 0), 4, :half], 0.0)
+    from_next = jnp.where(m < tiles - 1, got[jnp.minimum(m + 1, tiles - 1), 4, half:], 0.0)
     inverse_yz = along(m * SUB + iota((SUB, LANE), 0), total_y, edge_tables(total_y)[0]) * along(
         iota((SUB, LANE), 1), total_z, edge_tables(total_z)[0]
     )
@@ -274,7 +270,7 @@
         out[l] = tent_lanes((slope * stiff[l] - mass[l]) * inverse_weight * inverse)
 
 
-def gradient_copies(own, even, odd, out, *, slab):
+def gradient_copies(own, even, odd, packed, out, *, slab):
     is_even = lax.rem(lax.axis_index(slab), 2) == 0
     before = [jnp.where(is_even, odd[l], even[l]) for l in (0, 1)]
     after = [jnp.where(is_even, even[l], odd[l]) for l in (0, 1)]
@@ -282,6 +278,8 @@
     for r in range(out.shape[0]):
         out[r, 0] = pair[0]
         out[r, 1] = pair[1]
+        out[r, 2] = tail_rows(packed, 0)
+        out[r, 3] = tail_rows(packed, 1)
 
 
 def measure_xz(slab, total_x, total_z):
@@ -327,7 +325,7 @@
         y = along(r * SUB + iota((SUB, LANE), 0), total_y, edge_tables(total_y)[1])
         for l in (0, 1):
             measure = xz[l] * y
-            design = early[r, 4 + l]
+            design = early[r, 2 + l]
             at = l * tiles + r
             least[at] = jnp.maximum(design - MOVE_LIMIT, 0.0) * measure
             most[at] = jnp.minimum(design + MOVE_LIMIT, 1.0) * measure
@@ -336,7 +334,7 @@
     goals[0:1] = jnp.sum(goal, axis=0, keepdims=True)
 
 
-def first_round(got, early, least, most, goals, measures, gain, own, out, padded, parts, *, mode):
+def first_round(got, least, most, goals, measures, gain, own, out, padded, parts, *, mode):
     tiles = got.shape[0]
     m = lax.axis_index(mode)
     for l in (0, 1):
@@ -352,7 +350,7 @@
                 t = float(FR - abs(o)) * padded[l, start : start + SUB]
                 total = t if total is None else total + t
             at = l * tiles + r
-            gain[at] = early[r, 4 + l] * jnp.sqrt(jnp.maximum(total, 0.0) * measures[at])
+            gain[at] = got[r, 2 + l] * jnp.sqrt(jnp.maximum(total, 0.0) * measures[at])
         total = None
         for o in range(1 - FR, FR):
             t = float(FR - abs(o)) * padded[l, pl.ds(m * SUB + SUB + o, SUB)]
@@ -475,7 +473,7 @@
     sent, upper = pl.pallas_call(
         first_layer,
         out_shape=[
-            jax.ShapeDtypeStruct((modes, 7, SUB, LANE), F32),
+            jax.ShapeDtypeStruct((modes, 5, SUB, LANE), F32),
             jax.ShapeDtypeStruct((3 * total_y, LANE), F32),
         ],
         in_specs=[hbm, VMEM, SMEM],
@@ -487,7 +485,7 @@
     )(held, packed, eigenvalues)
     sent, rows = call(
         functools.partial(second_layer, mode=mode),
-        [(modes, 7, SUB, LANE), block],
+        [(modes, 5, SUB, LANE), block],
         [packed, upper, eigenvalues, got, before, sent],
         specs=[VMEM, VMEM, SMEM, VMEM, VMEM, VMEM],
         scratch=[pairs],
@@ -499,20 +497,22 @@
     even = swapped(gradient, slab, 0)
     odd = swapped(gradient, slab, 1)
     copies = call(
-        functools.partial(gradient_copies, slab=slab), [(modes, *block)], [gradient, even, odd]
+        functools.partial(gradient_copies, slab=slab),
+        [(modes, 4, SUB, LANE)],
+        [gradient, even, odd, packed],
     )
     whole = exchange(copies, mode)
     vectors = (2 * modes, SUB, LANE)
     least, most, goals, measures = call(
         functools.partial(bounds, slab=slab, sizes=sizes),
         [vectors, vectors, (SUB, LANE), vectors],
-        [early],
+        [whole],
         flops=100_000,
     )
     gain, own, sent = call(
         functools.partial(first_round, mode=mode),
         [vectors, block, (slabs, 1, LANE)],
-        [whole, early, least, most, goals, measures],
+        [whole, least, most, goals, measures],
         scratch=[padded, (FAN, LANE)],
     )
     got = exchange(sent, slab)

time: 97.5 us -> 96.5 us (0.990)
  blocking collectives: 59.4 us -> 71.7 us
  waiting for transfers between devices: 9.85 us -> 1.35 us
  starting transfers between devices: 18.8 us -> 14.7 us
    all_to_all x3 -> x4, blocking collectives: 59.4 us -> 71.7 us  [exchange(): return lax.all_to_all(value, axis, 0, 0, tiled=True)]
    all_to_all x1 -> x0, waiting for transfers between devices: 8.83 us -> none  [exchange(): return lax.all_to_all(value, axis, 0, 0, tiled=True)]
    all_to_all x1 -> x0, starting transfers between devices: 4.08 us -> none  [exchange(): return lax.all_to_all(value, axis, 0, 0, tiled=True)]
  transfers between devices with their start and end apart: 5 -> 4, of which waited for: 2 -> 1; matrix products, arithmetic and copies ran while one was open for 0% -> 0% of each run, Pallas kernels for 2% -> 2%
where the time goes in v11:
time: 96.5 us; the launch traced here: 96.1 us
  blocking collectives  71.7 us (74%)
  starting transfers between devices  14.7 us (15%)
  Pallas kernels  6.95 us (7%)
  between operations  1.38 us (1%)
  waiting for transfers between devices  1.35 us (1%)
    all_to_all x4, blocking collectives, exchange(): return lax.all_to_all(value, axis, 0, 0, tiled=True)  71.7 us
    ppermute x2, starting transfers between devices, swapped(): return lax.ppermute(value, axis, pairs)  7.99 us
    ppermute x1, starting transfers between devices, from_before(): return lax.ppermute(value, axis, [(i, i + 1) for i in range(count - 1)])  5.44 us
    pallas_call x7, Pallas kernels, call(): pl.pallas_call(kernel, out_shape=outs[0] if single else outs, in_specs=sp...  4.54 us
  transfers between devices with their start and end apart: 4, of which 1 were waited for; matrix products, arithmetic and copies ran while one was open for 0% of the time, Pallas kernels for 2%

profile of v11, /device:TPU:1, one launch (start us, length us, event | category | flops | bytes accessed | tf_op | source)
XLA Modules:
  0.0 96.1 jit_solution(1361640411925935801)
XLA Ops:
  0.6 0.0 copy-start
  0.6 1.0 pack.1.packed
  1.6 1.3 %collective-permute-start = (f32[400,128]{1,0:T(8,128)S(1)}, f32[400,128]{1,0:T(8,128)S(1)}, u32[]{:S(2)}, u32[]{:S(2)}) collective-permute-start(f32[400,128]{1,0:T(8,128)S(1)} %pack.1.packed), channel_id=1, source_target_pairs={{16,0},{32,16},{48,32},{64,48},{80,64},{96,80},{112,96},{128,112},... | collective-permute-start | bytes 614408 | tf_op jit(solution)/shard_map/ppermute | solution.py:435
  2.9 0.0 copy-done
  2.9 5.4 %collective-permute-start.1 = (f32[2,8,128]{2,1,0:T(8,128)S(1)}, f32[2,8,128]{2,1,0:T(8,128)S(1)}, u32[]{:S(2)}, u32[]{:S(2)}) collective-permute-start(f32[2,8,128]{2,1,0:T(8,128)S(1)} %copy-done), channel_id=1, source_target_pairs={{0,16},{16,32},{32,48},{48,64},{64,80},{80,96},{96,112},{112,128},... | collective-permute-start | bytes 24584 | tf_op jit(solution)/shard_map/ppermute | solution.py:430
  9.0 1.5 %first_layer.1 = (f32[16,5,8,128]{3,2,1,0:T(8,128)S(1)}, f32[384,128]{1,0:T(8,128)S(1)}) custom-call(f32[1,3,2,128,128]{4,3,2,1,0:T(8,128)} %modes.3, f32[400,128]{1,0:T(8,128)S(1)} %pack.1.packed, f32[1]{0:T(128)S(6)} %copy.7.eigen), custom_call_target="tpu_custom_call" | custom-call | flops 5000000 | bytes 600000 | tf_op jit(solution)/shard_map/first_layer/pallas_call | solution.py:473
  10.5 0.0 collective-permute-done.1.before
  10.5 0.0 collective-permute-done.got
  10.5 0.6 shard_map.50
  11.1 21.8 %all_to_all.20.got = f32[16,5,8,128]{3,2,1,0:T(8,128)S(1)} all-to-all(f32[16,5,8,128]{3,2,1,0:T(8,128)S(1)} %get-tuple-element.17), channel_id=1, replica_groups=mesh['slab'=32,'mode'=16] {'mode'}, dimensions={0} | all-to-all | bytes 655360 | tf_op jit(solution)/shard_map/all_to_all | solution.py:446
  32.9 0.2 shard_map.51.own
  33.1 0.7 collective-permute-start.3
  33.7 7.3 %collective-permute-start.2 = (f32[2,8,128]{2,1,0:T(8,128)S(1)}, f32[2,8,128]{2,1,0:T(8,128)S(1)}, u32[]{:S(2)}, u32[]{:S(2)}) collective-permute-start(f32[2,8,128]{2,1,0:T(8,128)S(1)} %shard_map.51.own), channel_id=1, source_target_pairs={{0,16},{16,0},{32,48},{48,32},{64,80},{80,64},{96,112},{112,96},{1... | collective-permute-start | bytes 24584 | tf_op jit(solution)/shard_map/ppermute | solution.py:442
  41.1 0.0 collective-permute-done.3.odd
  41.1 1.3 %collective-permute-done.2.even = f32[2,8,128]{2,1,0:T(8,128)S(1)} collective-permute-done((f32[2,8,128]{2,1,0:T(8,128)S(1)}, f32[2,8,128]{2,1,0:T(8,128)S(1)}, u32[]{:S(2)}, u32[]{:S(2)}) %collective-permute-start.2) | collective-permute-done | bytes 8224 | tf_op jit(solution)/shard_map/ppermute | solution.py:442
  42.5 15.2 %all_to_all.21.early.got = f32[16,4,8,128]{3,2,1,0:T(8,128)S(1)} all-to-all(f32[16,4,8,128]{3,2,1,0:T(8,128)S(1)} %shard_map.52), channel_id=1, replica_groups=mesh['slab'=32,'mode'=16] {'mode'}, dimensions={0} | all-to-all | bytes 524288 | tf_op jit(solution)/shard_map/all_to_all | solution.py:446
  57.7 0.1 shard_map.53
  57.7 1.4 %shard_map.54 = (f32[32,8,128]{2,1,0:T(8,128)S(1)}, f32[2,8,128]{2,1,0:T(8,128)S(1)}, f32[32,1,128]{2,1,0:T(1,128)S(1)}) custom-call(f32[16,4,8,128]{3,2,1,0:T(8,128)S(1)} %all_to_all.21.early.got, f32[32,8,128]{2,1,0:T(8,128)S(1)} %get-tuple-element.19.least, f32[32,8,128]{2,1,0:T(8,128)S(1)} %get-tuple-element.20.most, ...), custom_call_target="tpu_custom_call" | custom-call | flops 1000 | bytes 815104 | tf_op jit(solution)/shard_map/pallas_call | solution.py:416
  59.1 23.0 %all_to_all.22.got = f32[32,1,128]{2,1,0:T(1,128)S(1)} all-to-all(f32[32,1,128]{2,1,0:T(1,128)S(1)} %get-tuple-element.23), channel_id=1, replica_groups=mesh['slab'=32,'mode'=16] {'slab'}, dimensions={0} | all-to-all | bytes 32768 | tf_op jit(solution)/shard_map/all_to_all | solution.py:446
  82.1 1.6 %shard_map.55 = (f32[32,1,128]{2,1,0:T(1,128)S(1)}, f32[8,128]{1,0:T(8,128)S(1)}) custom-call(f32[32,1,128]{2,1,0:T(1,128)S(1)} %all_to_all.22.got, f32[32,8,128]{2,1,0:T(8,128)S(1)} %get-tuple-element.24.gain, f32[32,8,128]{2,1,0:T(8,128)S(1)} %get-tuple-element.19.least, f32[32,8,128]{2,1,0:T(8,128)S(1)} %get-tuple-element.20.most), custom_call_target="tpu_custom_call" | custom-call | flops 1000 | bytes 430080 | tf_op jit(solution)/shard_map/pallas_call | solution.py:416
  83.7 11.6 %all_to_all.23.got = f32[32,1,128]{2,1,0:T(1,128)S(1)} all-to-all(f32[32,1,128]{2,1,0:T(1,128)S(1)} %get-tuple-element.25), channel_id=1, replica_groups=mesh['slab'=32,'mode'=16] {'slab'}, dimensions={0} | all-to-all | bytes 32768 | tf_op jit(solution)/shard_map/all_to_all | solution.py:446
  95.3 0.8 shard_map.56
  (1 shorter events, 0.0 us)
Async XLA Ops:
  0.6 2.3 %copy-start = (f32[2,8,128]{2,1,0:T(8,128)S(1)}, f32[2,8,128]{2,1,0:T(8,128)}, u32[]{:S(2)}) copy-start(f32[2,8,128]{2,1,0:T(8,128)} %design.3) | copy-start | bytes 24580
  1.6 8.9 %collective-permute-start = (f32[400,128]{1,0:T(8,128)S(1)}, f32[400,128]{1,0:T(8,128)S(1)}, u32[]{:S(2)}, u32[]{:S(2)}) collective-permute-start(f32[400,128]{1,0:T(8,128)S(1)} %pack.1.packed), channel_id=1, source_target_pairs={{16,0},{32,16},{48,32},{64,48},{80,64},{96,80},{112,96},{128,112},... | collective-permute-start | bytes 614408 | tf_op jit(solution)/shard_map/ppermute | solution.py:435
  2.9 7.6 %collective-permute-start.1 = (f32[2,8,128]{2,1,0:T(8,128)S(1)}, f32[2,8,128]{2,1,0:T(8,128)S(1)}, u32[]{:S(2)}, u32[]{:S(2)}) collective-permute-start(f32[2,8,128]{2,1,0:T(8,128)S(1)} %copy-done), channel_id=1, source_target_pairs={{0,16},{16,32},{32,48},{48,64},{64,80},{80,96},{96,112},{112,128},... | collective-permute-start | bytes 24584 | tf_op jit(solution)/shard_map/ppermute | solution.py:430
  33.1 8.0 %collective-permute-start.3 = (f32[2,8,128]{2,1,0:T(8,128)S(1)}, f32[2,8,128]{2,1,0:T(8,128)S(1)}, u32[]{:S(2)}, u32[]{:S(2)}) collective-permute-start(f32[2,8,128]{2,1,0:T(8,128)S(1)} %shard_map.51.own), channel_id=1, source_target_pairs={{16,32},{32,16},{48,64},{64,48},{80,96},{96,80},{112,128},{128,112... | collective-permute-start | bytes 24584 | tf_op jit(solution)/shard_map/ppermute | solution.py:442
  33.7 8.7 %collective-permute-start.2 = (f32[2,8,128]{2,1,0:T(8,128)S(1)}, f32[2,8,128]{2,1,0:T(8,128)S(1)}, u32[]{:S(2)}, u32[]{:S(2)}) collective-permute-start(f32[2,8,128]{2,1,0:T(8,128)S(1)} %shard_map.51.own), channel_id=1, source_target_pairs={{0,16},{16,0},{32,48},{48,32},{64,80},{80,64},{96,112},{112,96},{1... | collective-permute-start | bytes 24584 | tf_op jit(solution)/shard_map/ppermute | solution.py:442

commit v12 on v11

--- a/solution.py
+++ b/solution.py
@@ -6,6 +6,7 @@
 from jax import lax
 from jax.experimental import pallas as pl
 from jax.experimental.pallas import tpu as pltpu
+from jax.sharding import Mesh
 from jax.sharding import PartitionSpec as P
 
 
@@ -45,6 +46,10 @@
         if abs(table[k] - middle) > 1e-12:
             value = jnp.where((position == k) | (position == n - 1 - k), F32(table[k]), value)
     return value
+
+
+def mode_index():
+    return 2 * lax.axis_index("row") + lax.axis_index("core")
 
 
 def iota(shape, axis):
@@ -211,7 +216,7 @@
     def load(c, a):
         return plane_rows(got if a else upper, c, span)
 
-    m = lax.axis_index(mode)
+    m = mode_index()
     own = tail_rows(packed, 0), tail_rows(packed, 1)
     after = tail_rows(got, 0), tail_rows(got, 1)
     pair = across_x(own, before, after)
@@ -240,7 +245,7 @@
 
 def own_gradient(got, rows, out, *, slab, mode, sizes):
     total_x, total_y, total_z = sizes
-    s, m = lax.axis_index(slab), lax.axis_index(mode)
+    s, m = lax.axis_index(slab), mode_index()
     stiff = (over_modes(got, 0), over_modes(got, 2))
     mass = (over_modes(got, 1), over_modes(got, 3))
     tiles = got.shape[0]
@@ -276,10 +281,8 @@
     after = [jnp.where(is_even, even[l], odd[l]) for l in (0, 1)]
     pair = across_x(own, before, after)
     for r in range(out.shape[0]):
-        out[r, 0] = pair[0]
-        out[r, 1] = pair[1]
-        out[r, 2] = tail_rows(packed, 0)
-        out[r, 3] = tail_rows(packed, 1)
+        out[r, 0] = pair[r % 2]
+        out[r, 1] = tail_rows(packed, r % 2)
 
 
 def measure_xz(slab, total_x, total_z):
@@ -316,46 +319,43 @@
     return jnp.sum(spread, axis=0, keepdims=True)
 
 
-def bounds(early, least, most, goals, measures, *, slab, sizes):
+def bounds(whole, least, most, goals, measures, *, sizes):
     total_x, total_y, total_z = sizes
-    tiles = early.shape[0]
-    xz = measure_xz(slab, total_x, total_z)
+    x = 2 * lax.axis_index("slab") + lax.axis_index("core")
+    xz = along(jnp.full((SUB, LANE), x, jnp.int32), total_x, edge_tables(total_x)[1])
+    xz = xz * along(iota((SUB, LANE), 1), total_z, edge_tables(total_z)[1])
     goal = jnp.zeros((SUB, LANE), F32)
+    for r in range(whole.shape[0]):
+        y = along(r * SUB + iota((SUB, LANE), 0), total_y, edge_tables(total_y)[1])
+        measure = xz * y
+        design = whole[r, 1]
+        least[r] = jnp.maximum(design - MOVE_LIMIT, 0.0) * measure
+        most[r] = jnp.minimum(design + MOVE_LIMIT, 1.0) * measure
+        measures[r] = measure
+        goal = goal + design * measure
+    goals[0:1] = jnp.sum(goal, axis=0, keepdims=True)
+
+
+def across_y(padded, start):
+    total = None
+    for o in range(1 - FR, FR):
+        t = float(FR - abs(o)) * padded[pl.ds(start + o, SUB)]
+        total = t if total is None else total + t
+    return total
+
+
+def first_round(got, least, most, goals, measures, gain, own, other, out, padded, parts):
+    tiles = got.shape[0]
+    padded[:SUB] = jnp.zeros((SUB, LANE), F32)
+    padded[(tiles + 1) * SUB :] = jnp.zeros((SUB, LANE), F32)
     for r in range(tiles):
-        y = along(r * SUB + iota((SUB, LANE), 0), total_y, edge_tables(total_y)[1])
-        for l in (0, 1):
-            measure = xz[l] * y
-            design = early[r, 2 + l]
-            at = l * tiles + r
-            least[at] = jnp.maximum(design - MOVE_LIMIT, 0.0) * measure
-            most[at] = jnp.minimum(design + MOVE_LIMIT, 1.0) * measure
-            measures[at] = measure
-            goal = goal + design * measure
-    goals[0:1] = jnp.sum(goal, axis=0, keepdims=True)
-
-
-def first_round(got, least, most, goals, measures, gain, own, out, padded, parts, *, mode):
-    tiles = got.shape[0]
-    m = lax.axis_index(mode)
-    for l in (0, 1):
-        padded[l, :SUB] = jnp.zeros((SUB, LANE), F32)
-        padded[l, (tiles + 1) * SUB :] = jnp.zeros((SUB, LANE), F32)
-        for r in range(tiles):
-            padded[l, (r + 1) * SUB : (r + 2) * SUB] = got[r, l]
-    for l in (0, 1):
-        for r in range(tiles):
-            total = None
-            for o in range(1 - FR, FR):
-                start = (r + 1) * SUB + o
-                t = float(FR - abs(o)) * padded[l, start : start + SUB]
-                total = t if total is None else total + t
-            at = l * tiles + r
-            gain[at] = got[r, 2 + l] * jnp.sqrt(jnp.maximum(total, 0.0) * measures[at])
-        total = None
-        for o in range(1 - FR, FR):
-            t = float(FR - abs(o)) * padded[l, pl.ds(m * SUB + SUB + o, SUB)]
-            total = t if total is None else total + t
-        own[l] = total
+        padded[(r + 1) * SUB : (r + 2) * SUB] = got[r, 0]
+    for r in range(tiles):
+        total = across_y(padded, (r + 1) * SUB)
+        gain[r] = got[r, 1] * jnp.sqrt(jnp.maximum(total, 0.0) * measures[r])
+    m = mode_index()
+    own[...] = across_y(padded, (m + 1) * SUB)
+    other[...] = across_y(padded, (m + 2 - 2 * lax.axis_index("core")) * SUB)
     levels = [float(np.exp(-0.5 * (LEVEL_LOW + COARSE * (i + 1)))) for i in range(FAN - 1)]
     volumes(levels, gain, least, most, parts)
     parts[FAN - 1 : FAN] = goals[0:1]
@@ -391,9 +391,9 @@
         out[k] = row
 
 
-def last_update(got, state, own, design, sens_out, out, *, slab, mode, sizes):
+def last_update(got, state, own, other, design, sens_out, out, *, slab, mode, sizes):
     total_x, total_y, total_z = sizes
-    m = lax.axis_index(mode)
+    m = mode_index()
     row = added(got)
     goal = state[1:2]
     level = state[0:1, 0:1] + FINE * (cells_above(row, goal) + 0.5)
@@ -401,7 +401,8 @@
     y = along(m * SUB + iota((SUB, LANE), 0), total_y, edge_tables(total_y)[1])
     xz = measure_xz(slab, total_x, total_z)
     for l in (0, 1):
-        d, s = design[l], own[l]
+        d = design[l]
+        s = jnp.where(lax.axis_index("core") == l, own[...], other[...])
         factor = jnp.sqrt(jnp.maximum(s, 0.0) / (scale * (xz[l] * y)))
         least = jnp.maximum(d - MOVE_LIMIT, 0.0)
         most = jnp.minimum(d + MOVE_LIMIT, 1.0)
@@ -447,13 +448,13 @@
 
 
 def local(design, mode_shapes, eigenvalues):
-    slab, mode = "slab", "mode"
+    slab, mode = "slab", ("row", "core")
     slabs, modes = lax.axis_size(slab), lax.axis_size(mode)
     _, _, _, total_y, total_z = mode_shapes.shape
     sizes = (2 * slabs, total_y, total_z)
     pairs = (3, 2, 2, total_y + SUB, LANE)
     block = (2, SUB, LANE)
-    padded = (2, total_y + 2 * SUB, LANE)
+    padded = (total_y + 2 * SUB, LANE)
     place = dict(slab=slab, mode=mode, sizes=sizes)
 
     held = pltpu.with_memory_space_constraint(mode_shapes, pltpu.HBM)
@@ -498,39 +499,43 @@
     odd = swapped(gradient, slab, 1)
     copies = call(
         functools.partial(gradient_copies, slab=slab),
-        [(modes, 4, SUB, LANE)],
+        [(modes, 2, SUB, LANE)],
         [gradient, even, odd, packed],
     )
     whole = exchange(copies, mode)
-    vectors = (2 * modes, SUB, LANE)
+    vectors = (modes, SUB, LANE)
+    peers = (2 * slabs, 1, LANE)
     least, most, goals, measures = call(
-        functools.partial(bounds, slab=slab, sizes=sizes),
+        functools.partial(bounds, sizes=sizes),
         [vectors, vectors, (SUB, LANE), vectors],
         [whole],
         flops=100_000,
     )
-    gain, own, sent = call(
-        functools.partial(first_round, mode=mode),
-        [vectors, block, (slabs, 1, LANE)],
+    gain, own, other, sent = call(
+        first_round,
+        [vectors, (SUB, LANE), (SUB, LANE), peers],
         [whole, least, most, goals, measures],
         scratch=[padded, (FAN, LANE)],
     )
-    got = exchange(sent, slab)
+    other = lax.ppermute(other, "core", [(0, 1), (1, 0)])
+    got = exchange(sent, (slab, "core"))
     sent, state = call(
-        second_round,
-        [(slabs, 1, LANE), (SUB, LANE)],
-        [got, gain, least, most],
-        scratch=[(FAN, LANE)],
-    )
-    got = exchange(sent, slab)
-    return call(functools.partial(last_update, **place), [block, block], [got, state, own, design])
+        second_round, [peers, (SUB, LANE)], [got, gain, least, most], scratch=[(FAN, LANE)]
+    )
+    got = exchange(sent, (slab, "core"))
+    return call(
+        functools.partial(last_update, **place), [block, block], [got, state, own, other, design]
+    )
 
 
 def solution(mesh):
-    in_specs = (P("slab", "mode", None), P("mode", None, "slab", None, None), P("mode"))
-    out_specs = (P("slab", "mode", None), P("slab", "mode", None))
+    slabs, modes = mesh.devices.shape
+    split = Mesh(mesh.devices.reshape(slabs, modes // 2, 2), ("slab", "row", "core"))
+    mode = ("row", "core")
+    in_specs = (P("slab", mode, None), P(mode, None, "slab", None, None), P(mode))
+    out_specs = (P("slab", mode, None), P("slab", mode, None))
 
     def step(design, mode_shapes, eigenvalues):
         return tuple(local(design, mode_shapes, eigenvalues))
 
-    return jax.shard_map(step, mesh=mesh, in_specs=in_specs, out_specs=out_specs, check_vma=False)
+    return jax.shard_map(step, mesh=split, in_specs=in_specs, out_specs=out_specs, check_vma=False)

time: 96.5 us -> 96.8 us (level)
  blocking collectives: 71.7 us -> 58.5 us
  starting transfers between devices: 14.7 us -> 21.9 us
  waiting for transfers between devices: 1.35 us -> 8.3 us
    all_to_all x4 -> x3, blocking collectives: 71.7 us -> 58.5 us  [exchange(): return lax.all_to_all(value, axis, 0, 0, tiled=True)]
    all_to_all x0 -> x1, waiting for transfers between devices: none -> 6.15 us  [exchange(): return lax.all_to_all(value, axis, 0, 0, tiled=True)]
    all_to_all x0 -> x1, starting transfers between devices: none -> 4.65 us  [exchange(): return lax.all_to_all(value, axis, 0, 0, tiled=True)]
    ppermute x0 -> x1, starting transfers between devices: none -> 2.48 us  [local(): other = lax.ppermute(other, 'core', [(0, 1), (1, 0)])]
  transfers between devices with their start and end apart: 4 -> 6, of which waited for: 1 -> 3; matrix products, arithmetic and copies ran while one was open for 0% -> 0% of each run, Pallas kernels for 2% -> 2%
where the time goes in v12:
time: 96.8 us; the launch traced here: 96.3 us
  blocking collectives  58.5 us (60%)
  starting transfers between devices  21.9 us (23%)
  waiting for transfers between devices  8.3 us (9%)
  Pallas kernels  6.21 us (6%)
  between operations  1.4 us (1%)
    all_to_all x3, blocking collectives, exchange(): return lax.all_to_all(value, axis, 0, 0, tiled=True)  58.5 us
    ppermute x2, starting transfers between devices, swapped(): return lax.ppermute(value, axis, pairs)  7.99 us
    all_to_all x1, waiting for transfers between devices, exchange(): return lax.all_to_all(value, axis, 0, 0, tiled=True)  6.15 us
    ppermute x1, starting transfers between devices, from_before(): return lax.ppermute(value, axis, [(i, i + 1) for i in range(count - 1)])  5.44 us
    all_to_all x1, starting transfers between devices, exchange(): return lax.all_to_all(value, axis, 0, 0, tiled=True)  4.65 us
    pallas_call x7, Pallas kernels, call(): pl.pallas_call(kernel, out_shape=outs[0] if single else outs, in_specs=sp...  3.8 us
    ppermute x1, starting transfers between devices, local(): other = lax.ppermute(other, 'core', [(0, 1), (1, 0)])  2.48 us
  transfers between devices with their start and end apart: 6, of which 3 were waited for; matrix products, arithmetic and copies ran while one was open for 0% of the time, Pallas kernels for 2%

profile of v12, /device:TPU:1, one launch (start us, length us, event | category | flops | bytes accessed | tf_op | source)
XLA Modules:
  0.0 96.3 jit_solution(18338773339218744279)
XLA Ops:
  0.6 0.0 copy-start
  0.6 1.0 pack.1.packed
  1.6 1.3 %collective-permute-start = (f32[400,128]{1,0:T(8,128)S(1)}, f32[400,128]{1,0:T(8,128)S(1)}, u32[]{:S(2)}, u32[]{:S(2)}) collective-permute-start(f32[400,128]{1,0:T(8,128)S(1)} %pack.1.packed), channel_id=1, source_target_pairs={{16,0},{32,16},{48,32},{64,48},{80,64},{96,80},{112,96},{128,112},... | collective-permute-start | bytes 614408 | tf_op jit(solution)/shard_map/ppermute | solution.py:436
  2.9 0.0 copy-done
  2.9 5.4 %collective-permute-start.1 = (f32[2,8,128]{2,1,0:T(8,128)S(1)}, f32[2,8,128]{2,1,0:T(8,128)S(1)}, u32[]{:S(2)}, u32[]{:S(2)}) collective-permute-start(f32[2,8,128]{2,1,0:T(8,128)S(1)} %copy-done), channel_id=1, source_target_pairs={{0,16},{16,32},{32,48},{48,64},{64,80},{80,96},{96,112},{112,128},... | collective-permute-start | bytes 24584 | tf_op jit(solution)/shard_map/ppermute | solution.py:431
  9.0 1.5 %first_layer.1 = (f32[16,5,8,128]{3,2,1,0:T(8,128)S(1)}, f32[384,128]{1,0:T(8,128)S(1)}) custom-call(f32[1,3,2,128,128]{4,3,2,1,0:T(8,128)} %modes.3, f32[400,128]{1,0:T(8,128)S(1)} %pack.1.packed, f32[1]{0:T(128)S(6)} %copy.7.eigen), custom_call_target="tpu_custom_call" | custom-call | flops 5000000 | bytes 600000 | tf_op jit(solution)/shard_map/first_layer/pallas_call | solution.py:474
  10.5 0.0 collective-permute-done.1.before
  10.5 0.0 collective-permute-done.got
  10.5 0.6 shard_map.50
  11.1 21.8 %all_to_all.20.got = f32[16,5,8,128]{3,2,1,0:T(8,128)S(1)} all-to-all(f32[16,5,8,128]{3,2,1,0:T(8,128)S(1)} %get-tuple-element.18), channel_id=1, replica_groups=mesh['slab'=32,'row'=8,'core'=2] {'row','core'}, dimensions={0} | all-to-all | bytes 655360 | tf_op jit(solution)/shard_map/all_to_all | solution.py:447
  32.9 0.2 shard_map.51.own
  33.1 0.7 collective-permute-start.3
  33.7 7.3 %collective-permute-start.2 = (f32[2,8,128]{2,1,0:T(8,128)S(1)}, f32[2,8,128]{2,1,0:T(8,128)S(1)}, u32[]{:S(2)}, u32[]{:S(2)}) collective-permute-start(f32[2,8,128]{2,1,0:T(8,128)S(1)} %shard_map.51.own), channel_id=1, source_target_pairs={{0,16},{16,0},{32,48},{48,32},{64,80},{80,64},{96,112},{112,96},{1... | collective-permute-start | bytes 24584 | tf_op jit(solution)/shard_map/ppermute | solution.py:443
  41.1 0.0 collective-permute-done.3.odd
  41.1 1.3 %collective-permute-done.2.even = f32[2,8,128]{2,1,0:T(8,128)S(1)} collective-permute-done((f32[2,8,128]{2,1,0:T(8,128)S(1)}, f32[2,8,128]{2,1,0:T(8,128)S(1)}, u32[]{:S(2)}, u32[]{:S(2)}) %collective-permute-start.2) | collective-permute-done | bytes 8224 | tf_op jit(solution)/shard_map/ppermute | solution.py:443
  42.5 12.5 %all_to_all.21.whole.got = f32[16,2,8,128]{3,2,1,0:T(8,128)S(1)} all-to-all(f32[16,2,8,128]{3,2,1,0:T(8,128)S(1)} %shard_map.52), channel_id=1, replica_groups=mesh['slab'=32,'row'=8,'core'=2] {'row','core'}, dimensions={0} | all-to-all | bytes 262144 | tf_op jit(solution)/shard_map/all_to_all | solution.py:447
  55.0 0.8 shard_map.54
  55.8 24.2 %all_to_all.22.got = f32[64,1,128]{2,1,0:T(1,128)S(1)} all-to-all(f32[64,1,128]{2,1,0:T(1,128)S(1)} %get-tuple-element.24), channel_id=1, replica_groups=mesh['slab'=32,'row'=8,'core'=2] {'slab','core'}, dimensions={0} | all-to-all | bytes 65536 | tf_op jit(solution)/shard_map/all_to_all | solution.py:447
  80.0 1.5 %shard_map.55 = (f32[64,1,128]{2,1,0:T(1,128)}, f32[8,128]{1,0:T(8,128)S(1)}) custom-call(f32[64,1,128]{2,1,0:T(1,128)S(1)} %all_to_all.22.got, f32[16,8,128]{2,1,0:T(8,128)S(1)} %get-tuple-element.25.gain, f32[16,8,128]{2,1,0:T(8,128)S(1)} %get-tuple-element.20.least, f32[16,8,128]{2,1,0:T(8,128)S(1)} %get-tuple-element.21.most), custom_call_target="tpu_custom_call" | custom-call | flops 1000 | bytes 266240 | tf_op jit(solution)/shard_map/pallas_call | solution.py:417
  81.4 4.7 %all-to-all-start.3 = ((f32[64,1,128]{2,1,0:T(1,128)}), f32[64,1,128]{2,1,0:T(1,128)S(1)}, u32[]{:S(2)}, u32[]{:S(2)}) async-start(f32[64,1,128]{2,1,0:T(1,128)} %get-tuple-element.26), calls=%async_computation.3 | async-start | bytes 65536 | tf_op jit(solution)/shard_map/all_to_all | solution.py:447
  86.1 2.5 %collective-permute-start.4 = (f32[8,128]{1,0:T(8,128)S(1)}, f32[8,128]{1,0:T(8,128)S(1)}, u32[]{:S(2)}, u32[]{:S(2)}) collective-permute-start(f32[8,128]{1,0:T(8,128)S(1)} %get-tuple-element.29), channel_id=1, source_target_pairs={{0,1},{1,0},{2,3},{3,2},{4,5},{5,4},{6,7},{7,6},{8,9},{9,8},{10,11... | collective-permute-start | bytes 12296 | tf_op jit(solution)/shard_map/ppermute | solution.py:520
  88.6 0.8 collective-permute-done.4.other
  89.4 6.1 %all-to-all-done.3.got = f32[64,1,128]{2,1,0:T(1,128)S(1)} async-done(((f32[64,1,128]{2,1,0:T(1,128)}), f32[64,1,128]{2,1,0:T(1,128)S(1)}, u32[]{:S(2)}, u32[]{:S(2)}) %all-to-all-start.3) | async-done | bytes 32800 | tf_op jit(solution)/shard_map/all_to_all | solution.py:447
  95.5 0.8 shard_map.56
  (2 shorter events, 0.1 us)
Async XLA Ops:
  0.6 2.3 %copy-start = (f32[2,8,128]{2,1,0:T(8,128)S(1)}, f32[2,8,128]{2,1,0:T(8,128)}, u32[]{:S(2)}) copy-start(f32[2,8,128]{2,1,0:T(8,128)} %design.3) | copy-start | bytes 24580
  1.6 8.9 %collective-permute-start = (f32[400,128]{1,0:T(8,128)S(1)}, f32[400,128]{1,0:T(8,128)S(1)}, u32[]{:S(2)}, u32[]{:S(2)}) collective-permute-start(f32[400,128]{1,0:T(8,128)S(1)} %pack.1.packed), channel_id=1, source_target_pairs={{16,0},{32,16},{48,32},{64,48},{80,64},{96,80},{112,96},{128,112},... | collective-permute-start | bytes 614408 | tf_op jit(solution)/shard_map/ppermute | solution.py:436
  2.9 7.6 %collective-permute-start.1 = (f32[2,8,128]{2,1,0:T(8,128)S(1)}, f32[2,8,128]{2,1,0:T(8,128)S(1)}, u32[]{:S(2)}, u32[]{:S(2)}) collective-permute-start(f32[2,8,128]{2,1,0:T(8,128)S(1)} %copy-done), channel_id=1, source_target_pairs={{0,16},{16,32},{32,48},{48,64},{64,80},{80,96},{96,112},{112,128},... | collective-permute-start | bytes 24584 | tf_op jit(solution)/shard_map/ppermute | solution.py:431
  33.1 8.0 %collective-permute-start.3 = (f32[2,8,128]{2,1,0:T(8,128)S(1)}, f32[2,8,128]{2,1,0:T(8,128)S(1)}, u32[]{:S(2)}, u32[]{:S(2)}) collective-permute-start(f32[2,8,128]{2,1,0:T(8,128)S(1)} %shard_map.51.own), channel_id=1, source_target_pairs={{16,32},{32,16},{48,64},{64,48},{80,96},{96,80},{112,128},{128,112... | collective-permute-start | bytes 24584 | tf_op jit(solution)/shard_map/ppermute | solution.py:443
  33.7 8.7 %collective-permute-start.2 = (f32[2,8,128]{2,1,0:T(8,128)S(1)}, f32[2,8,128]{2,1,0:T(8,128)S(1)}, u32[]{:S(2)}, u32[]{:S(2)}) collective-permute-start(f32[2,8,128]{2,1,0:T(8,128)S(1)} %shard_map.51.own), channel_id=1, source_target_pairs={{0,16},{16,0},{32,48},{48,32},{64,80},{80,64},{96,112},{112,96},{1... | collective-permute-start | bytes 24584 | tf_op jit(solution)/shard_map/ppermute | solution.py:443
  81.4 14.1 %all-to-all-start.3 = ((f32[64,1,128]{2,1,0:T(1,128)}), f32[64,1,128]{2,1,0:T(1,128)S(1)}, u32[]{:S(2)}, u32[]{:S(2)}) async-start(f32[64,1,128]{2,1,0:T(1,128)} %get-tuple-element.26), calls=%async_computation.3 | async-start | bytes 65536 | tf_op jit(solution)/shard_map/all_to_all | solution.py:447
  86.1 3.3 %collective-permute-start.4 = (f32[8,128]{1,0:T(8,128)S(1)}, f32[8,128]{1,0:T(8,128)S(1)}, u32[]{:S(2)}, u32[]{:S(2)}) collective-permute-start(f32[8,128]{1,0:T(8,128)S(1)} %get-tuple-element.29), channel_id=1, source_target_pairs={{0,1},{1,0},{2,3},{3,2},{4,5},{5,4},{6,7},{7,6},{8,9},{9,8},{10,11... | collective-permute-start | bytes 12296 | tf_op jit(solution)/shard_map/ppermute | solution.py:520

commit v13 on v11

--- a/solution.py
+++ b/solution.py
@@ -303,7 +303,7 @@
             )
 
         zeros = tuple(jnp.zeros((SUB, LANE), F32) for _ in chunk)
-        totals = lax.fori_loop(0, count, body, zeros, unroll=16)
+        totals = lax.fori_loop(0, count, body, zeros, unroll=32)
         for i, t in enumerate(totals):
             parts[start + i : start + i + 1] = jnp.sum(t, axis=0, keepdims=True)
 
@@ -316,27 +316,12 @@
     return jnp.sum(spread, axis=0, keepdims=True)
 
 
-def bounds(early, least, most, goals, measures, *, slab, sizes):
+def first_round(got, gain, least, most, own, out, padded, parts, *, slab, mode, sizes):
     total_x, total_y, total_z = sizes
-    tiles = early.shape[0]
+    tiles = got.shape[0]
+    m = lax.axis_index(mode)
     xz = measure_xz(slab, total_x, total_z)
     goal = jnp.zeros((SUB, LANE), F32)
-    for r in range(tiles):
-        y = along(r * SUB + iota((SUB, LANE), 0), total_y, edge_tables(total_y)[1])
-        for l in (0, 1):
-            measure = xz[l] * y
-            design = early[r, 2 + l]
-            at = l * tiles + r
-            least[at] = jnp.maximum(design - MOVE_LIMIT, 0.0) * measure
-            most[at] = jnp.minimum(design + MOVE_LIMIT, 1.0) * measure
-            measures[at] = measure
-            goal = goal + design * measure
-    goals[0:1] = jnp.sum(goal, axis=0, keepdims=True)
-
-
-def first_round(got, least, most, goals, measures, gain, own, out, padded, parts, *, mode):
-    tiles = got.shape[0]
-    m = lax.axis_index(mode)
     for l in (0, 1):
         padded[l, :SUB] = jnp.zeros((SUB, LANE), F32)
         padded[l, (tiles + 1) * SUB :] = jnp.zeros((SUB, LANE), F32)
@@ -349,8 +334,14 @@
                 start = (r + 1) * SUB + o
                 t = float(FR - abs(o)) * padded[l, start : start + SUB]
                 total = t if total is None else total + t
+            y = along(r * SUB + iota((SUB, LANE), 0), total_y, edge_tables(total_y)[1])
+            measure = xz[l] * y
+            design = got[r, 2 + l]
             at = l * tiles + r
-            gain[at] = got[r, 2 + l] * jnp.sqrt(jnp.maximum(total, 0.0) * measures[at])
+            gain[at] = design * jnp.sqrt(jnp.maximum(total, 0.0) * measure)
+            least[at] = jnp.maximum(design - MOVE_LIMIT, 0.0) * measure
+            most[at] = jnp.minimum(design + MOVE_LIMIT, 1.0) * measure
+            goal = goal + design * measure
         total = None
         for o in range(1 - FR, FR):
             t = float(FR - abs(o)) * padded[l, pl.ds(m * SUB + SUB + o, SUB)]
@@ -358,7 +349,7 @@
         own[l] = total
     levels = [float(np.exp(-0.5 * (LEVEL_LOW + COARSE * (i + 1)))) for i in range(FAN - 1)]
     volumes(levels, gain, least, most, parts)
-    parts[FAN - 1 : FAN] = goals[0:1]
+    parts[FAN - 1 : FAN] = jnp.sum(goal, axis=0, keepdims=True)
     row = lane_totals(parts)
     for k in range(out.shape[0]):
         out[k] = row
@@ -503,16 +494,10 @@
     )
     whole = exchange(copies, mode)
     vectors = (2 * modes, SUB, LANE)
-    least, most, goals, measures = call(
-        functools.partial(bounds, slab=slab, sizes=sizes),
-        [vectors, vectors, (SUB, LANE), vectors],
+    gain, least, most, own, sent = call(
+        functools.partial(first_round, **place),
+        [vectors, vectors, vectors, block, (slabs, 1, LANE)],
         [whole],
-        flops=100_000,
-    )
-    gain, own, sent = call(
-        functools.partial(first_round, mode=mode),
-        [vectors, block, (slabs, 1, LANE)],
-        [whole, least, most, goals, measures],
         scratch=[padded, (FAN, LANE)],
     )
     got = exchange(sent, slab)

time: 96.5 us -> 96.2 us (level)
    pallas_call x7 -> x6, Pallas kernels: 4.54 us -> 4.24 us  [call(): pl.pallas_call(kernel, out_shape=outs[0] if single else outs, in_specs=sp...]
where the time goes in v13:
time: 96.2 us; the launch traced here: 95.8 us
  blocking collectives  71.7 us (75%)
  starting transfers between devices  14.7 us (15%)
  Pallas kernels  6.64 us (7%)
  between operations  1.39 us (1%)
  waiting for transfers between devices  1.35 us (1%)
    all_to_all x4, blocking collectives, exchange(): return lax.all_to_all(value, axis, 0, 0, tiled=True)  71.7 us
    ppermute x2, starting transfers between devices, swapped(): return lax.ppermute(value, axis, pairs)  7.99 us
    ppermute x1, starting transfers between devices, from_before(): return lax.ppermute(value, axis, [(i, i + 1) for i in range(count - 1)])  5.44 us
    pallas_call x6, Pallas kernels, call(): pl.pallas_call(kernel, out_shape=outs[0] if single else outs, in_specs=sp...  4.24 us
  transfers between devices with their start and end apart: 4, of which 1 were waited for; matrix products, arithmetic and copies ran while one was open for 0% of the time, Pallas kernels for 2%

profile of v13, /device:TPU:1, one launch (start us, length us, event | category | flops | bytes accessed | tf_op | source)
XLA Modules:
  0.0 95.8 jit_solution(435159883015289923)
XLA Ops:
  0.6 0.0 copy-start
  0.6 1.0 pack.1.packed
  1.6 1.3 %collective-permute-start = (f32[400,128]{1,0:T(8,128)S(1)}, f32[400,128]{1,0:T(8,128)S(1)}, u32[]{:S(2)}, u32[]{:S(2)}) collective-permute-start(f32[400,128]{1,0:T(8,128)S(1)} %pack.1.packed), channel_id=1, source_target_pairs={{16,0},{32,16},{48,32},{64,48},{80,64},{96,80},{112,96},{128,112},... | collective-permute-start | bytes 614408 | tf_op jit(solution)/shard_map/ppermute | solution.py:426
  2.9 0.0 copy-done
  2.9 5.4 %collective-permute-start.1 = (f32[2,8,128]{2,1,0:T(8,128)S(1)}, f32[2,8,128]{2,1,0:T(8,128)S(1)}, u32[]{:S(2)}, u32[]{:S(2)}) collective-permute-start(f32[2,8,128]{2,1,0:T(8,128)S(1)} %copy-done), channel_id=1, source_target_pairs={{0,16},{16,32},{32,48},{48,64},{64,80},{80,96},{96,112},{112,128},... | collective-permute-start | bytes 24584 | tf_op jit(solution)/shard_map/ppermute | solution.py:421
  9.0 1.5 %first_layer.1 = (f32[16,5,8,128]{3,2,1,0:T(8,128)S(1)}, f32[384,128]{1,0:T(8,128)S(1)}) custom-call(f32[1,3,2,128,128]{4,3,2,1,0:T(8,128)} %modes.3, f32[400,128]{1,0:T(8,128)S(1)} %pack.1.packed, f32[1]{0:T(128)S(6)} %copy.7.eigen), custom_call_target="tpu_custom_call" | custom-call | flops 5000000 | bytes 600000 | tf_op jit(solution)/shard_map/first_layer/pallas_call | solution.py:464
  10.5 0.0 collective-permute-done.1.before
  10.5 0.0 collective-permute-done.got
  10.5 0.6 shard_map.50
  11.1 21.8 %all_to_all.20.got = f32[16,5,8,128]{3,2,1,0:T(8,128)S(1)} all-to-all(f32[16,5,8,128]{3,2,1,0:T(8,128)S(1)} %get-tuple-element.15), channel_id=1, replica_groups=mesh['slab'=32,'mode'=16] {'mode'}, dimensions={0} | all-to-all | bytes 655360 | tf_op jit(solution)/shard_map/all_to_all | solution.py:437
  32.9 0.2 shard_map.51.own
  33.1 0.7 collective-permute-start.3
  33.7 7.3 %collective-permute-start.2 = (f32[2,8,128]{2,1,0:T(8,128)S(1)}, f32[2,8,128]{2,1,0:T(8,128)S(1)}, u32[]{:S(2)}, u32[]{:S(2)}) collective-permute-start(f32[2,8,128]{2,1,0:T(8,128)S(1)} %shard_map.51.own), channel_id=1, source_target_pairs={{0,16},{16,0},{32,48},{48,32},{64,80},{80,64},{96,112},{112,96},{1... | collective-permute-start | bytes 24584 | tf_op jit(solution)/shard_map/ppermute | solution.py:433
  41.1 0.0 collective-permute-done.3.odd
  41.1 1.3 %collective-permute-done.2.even = f32[2,8,128]{2,1,0:T(8,128)S(1)} collective-permute-done((f32[2,8,128]{2,1,0:T(8,128)S(1)}, f32[2,8,128]{2,1,0:T(8,128)S(1)}, u32[]{:S(2)}, u32[]{:S(2)}) %collective-permute-start.2) | collective-permute-done | bytes 8224 | tf_op jit(solution)/shard_map/ppermute | solution.py:433
  42.5 15.2 %all_to_all.21.got = f32[16,4,8,128]{3,2,1,0:T(8,128)S(1)} all-to-all(f32[16,4,8,128]{3,2,1,0:T(8,128)S(1)} %shard_map.52), channel_id=1, replica_groups=mesh['slab'=32,'mode'=16] {'mode'}, dimensions={0} | all-to-all | bytes 524288 | tf_op jit(solution)/shard_map/all_to_all | solution.py:437
  57.7 1.3 %shard_map.53 = (f32[32,8,128]{2,1,0:T(8,128)S(1)}, f32[32,8,128]{2,1,0:T(8,128)S(1)}, f32[32,8,128]{2,1,0:T(8,128)S(1)}, f32[2,8,128]{2,1,0:T(8,128)S(1)}, f32[32,1,128]{2,1,0:T(1,128)S(1)}) custom-call(f32[16,4,8,128]{3,2,1,0:T(8,128)S(1)} %all_to_all.21.got), custom_call_target="tpu_custom_call" | custom-call | flops 1000 | bytes 679936 | tf_op jit(solution)/shard_map/pallas_call | solution.py:407
  59.0 23.0 %all_to_all.22.got = f32[32,1,128]{2,1,0:T(1,128)S(1)} all-to-all(f32[32,1,128]{2,1,0:T(1,128)S(1)} %get-tuple-element.17), channel_id=1, replica_groups=mesh['slab'=32,'mode'=16] {'slab'}, dimensions={0} | all-to-all | bytes 32768 | tf_op jit(solution)/shard_map/all_to_all | solution.py:437
  82.0 1.4 %shard_map.54 = (f32[32,1,128]{2,1,0:T(1,128)S(1)}, f32[8,128]{1,0:T(8,128)S(1)}) custom-call(f32[32,1,128]{2,1,0:T(1,128)S(1)} %all_to_all.22.got, f32[32,8,128]{2,1,0:T(8,128)S(1)} %get-tuple-element.18.gain, f32[32,8,128]{2,1,0:T(8,128)S(1)} %get-tuple-element.19.least, f32[32,8,128]{2,1,0:T(8,128)S(1)} %get-tuple-element.20.most), custom_call_target="tpu_custom_call" | custom-call | flops 1000 | bytes 430080 | tf_op jit(solution)/shard_map/pallas_call | solution.py:407
  83.4 11.6 %all_to_all.23.got = f32[32,1,128]{2,1,0:T(1,128)S(1)} all-to-all(f32[32,1,128]{2,1,0:T(1,128)S(1)} %get-tuple-element.21), channel_id=1, replica_groups=mesh['slab'=32,'mode'=16] {'slab'}, dimensions={0} | all-to-all | bytes 32768 | tf_op jit(solution)/shard_map/all_to_all | solution.py:437
  95.0 0.8 shard_map.55
  (1 shorter events, 0.0 us)
Async XLA Ops:
  0.6 2.3 %copy-start = (f32[2,8,128]{2,1,0:T(8,128)S(1)}, f32[2,8,128]{2,1,0:T(8,128)}, u32[]{:S(2)}) copy-start(f32[2,8,128]{2,1,0:T(8,128)} %design.3) | copy-start | bytes 24580
  1.6 8.9 %collective-permute-start = (f32[400,128]{1,0:T(8,128)S(1)}, f32[400,128]{1,0:T(8,128)S(1)}, u32[]{:S(2)}, u32[]{:S(2)}) collective-permute-start(f32[400,128]{1,0:T(8,128)S(1)} %pack.1.packed), channel_id=1, source_target_pairs={{16,0},{32,16},{48,32},{64,48},{80,64},{96,80},{112,96},{128,112},... | collective-permute-start | bytes 614408 | tf_op jit(solution)/shard_map/ppermute | solution.py:426
  2.9 7.6 %collective-permute-start.1 = (f32[2,8,128]{2,1,0:T(8,128)S(1)}, f32[2,8,128]{2,1,0:T(8,128)S(1)}, u32[]{:S(2)}, u32[]{:S(2)}) collective-permute-start(f32[2,8,128]{2,1,0:T(8,128)S(1)} %copy-done), channel_id=1, source_target_pairs={{0,16},{16,32},{32,48},{48,64},{64,80},{80,96},{96,112},{112,128},... | collective-permute-start | bytes 24584 | tf_op jit(solution)/shard_map/ppermute | solution.py:421
  33.1 8.0 %collective-permute-start.3 = (f32[2,8,128]{2,1,0:T(8,128)S(1)}, f32[2,8,128]{2,1,0:T(8,128)S(1)}, u32[]{:S(2)}, u32[]{:S(2)}) collective-permute-start(f32[2,8,128]{2,1,0:T(8,128)S(1)} %shard_map.51.own), channel_id=1, source_target_pairs={{16,32},{32,16},{48,64},{64,48},{80,96},{96,80},{112,128},{128,112... | collective-permute-start | bytes 24584 | tf_op jit(solution)/shard_map/ppermute | solution.py:433
  33.7 8.7 %collective-permute-start.2 = (f32[2,8,128]{2,1,0:T(8,128)S(1)}, f32[2,8,128]{2,1,0:T(8,128)S(1)}, u32[]{:S(2)}, u32[]{:S(2)}) collective-permute-start(f32[2,8,128]{2,1,0:T(8,128)S(1)} %shard_map.51.own), channel_id=1, source_target_pairs={{0,16},{16,0},{32,48},{48,32},{64,80},{80,64},{96,112},{112,96},{1... | collective-permute-start | bytes 24584 | tf_op jit(solution)/shard_map/ppermute | solution.py:433

commit v14 on v13

--- a/solution.py
+++ b/solution.py
@@ -138,18 +138,14 @@
     return weight
 
 
-def fetch(pieces, sems):
-    return [
-        pltpu.make_async_copy(source, to.at[pl.ds(start, size)], sems.at[k])
-        for k, (source, to, start, size) in enumerate(pieces)
-    ]
-
-
 def pack(modes, design, out, sems):
     planes, rows = modes.shape[1], modes.shape[3]
-    pieces = [(modes.at[0, c, 0], out, c * rows, rows) for c in range(planes)]
-    pieces += [(design.at[l], out, planes * rows + l * SUB, SUB) for l in (0, 1)]
-    copies = fetch(pieces, sems)
+    first = out.at[pl.ds(0, planes * rows)].reshape(planes, rows, LANE)
+    last = out.at[pl.ds(planes * rows, 2 * SUB)].reshape(2, SUB, LANE)
+    copies = [
+        pltpu.make_async_copy(modes.at[0, :, 0], first, sems.at[0]),
+        pltpu.make_async_copy(design, last, sems.at[1]),
+    ]
     for copy in copies:
         copy.start()
     for copy in copies:
@@ -167,7 +163,8 @@
 
 def first_layer(modes, packed, eigen, out, upper, pairs, sems):
     planes, rows = modes.shape[1], modes.shape[3]
-    copies = fetch([(modes.at[0, c, 1], upper, c * rows, rows) for c in range(planes)], sems)
+    first = upper.at[pl.ds(0, planes * rows)].reshape(planes, rows, LANE)
+    copies = [pltpu.make_async_copy(modes.at[0, :, 1], first, sems.at[0])]
     for copy in copies:
         copy.start()
     for copy in copies:
@@ -455,7 +452,7 @@
         out_shape=jax.ShapeDtypeStruct((3 * total_y + 2 * SUB, LANE), F32),
         in_specs=[hbm, hbm],
         out_specs=VMEM,
-        scratch_shapes=[pltpu.SemaphoreType.DMA((5,))],
+        scratch_shapes=[pltpu.SemaphoreType.DMA((2,))],
         compiler_params=params,
         name="pack",
     )(held, pltpu.with_memory_space_constraint(design, pltpu.HBM))
@@ -469,7 +466,7 @@
         ],
         in_specs=[hbm, VMEM, SMEM],
         out_specs=[VMEM, VMEM],
-        scratch_shapes=[pltpu.VMEM(pairs, F32), pltpu.SemaphoreType.DMA((3,))],
+        scratch_shapes=[pltpu.VMEM(pairs, F32), pltpu.SemaphoreType.DMA((1,))],
         cost_estimate=pl.CostEstimate(flops=5_000_000, bytes_accessed=600_000, transcendentals=0),
         compiler_params=params,
         name="first_layer",

time: 96.2 us -> 96.2 us (level)
  no operation moved by 1% of the time
where the time goes in v14:
time: 96.2 us; the launch traced here: 95.8 us
  blocking collectives  71.7 us (75%)
  starting transfers between devices  14.7 us (15%)
  Pallas kernels  6.65 us (7%)
  between operations  1.39 us (1%)
  waiting for transfers between devices  1.35 us (1%)
    all_to_all x4, blocking collectives, exchange(): return lax.all_to_all(value, axis, 0, 0, tiled=True)  71.7 us
    ppermute x2, starting transfers between devices, swapped(): return lax.ppermute(value, axis, pairs)  7.99 us
    ppermute x1, starting transfers between devices, from_before(): return lax.ppermute(value, axis, [(i, i + 1) for i in range(count - 1)])  5.44 us
    pallas_call x6, Pallas kernels, call(): pl.pallas_call(kernel, out_shape=outs[0] if single else outs, in_specs=sp...  4.24 us
  transfers between devices with their start and end apart: 4, of which 1 were waited for; matrix products, arithmetic and copies ran while one was open for 0% of the time, Pallas kernels for 2%

profile of v14, /device:TPU:1, one launch (start us, length us, event | category | flops | bytes accessed | tf_op | source)
XLA Modules:
  0.0 95.8 jit_solution(725256486772244195)
XLA Ops:
  0.6 0.0 copy-start
  0.6 1.0 pack.1.packed
  1.6 1.3 %collective-permute-start = (f32[400,128]{1,0:T(8,128)S(1)}, f32[400,128]{1,0:T(8,128)S(1)}, u32[]{:S(2)}, u32[]{:S(2)}) collective-permute-start(f32[400,128]{1,0:T(8,128)S(1)} %pack.1.packed), channel_id=1, source_target_pairs={{16,0},{32,16},{48,32},{64,48},{80,64},{96,80},{112,96},{128,112},... | collective-permute-start | bytes 614408 | tf_op jit(solution)/shard_map/ppermute | solution.py:423
  2.9 0.0 copy-done
  2.9 5.4 %collective-permute-start.1 = (f32[2,8,128]{2,1,0:T(8,128)S(1)}, f32[2,8,128]{2,1,0:T(8,128)S(1)}, u32[]{:S(2)}, u32[]{:S(2)}) collective-permute-start(f32[2,8,128]{2,1,0:T(8,128)S(1)} %copy-done), channel_id=1, source_target_pairs={{0,16},{16,32},{32,48},{48,64},{64,80},{80,96},{96,112},{112,128},... | collective-permute-start | bytes 24584 | tf_op jit(solution)/shard_map/ppermute | solution.py:418
  9.0 1.5 %first_layer.1 = (f32[16,5,8,128]{3,2,1,0:T(8,128)S(1)}, f32[384,128]{1,0:T(8,128)S(1)}) custom-call(f32[1,3,2,128,128]{4,3,2,1,0:T(8,128)} %modes.3, f32[400,128]{1,0:T(8,128)S(1)} %pack.1.packed, f32[1]{0:T(128)S(6)} %copy.7.eigen), custom_call_target="tpu_custom_call" | custom-call | flops 5000000 | bytes 600000 | tf_op jit(solution)/shard_map/first_layer/pallas_call | solution.py:461
  10.5 0.0 collective-permute-done.1.before
  10.5 0.0 collective-permute-done.got
  10.5 0.6 shard_map.50
  11.1 21.8 %all_to_all.20.got = f32[16,5,8,128]{3,2,1,0:T(8,128)S(1)} all-to-all(f32[16,5,8,128]{3,2,1,0:T(8,128)S(1)} %get-tuple-element.15), channel_id=1, replica_groups=mesh['slab'=32,'mode'=16] {'mode'}, dimensions={0} | all-to-all | bytes 655360 | tf_op jit(solution)/shard_map/all_to_all | solution.py:434
  32.9 0.2 shard_map.51.own
  33.1 0.7 collective-permute-start.3
  33.7 7.3 %collective-permute-start.2 = (f32[2,8,128]{2,1,0:T(8,128)S(1)}, f32[2,8,128]{2,1,0:T(8,128)S(1)}, u32[]{:S(2)}, u32[]{:S(2)}) collective-permute-start(f32[2,8,128]{2,1,0:T(8,128)S(1)} %shard_map.51.own), channel_id=1, source_target_pairs={{0,16},{16,0},{32,48},{48,32},{64,80},{80,64},{96,112},{112,96},{1... | collective-permute-start | bytes 24584 | tf_op jit(solution)/shard_map/ppermute | solution.py:430
  41.1 0.0 collective-permute-done.3.odd
  41.1 1.3 %collective-permute-done.2.even = f32[2,8,128]{2,1,0:T(8,128)S(1)} collective-permute-done((f32[2,8,128]{2,1,0:T(8,128)S(1)}, f32[2,8,128]{2,1,0:T(8,128)S(1)}, u32[]{:S(2)}, u32[]{:S(2)}) %collective-permute-start.2) | collective-permute-done | bytes 8224 | tf_op jit(solution)/shard_map/ppermute | solution.py:430
  42.5 15.2 %all_to_all.21.got = f32[16,4,8,128]{3,2,1,0:T(8,128)S(1)} all-to-all(f32[16,4,8,128]{3,2,1,0:T(8,128)S(1)} %shard_map.52), channel_id=1, replica_groups=mesh['slab'=32,'mode'=16] {'mode'}, dimensions={0} | all-to-all | bytes 524288 | tf_op jit(solution)/shard_map/all_to_all | solution.py:434
  57.7 1.3 %shard_map.53 = (f32[32,8,128]{2,1,0:T(8,128)S(1)}, f32[32,8,128]{2,1,0:T(8,128)S(1)}, f32[32,8,128]{2,1,0:T(8,128)S(1)}, f32[2,8,128]{2,1,0:T(8,128)S(1)}, f32[32,1,128]{2,1,0:T(1,128)S(1)}) custom-call(f32[16,4,8,128]{3,2,1,0:T(8,128)S(1)} %all_to_all.21.got), custom_call_target="tpu_custom_call" | custom-call | flops 1000 | bytes 679936 | tf_op jit(solution)/shard_map/pallas_call | solution.py:404
  59.0 23.0 %all_to_all.22.got = f32[32,1,128]{2,1,0:T(1,128)S(1)} all-to-all(f32[32,1,128]{2,1,0:T(1,128)S(1)} %get-tuple-element.17), channel_id=1, replica_groups=mesh['slab'=32,'mode'=16] {'slab'}, dimensions={0} | all-to-all | bytes 32768 | tf_op jit(solution)/shard_map/all_to_all | solution.py:434
  82.0 1.4 %shard_map.54 = (f32[32,1,128]{2,1,0:T(1,128)S(1)}, f32[8,128]{1,0:T(8,128)S(1)}) custom-call(f32[32,1,128]{2,1,0:T(1,128)S(1)} %all_to_all.22.got, f32[32,8,128]{2,1,0:T(8,128)S(1)} %get-tuple-element.18.gain, f32[32,8,128]{2,1,0:T(8,128)S(1)} %get-tuple-element.19.least, f32[32,8,128]{2,1,0:T(8,128)S(1)} %get-tuple-element.20.most), custom_call_target="tpu_custom_call" | custom-call | flops 1000 | bytes 430080 | tf_op jit(solution)/shard_map/pallas_call | solution.py:404
  83.4 11.6 %all_to_all.23.got = f32[32,1,128]{2,1,0:T(1,128)S(1)} all-to-all(f32[32,1,128]{2,1,0:T(1,128)S(1)} %get-tuple-element.21), channel_id=1, replica_groups=mesh['slab'=32,'mode'=16] {'slab'}, dimensions={0} | all-to-all | bytes 32768 | tf_op jit(solution)/shard_map/all_to_all | solution.py:434
  95.0 0.8 shard_map.55
  (1 shorter events, 0.0 us)
Async XLA Ops:
  0.6 2.3 %copy-start = (f32[2,8,128]{2,1,0:T(8,128)S(1)}, f32[2,8,128]{2,1,0:T(8,128)}, u32[]{:S(2)}) copy-start(f32[2,8,128]{2,1,0:T(8,128)} %design.3) | copy-start | bytes 24580
  1.6 8.9 %collective-permute-start = (f32[400,128]{1,0:T(8,128)S(1)}, f32[400,128]{1,0:T(8,128)S(1)}, u32[]{:S(2)}, u32[]{:S(2)}) collective-permute-start(f32[400,128]{1,0:T(8,128)S(1)} %pack.1.packed), channel_id=1, source_target_pairs={{16,0},{32,16},{48,32},{64,48},{80,64},{96,80},{112,96},{128,112},... | collective-permute-start | bytes 614408 | tf_op jit(solution)/shard_map/ppermute | solution.py:423
  2.9 7.6 %collective-permute-start.1 = (f32[2,8,128]{2,1,0:T(8,128)S(1)}, f32[2,8,128]{2,1,0:T(8,128)S(1)}, u32[]{:S(2)}, u32[]{:S(2)}) collective-permute-start(f32[2,8,128]{2,1,0:T(8,128)S(1)} %copy-done), channel_id=1, source_target_pairs={{0,16},{16,32},{32,48},{48,64},{64,80},{80,96},{96,112},{112,128},... | collective-permute-start | bytes 24584 | tf_op jit(solution)/shard_map/ppermute | solution.py:418
  33.1 8.0 %collective-permute-start.3 = (f32[2,8,128]{2,1,0:T(8,128)S(1)}, f32[2,8,128]{2,1,0:T(8,128)S(1)}, u32[]{:S(2)}, u32[]{:S(2)}) collective-permute-start(f32[2,8,128]{2,1,0:T(8,128)S(1)} %shard_map.51.own), channel_id=1, source_target_pairs={{16,32},{32,16},{48,64},{64,48},{80,96},{96,80},{112,128},{128,112... | collective-permute-start | bytes 24584 | tf_op jit(solution)/shard_map/ppermute | solution.py:430
  33.7 8.7 %collective-permute-start.2 = (f32[2,8,128]{2,1,0:T(8,128)S(1)}, f32[2,8,128]{2,1,0:T(8,128)S(1)}, u32[]{:S(2)}, u32[]{:S(2)}) collective-permute-start(f32[2,8,128]{2,1,0:T(8,128)S(1)} %shard_map.51.own), channel_id=1, source_target_pairs={{0,16},{16,0},{32,48},{48,32},{64,80},{80,64},{96,112},{112,96},{1... | collective-permute-start | bytes 24584 | tf_op jit(solution)/shard_map/ppermute | solution.py:430

commit v15 on v14

--- a/solution.py
+++ b/solution.py
@@ -134,7 +134,7 @@
         store(r, weight * stiff, eigen_weight * mass)
         return 0
 
-    lax.fori_loop(0, tiles, tile, 0, unroll=2)
+    lax.fori_loop(0, tiles, tile, 0, unroll=16)
     return weight
 
 
@@ -290,8 +290,8 @@
 
 def volumes(levels, gain, least, most, parts):
     count = gain.shape[0]
-    for start in range(0, len(levels), 8):
-        chunk = levels[start : start + 8]
+    for start in range(0, len(levels), 9):
+        chunk = levels[start : start + 9]
 
         def body(v, totals):
             g, lo, hi = gain[v], least[v], most[v]

time: 96.2 us -> 96.1 us (level)
  transfers between devices with their start and end apart: 4 -> 4, of which waited for: 1 -> 1; matrix products, arithmetic and copies ran while one was open for 0% -> 0% of each run, Pallas kernels for 2% -> 1%
where the time goes in v15:
time: 96.1 us; the launch traced here: 95.7 us
  blocking collectives  71.7 us (75%)
  starting transfers between devices  14.7 us (15%)
  Pallas kernels  6.58 us (7%)
  between operations  1.39 us (1%)
  waiting for transfers between devices  1.35 us (1%)
    all_to_all x4, blocking collectives, exchange(): return lax.all_to_all(value, axis, 0, 0, tiled=True)  71.7 us
    ppermute x2, starting transfers between devices, swapped(): return lax.ppermute(value, axis, pairs)  7.99 us
    ppermute x1, starting transfers between devices, from_before(): return lax.ppermute(value, axis, [(i, i + 1) for i in range(count - 1)])  5.44 us
    pallas_call x6, Pallas kernels, call(): pl.pallas_call(kernel, out_shape=outs[0] if single else outs, in_specs=sp...  4.21 us
  transfers between devices with their start and end apart: 4, of which 1 were waited for; matrix products, arithmetic and copies ran while one was open for 0% of the time, Pallas kernels for 1%

profile of v15, /device:TPU:1, one launch (start us, length us, event | category | flops | bytes accessed | tf_op | source)
XLA Modules:
  0.0 95.7 jit_solution(10413330853034154567)
XLA Ops:
  0.6 0.0 copy-start
  0.6 1.0 pack.1.packed
  1.6 1.3 %collective-permute-start = (f32[400,128]{1,0:T(8,128)S(1)}, f32[400,128]{1,0:T(8,128)S(1)}, u32[]{:S(2)}, u32[]{:S(2)}) collective-permute-start(f32[400,128]{1,0:T(8,128)S(1)} %pack.1.packed), channel_id=1, source_target_pairs={{16,0},{32,16},{48,32},{64,48},{80,64},{96,80},{112,96},{128,112},... | collective-permute-start | bytes 614408 | tf_op jit(solution)/shard_map/ppermute | solution.py:423
  2.9 0.0 copy-done
  2.9 5.4 %collective-permute-start.1 = (f32[2,8,128]{2,1,0:T(8,128)S(1)}, f32[2,8,128]{2,1,0:T(8,128)S(1)}, u32[]{:S(2)}, u32[]{:S(2)}) collective-permute-start(f32[2,8,128]{2,1,0:T(8,128)S(1)} %copy-done), channel_id=1, source_target_pairs={{0,16},{16,32},{32,48},{48,64},{64,80},{80,96},{96,112},{112,128},... | collective-permute-start | bytes 24584 | tf_op jit(solution)/shard_map/ppermute | solution.py:418
  9.0 1.4 %first_layer.1 = (f32[16,5,8,128]{3,2,1,0:T(8,128)S(1)}, f32[384,128]{1,0:T(8,128)S(1)}) custom-call(f32[1,3,2,128,128]{4,3,2,1,0:T(8,128)} %modes.3, f32[400,128]{1,0:T(8,128)S(1)} %pack.1.packed, f32[1]{0:T(128)S(6)} %copy.7.eigen), custom_call_target="tpu_custom_call" | custom-call | flops 5000000 | bytes 600000 | tf_op jit(solution)/shard_map/first_layer/pallas_call | solution.py:461
  10.4 0.0 collective-permute-done.1.before
  10.4 0.0 collective-permute-done.got
  10.5 0.5 shard_map.50
  11.0 21.9 %all_to_all.20.got = f32[16,5,8,128]{3,2,1,0:T(8,128)S(1)} all-to-all(f32[16,5,8,128]{3,2,1,0:T(8,128)S(1)} %get-tuple-element.15), channel_id=1, replica_groups=mesh['slab'=32,'mode'=16] {'mode'}, dimensions={0} | all-to-all | bytes 655360 | tf_op jit(solution)/shard_map/all_to_all | solution.py:434
  32.8 0.2 shard_map.51.own
  33.0 0.7 collective-permute-start.3
  33.7 7.3 %collective-permute-start.2 = (f32[2,8,128]{2,1,0:T(8,128)S(1)}, f32[2,8,128]{2,1,0:T(8,128)S(1)}, u32[]{:S(2)}, u32[]{:S(2)}) collective-permute-start(f32[2,8,128]{2,1,0:T(8,128)S(1)} %shard_map.51.own), channel_id=1, source_target_pairs={{0,16},{16,0},{32,48},{48,32},{64,80},{80,64},{96,112},{112,96},{1... | collective-permute-start | bytes 24584 | tf_op jit(solution)/shard_map/ppermute | solution.py:430
  41.0 0.0 collective-permute-done.3.odd
  41.0 1.3 %collective-permute-done.2.even = f32[2,8,128]{2,1,0:T(8,128)S(1)} collective-permute-done((f32[2,8,128]{2,1,0:T(8,128)S(1)}, f32[2,8,128]{2,1,0:T(8,128)S(1)}, u32[]{:S(2)}, u32[]{:S(2)}) %collective-permute-start.2) | collective-permute-done | bytes 8224 | tf_op jit(solution)/shard_map/ppermute | solution.py:430
  42.4 15.2 %all_to_all.21.got = f32[16,4,8,128]{3,2,1,0:T(8,128)S(1)} all-to-all(f32[16,4,8,128]{3,2,1,0:T(8,128)S(1)} %shard_map.52), channel_id=1, replica_groups=mesh['slab'=32,'mode'=16] {'mode'}, dimensions={0} | all-to-all | bytes 524288 | tf_op jit(solution)/shard_map/all_to_all | solution.py:434
  57.6 1.4 %shard_map.53 = (f32[32,8,128]{2,1,0:T(8,128)S(1)}, f32[32,8,128]{2,1,0:T(8,128)S(1)}, f32[32,8,128]{2,1,0:T(8,128)S(1)}, f32[2,8,128]{2,1,0:T(8,128)S(1)}, f32[32,1,128]{2,1,0:T(1,128)S(1)}) custom-call(f32[16,4,8,128]{3,2,1,0:T(8,128)S(1)} %all_to_all.21.got), custom_call_target="tpu_custom_call" | custom-call | flops 1000 | bytes 679936 | tf_op jit(solution)/shard_map/pallas_call | solution.py:404
  59.0 23.0 %all_to_all.22.got = f32[32,1,128]{2,1,0:T(1,128)S(1)} all-to-all(f32[32,1,128]{2,1,0:T(1,128)S(1)} %get-tuple-element.17), channel_id=1, replica_groups=mesh['slab'=32,'mode'=16] {'slab'}, dimensions={0} | all-to-all | bytes 32768 | tf_op jit(solution)/shard_map/all_to_all | solution.py:434
  81.9 1.4 %shard_map.54 = (f32[32,1,128]{2,1,0:T(1,128)S(1)}, f32[8,128]{1,0:T(8,128)S(1)}) custom-call(f32[32,1,128]{2,1,0:T(1,128)S(1)} %all_to_all.22.got, f32[32,8,128]{2,1,0:T(8,128)S(1)} %get-tuple-element.18.gain, f32[32,8,128]{2,1,0:T(8,128)S(1)} %get-tuple-element.19.least, f32[32,8,128]{2,1,0:T(8,128)S(1)} %get-tuple-element.20.most), custom_call_target="tpu_custom_call" | custom-call | flops 1000 | bytes 430080 | tf_op jit(solution)/shard_map/pallas_call | solution.py:404
  83.4 11.6 %all_to_all.23.got = f32[32,1,128]{2,1,0:T(1,128)S(1)} all-to-all(f32[32,1,128]{2,1,0:T(1,128)S(1)} %get-tuple-element.21), channel_id=1, replica_groups=mesh['slab'=32,'mode'=16] {'slab'}, dimensions={0} | all-to-all | bytes 32768 | tf_op jit(solution)/shard_map/all_to_all | solution.py:434
  95.0 0.8 shard_map.55
  (1 shorter events, 0.0 us)
Async XLA Ops:
  0.6 2.3 %copy-start = (f32[2,8,128]{2,1,0:T(8,128)S(1)}, f32[2,8,128]{2,1,0:T(8,128)}, u32[]{:S(2)}) copy-start(f32[2,8,128]{2,1,0:T(8,128)} %design.3) | copy-start | bytes 24580
  1.6 8.8 %collective-permute-start = (f32[400,128]{1,0:T(8,128)S(1)}, f32[400,128]{1,0:T(8,128)S(1)}, u32[]{:S(2)}, u32[]{:S(2)}) collective-permute-start(f32[400,128]{1,0:T(8,128)S(1)} %pack.1.packed), channel_id=1, source_target_pairs={{16,0},{32,16},{48,32},{64,48},{80,64},{96,80},{112,96},{128,112},... | collective-permute-start | bytes 614408 | tf_op jit(solution)/shard_map/ppermute | solution.py:423
  2.9 7.5 %collective-permute-start.1 = (f32[2,8,128]{2,1,0:T(8,128)S(1)}, f32[2,8,128]{2,1,0:T(8,128)S(1)}, u32[]{:S(2)}, u32[]{:S(2)}) collective-permute-start(f32[2,8,128]{2,1,0:T(8,128)S(1)} %copy-done), channel_id=1, source_target_pairs={{0,16},{16,32},{32,48},{48,64},{64,80},{80,96},{96,112},{112,128},... | collective-permute-start | bytes 24584 | tf_op jit(solution)/shard_map/ppermute | solution.py:418
  33.0 8.0 %collective-permute-start.3 = (f32[2,8,128]{2,1,0:T(8,128)S(1)}, f32[2,8,128]{2,1,0:T(8,128)S(1)}, u32[]{:S(2)}, u32[]{:S(2)}) collective-permute-start(f32[2,8,128]{2,1,0:T(8,128)S(1)} %shard_map.51.own), channel_id=1, source_target_pairs={{16,32},{32,16},{48,64},{64,48},{80,96},{96,80},{112,128},{128,112... | collective-permute-start | bytes 24584 | tf_op jit(solution)/shard_map/ppermute | solution.py:430
  33.7 8.7 %collective-permute-start.2 = (f32[2,8,128]{2,1,0:T(8,128)S(1)}, f32[2,8,128]{2,1,0:T(8,128)S(1)}, u32[]{:S(2)}, u32[]{:S(2)}) collective-permute-start(f32[2,8,128]{2,1,0:T(8,128)S(1)} %shard_map.51.own), channel_id=1, source_target_pairs={{0,16},{16,0},{32,48},{48,32},{64,80},{80,64},{96,112},{112,96},{1... | collective-permute-start | bytes 24584 | tf_op jit(solution)/shard_map/ppermute | solution.py:430
